TPU v7x, 256 devices: a whole 4x4x8 slice. The times are simulated.
256 devices in a mesh: zone: 32 (over z, y), var: 8 (over x, core).
Axes of the slice: x: 4, y: 4, z: 8, core: 2. Of those that a mesh axis runs over, the one named last changes fastest.
Arguments:
- history: float32 [48, 64, 16384], P('var', None, 'zone'), may hold values from -6 to 6
- adjacency: int32 [6, 16384], P(None, 'zone'), may hold values from -1 to 16383, as said below
- volume_op: float32 [64, 64], replicated, may hold values from -0.375 to 0.375
- face_lift: float32 [6, 64, 64], replicated, may hold values from -0.1875 to 0.1875
- schmid_map: float32 [48, 12], replicated, may hold values from -0.875 to 0.875
- hardening: float32 [12, 48], replicated, may hold values from -1.75 to 1.75
Outputs:
- remapped: float32 [48, 64, 16384], P('var', None, 'zone')
Inputs may be any that keep to these rules, and one draw needn't show every extreme that they name: `adjacency`: every entry is -1 or a zone whose index differs from the zone's own by at most 64; differences of exactly 64 and -64 occur.
All inputs are finite; a program needn't handle non-finite values.
Results may differ from a plain program's by a relative error of at most 0.0001.
Values sent between devices are 32-bit elements; how exact they have to be, the bound alone decides.
No kernel may reach another device: no remote copies, remote signals or barrier semaphores. Data moves between devices by JAX's collectives and lax.ppermute only.
A program may use at most 64 MiB of HBM per device.

v0:
```python
import jax
import jax.numpy as jnp
from jax import lax
from jax.experimental import pallas as pl
from jax.experimental.pallas import tpu as pltpu
from jax.sharding import PartitionSpec as P


F32 = jnp.float32
BF16 = jnp.bfloat16
NV = 6
NP = 64
NZ = 512
ROWS = NV * NP
LANE = 128
HALF = 64
NFACE = 6
MATMUL_FACES = 4
KDIM = (NFACE + 1) * NP
SLOTS = [(0, 0), (2, 0), (2, 1), (1, 0), (3, 0), (1, 1), (3, 1), (0, 1)]
EARLY = (0, 1, 2, 7)
LATE = (3, 4, 5, 6)


def first_half(rows):
    return lax.broadcasted_iota(jnp.int32, (rows, LANE), 1) < HALF


def swap(x):
    return pltpu.roll(x, HALF, 1)


def straddle(left, right):
    return jnp.where(first_half(left.shape[0]), swap(left), swap(right))


def split(x):
    high = x.astype(BF16)
    low = (x - high.astype(F32)).astype(BF16)
    return high, low


def cols(b, n=1):
    return slice(b * LANE, (b + n) * LANE)


def put_parts(parts, where, x):
    high, low = split(x)
    parts[0:ROWS, where] = high
    parts[ROWS:, where] = low


def fetch(pairs, sems):
    copies = [pltpu.make_async_copy(source, target, sems.at[i]) for i, (source, target) in enumerate(pairs)]
    for copy in copies:
        copy.start()
    return copies


def pack_kernel(
    place_ref, history_hbm, adjacency_hbm, near_one, near_two, far_one, far_two, history, adjacency, sems
):
    half = ROWS // 2
    first = first_half(half)
    odd = place_ref[3] == 1
    copies = fetch(
        [(history_hbm.at[:, cols(c)], history.at[:, cols(c)]) for c in (0, 3, 1, 2)] + [(adjacency_hbm, adjacency)],
        sems,
    )

    def put(one, two, rows, forward, backward):
        one[rows, :] = jnp.where(odd, forward, backward)
        two[rows, :] = jnp.where(odd, backward, forward)

    copies[0].wait()
    copies[1].wait()
    forward = jnp.where(first, swap(history[0:half, cols(3)]), history[half:, cols(3)])
    backward = jnp.where(first, history[0:half, cols(0)], swap(history[half:, cols(0)]))
    put(near_one, near_two, slice(0, half), forward, backward)
    copies[2].wait()
    copies[3].wait()
    forward = straddle(history[:, cols(2)], history[:, cols(3)])
    backward = straddle(history[:, cols(0)], history[:, cols(1)])
    put(far_one, far_two, slice(0, ROWS), forward, backward)
    copies[4].wait()
    for target in (far_one, far_two):
        target[ROWS:, :] = jnp.zeros((8, LANE), F32)
    put(
        far_one, far_two, slice(ROWS, ROWS + NFACE), adjacency[:, cols(3)].astype(F32), adjacency[:, cols(0)].astype(F32)
    )


def place(adjacency, start):
    return jnp.where(adjacency < 0, 1000, adjacency - start)


def write_onehots(onehots, slot, rel):
    position = lax.broadcasted_iota(jnp.int32, (2 * LANE, LANE), 0)
    for face in range(MATMUL_FACES):
        hit = position == rel[face : face + 1, :]
        onehots[slot, :, cols(face)] = jnp.where(hit, 1.0, 0.0).astype(BF16)


def apply_block(close, beyond, parts, col, onehots, slot, rel, own, gathered, weights):
    for pair in range(MATMUL_FACES // 2):
        picked = jnp.dot(
            parts[:, pl.ds(col, 2 * LANE)], onehots[slot, :, cols(2 * pair, 2)], preferred_element_type=F32
        ).astype(BF16)
        for part in range(2):
            for v in range(NV):
                row = part * ROWS + v * NP
                for k in range(2):
                    face = 2 * pair + k
                    gathered[part, face * NP : (face + 1) * NP, cols(v)] = picked[row : row + NP, cols(k)]
    for face in range(MATMUL_FACES, NFACE):
        index = jnp.broadcast_to(rel[face : face + 1, :], (ROWS, LANE))
        lane = index & (LANE - 1)
        near = jnp.take_along_axis(close, lane, axis=1)
        far = jnp.take_along_axis(beyond, lane, axis=1)
        value = jnp.where(index >= 2 * LANE, 0.0, jnp.where(index >= LANE, far, near))
        for part, piece in enumerate(split(value)):
            for v in range(NV):
                gathered[part, face * NP : (face + 1) * NP, cols(v)] = piece[v * NP : (v + 1) * NP]
    for part, piece in enumerate(split(own)):
        for v in range(NV):
            gathered[part, NFACE * NP :, cols(v)] = piece[v * NP : (v + 1) * NP]
    both = jnp.dot(weights[...], gathered[0], preferred_element_type=F32)
    rest = jnp.dot(weights[0:NP, :], gathered[1], preferred_element_type=F32)
    value = both[0:NP] + (both[NP:] + rest)
    return [value[:, cols(v)] for v in range(NV)]


def finish(values, base, scale, target, parts, where):
    for v in range(NV):
        rows = slice(v * NP, (v + 1) * NP)
        result = base[rows] + values[v] * scale
        target[rows, where] = result
        high, low = split(result)
        parts[rows, where] = high
        parts[ROWS + v * NP : ROWS + (v + 1) * NP, where] = low


def mix(left, right):
    return jnp.where(first_half(NFACE), pltpu.roll(left, HALF, 1), pltpu.roll(right, HALF, 1))


def inner_kernel(
    place_ref, history, adjacency, volume_hbm, face_hbm,
    u0, parts, onehots, t1, parts2, t2, parts3, weights,
    gat_a, gat_b, volume_op, face_lift, sems,
):
    copies = fetch([(volume_hbm, volume_op), (face_hbm, face_lift)], sems)
    origin = place_ref[0]
    zero = jnp.zeros((ROWS, LANE), F32)
    blocks = [history[:, cols(b)] for b in range(4)]
    padded = [zero] + blocks + [zero]
    for c in range(5):
        u0[:, cols(c)] = straddle(padded[c], padded[c + 1])
    for c in range(1, 4):
        put_parts(parts, cols(c - 1), u0[:, cols(c)])
    for b in range(4):
        write_onehots(onehots, b, place(adjacency[:, cols(b)], origin + (128 * b + 128)))
    near = [mix(adjacency[:, cols(b)], adjacency[:, cols(b + 1)]) for b in range(3)]
    for b in range(3):
        write_onehots(onehots, 4 + b, place(near[b], origin + (128 * b + 192)))
    for copy in copies:
        copy.wait()
    for lanes, matrix in ((slice(0, 384), face_lift[...].T), (slice(384, 448), volume_op[...].T)):
        high, low = split(matrix)
        weights[0:NP, lanes] = high
        weights[NP:, lanes] = low
    for b, gathered in ((2, gat_a), (3, gat_b)):
        rel = place(adjacency[:, cols(b - 1)], origin + 128 * b)
        values = apply_block(
            u0[:, cols(b - 1)], u0[:, cols(b)], parts, (b - 2) * LANE, onehots, b - 1, rel, blocks[b - 1], gathered, weights
        )
        finish(values, blocks[b - 1], 1.0 / 3.0, t1, parts2, cols(b - 2))
    rel = place(near[1], origin + 320)
    own = straddle(t1[:, cols(0)], t1[:, cols(1)])
    values = apply_block(t1[:, cols(0)], t1[:, cols(1)], parts2, 0, onehots, 5, rel, own, gat_a, weights)
    finish(values, u0[:, cols(2)], 0.5, t2, parts3, cols(0))


def middle_kernel(
    place_ref, history, adjacency, near_one, near_two, u0m, partsm, onehots, t1m, parts2m, t2m, parts3m, weights,
    ends, end_parts, rim, rim_parts, t2, parts3,
    left, right, t1, parts2, gat_a, gat_b,
):
    origin = place_ref[0]
    odd = place_ref[3] == 1
    half = ROWS // 2
    first = first_half(half)
    low = jnp.where(odd, near_two[...], near_one[...])
    high = jnp.where(odd, near_one[...], near_two[...])
    ends[0:half, cols(0)] = jnp.where(first, low, u0m[0:half, cols(0)])
    ends[half:, cols(0)] = jnp.where(first, swap(low), u0m[half:, cols(0)])
    ends[0:half, cols(1)] = jnp.where(first, u0m[0:half, cols(4)], swap(high))
    ends[half:, cols(1)] = jnp.where(first, u0m[half:, cols(4)], high)
    put_parts(end_parts, cols(0), ends[:, cols(0)])
    put_parts(end_parts, cols(1), ends[:, cols(1)])
    left[:, cols(0)] = end_parts[:, cols(0)]
    left[:, cols(1)] = partsm[:, cols(0)]
    right[:, cols(0)] = partsm[:, cols(2)]
    right[:, cols(1)] = end_parts[:, cols(1)]
    t1[:, cols(1, 2)] = t1m[...]
    parts2[:, cols(1, 2)] = parts2m[...]
    t2[:, cols(1)] = t2m[...]
    parts3[:, cols(1)] = parts3m[...]
    rel = place(adjacency[:, cols(0)], origin + 128)
    base = history[:, cols(0)]
    values = apply_block(ends[:, cols(0)], u0m[:, cols(1)], left, 0, onehots, 0, rel, base, gat_a, weights)
    finish(values, base, 1.0 / 3.0, t1, parts2, cols(0))
    rel = place(adjacency[:, cols(3)], origin + 512)
    base = history[:, cols(3)]
    values = apply_block(u0m[:, cols(3)], ends[:, cols(1)], right, 0, onehots, 3, rel, base, gat_b, weights)
    finish(values, base, 1.0 / 3.0, t1, parts2, cols(3))
    for b, gathered in ((0, gat_a), (2, gat_b)):
        rel = place(mix(adjacency[:, cols(b)], adjacency[:, cols(b + 1)]), origin + (128 * b + 192))
        close, beyond = t1[:, cols(b)], t1[:, cols(b + 1)]
        values = apply_block(
            close, beyond, parts2, b * LANE, onehots, 4 + b, rel, straddle(close, beyond), gathered, weights
        )
        finish(values, u0m[:, cols(b + 1)], 0.5, t2, parts3, cols(b))
    for i, c in ((0, 0), (1, 3)):
        rim[:, cols(i)] = t1[:, cols(c)]
        rim_parts[:, cols(i)] = parts2[:, cols(c)]


def edge_kernel(
    place_ref, history, adjacency, far_one, far_two, onehots, weights, ends, end_parts, rim, rim_parts, t2m, parts3m,
    *rest,
):
    outs = rest[:8]
    low, high, left, right, left2, right2, edge, tips, t2, parts3, gat_a, gat_b = rest[8:]
    origin = place_ref[0]
    x = place_ref[1]
    odd = place_ref[3] == 1
    upper = place_ref[2] == 1
    low[...] = jnp.where(odd, far_two[...], far_one[...])
    high[...] = jnp.where(odd, far_one[...], far_two[...])
    low_adj = low[ROWS:, :].astype(jnp.int32)[0:NFACE]
    high_adj = high[ROWS:, :].astype(jnp.int32)[0:NFACE]
    rels = [
        place(low_adj, origin),
        place(high_adj, origin + 640),
        place(mix(low_adj, adjacency[:, cols(0)]), origin + 64),
        place(mix(adjacency[:, cols(3)], high_adj), origin + 576),
    ]
    for slot, rel in enumerate(rels):
        write_onehots(edge, slot, rel)
    put_parts(left, cols(0), low[0:ROWS, :])
    left[:, cols(1)] = end_parts[:, cols(0)]
    right[:, cols(0)] = end_parts[:, cols(1)]
    put_parts(right, cols(1), high[0:ROWS, :])
    left2[:, cols(1)] = rim_parts[:, cols(0)]
    right2[:, cols(0)] = rim_parts[:, cols(1)]
    t2[:, cols(1, 3)] = t2m[...]
    parts3[:, cols(1, 3)] = parts3m[...]
    close, beyond = low[0:ROWS, :], ends[:, cols(0)]
    base = straddle(close, beyond)
    values = apply_block(close, beyond, left, 0, edge, 0, rels[0], base, gat_a, weights)
    finish(values, base, 1.0 / 3.0, tips, left2, cols(0))
    close, beyond = ends[:, cols(1)], high[0:ROWS, :]
    base = straddle(close, beyond)
    values = apply_block(close, beyond, right, 0, edge, 1, rels[1], base, gat_b, weights)
    finish(values, base, 1.0 / 3.0, tips, right2, cols(1))
    close, beyond = tips[:, cols(0)], rim[:, cols(0)]
    values = apply_block(close, beyond, left2, 0, edge, 2, rels[2], straddle(close, beyond), gat_a, weights)
    finish(values, ends[:, cols(0)], 0.5, t2, parts3, cols(0))
    close, beyond = rim[:, cols(1)], tips[:, cols(1)]
    values = apply_block(close, beyond, right2, 0, edge, 3, rels[3], straddle(close, beyond), gat_b, weights)
    finish(values, ends[:, cols(1)], 0.5, t2, parts3, cols(4))
    for dx, gathered in ((2, gat_a), (1, gat_b), (3, gat_a), (0, gat_b)):
        b = (x + dx) & 3
        col = pl.multiple_of(b * LANE, LANE)
        rel = place(adjacency[:, pl.ds(col, LANE)], origin + 128 + col)
        close, beyond = t2[:, pl.ds(col, LANE)], t2[:, pl.ds(col + LANE, LANE)]
        values = apply_block(
            close, beyond, parts3, col, onehots, b, rel, straddle(close, beyond), gathered, weights
        )
        for v in range(NV):
            result = history[v * NP : (v + 1) * NP, pl.ds(col, LANE)] + values[v]
            below, above = result[0:32], result[32:64]
            outs[SLOTS.index((dx, 0))][v] = jnp.where(upper, above, below)
            outs[SLOTS.index((dx, 1))][v] = jnp.where(upper, below, above)


def source_of(x, core, slot):
    dx, dc = SLOTS[slot]
    return ((x - dx) & 3) * 2 + (core ^ dc)


def table_kernel(place_ref, schmid_hbm, hardening_hbm, mixing, renewing, schmid_map, hardening, sems):
    x = place_ref[1]
    core = place_ref[2]
    for copy in fetch([(schmid_hbm, schmid_map), (hardening_hbm, hardening)], sems):
        copy.wait()

    def variable(index):
        total = jnp.zeros(index.shape, jnp.int32)
        for slot in range(8):
            inside = (index >= slot * 48) & (index < slot * 48 + 48)
            total = jnp.where(inside, source_of(x, core, slot) * NV + ((index - slot * 48) >> 3), total)
        return total

    def onehot(hit):
        return jnp.where(hit, 1.0, 0.0).astype(BF16)

    def iota(shape, axis):
        return lax.broadcasted_iota(jnp.int32, shape, axis)

    columns = onehot(iota((48, ROWS), 0) == variable(iota((48, ROWS), 1)))
    rows = onehot(iota((ROWS, 48), 1) == variable(iota((ROWS, 48), 0)))
    slips = onehot(iota((96, 12), 1) == (iota((96, 12), 0) >> 3))
    spread = onehot(iota((12, 96), 0) == (iota((12, 96), 1) >> 3))
    wide = onehot((iota((96, ROWS), 0) & 7) == (iota((96, ROWS), 1) & 7)).astype(F32)
    tall = onehot((iota((ROWS, 96), 0) & 7) == (iota((ROWS, 96), 1) & 7)).astype(F32)
    second = (((1,), (1,)), ((), ()))
    for part, piece in enumerate(split(schmid_map[...])):
        picked = jnp.dot(slips, piece, preferred_element_type=F32).astype(BF16)
        picked = jnp.dot(picked, columns, preferred_element_type=F32) * wide
        mixing[part * 96 : (part + 1) * 96, :] = picked.astype(BF16)
    for part, piece in enumerate(split(hardening[...])):
        picked = lax.dot_general(rows, piece, second, preferred_element_type=F32).astype(BF16)
        picked = (jnp.dot(picked, spread, preferred_element_type=F32) * tall).astype(BF16)
        if part == 0:
            renewing[:, 0:96] = picked
            renewing[:, 96:192] = picked
        else:
            renewing[:, 192:288] = picked


def point_kernel(place_ref, mixing, renewing, *rest):
    own = [source_of(place_ref[1], place_ref[2], slot) < 4 for slot in range(8)]
    points = rest[:8]
    outs = rest[8:16]
    highs, lows, rate_parts = rest[16:]
    for slot in range(8):
        for i in range(NV):
            row = (slot * NV + i) * 8
            for g in range(4):
                high, low = split(points[slot][i, g * 8 : (g + 1) * 8, :])
                highs[row : row + 8, cols(g)] = high
                lows[row : row + 8, cols(g)] = low
    both = jnp.dot(mixing[...], highs[...], preferred_element_type=F32)
    rest_ = jnp.dot(mixing[0:96, :], lows[...], preferred_element_type=F32)
    rates = jnp.tanh(both[0:96] + (both[96:] + rest_))
    high, low = split(rates)
    rate_parts[0:96, :] = high
    rate_parts[96:192, :] = low
    rate_parts[192:288, :] = high
    change = jnp.dot(renewing[...], rate_parts[...], preferred_element_type=F32)
    for g in range(4):
        rows = [points[slot][0, g * 8 : (g + 1) * 8, :] + change[slot * 48 : slot * 48 + 8, cols(g)] for slot in range(8)]
        square = jnp.zeros((8, LANE), F32)
        for slot in range(8):
            square = square + jnp.where(own[slot], rows[slot] * rows[slot], 0.0)
        factor = 1.0 / jnp.maximum(jnp.sqrt(square), 1.0)
        for slot in range(8):
            outs[slot][0, g * 8 : (g + 1) * 8, :] = jnp.where(own[slot], rows[slot] * factor, rows[slot])
            for i in range(1, NV):
                row = (slot * NV + i) * 8
                outs[slot][i, g * 8 : (g + 1) * 8, :] = (
                    points[slot][i, g * 8 : (g + 1) * 8, :] + change[row : row + 8, cols(g)]
                )


def merge_kernel(slots):
    def kernel(place_ref, *rest):
        pieces = rest[: len(slots)]
        out, sems = rest[-2:]
        x = place_ref[1]
        core = place_ref[2]
        pairs = []
        for piece, slot in zip(pieces, slots):
            dx, dc = SLOTS[slot]
            col = pl.multiple_of(((x + dx) & 3) * LANE, LANE)
            row = pl.multiple_of((core ^ dc) * 32, 32)
            pairs.append((piece, out.at[:, pl.ds(row, 32), pl.ds(col, LANE)]))
        for copy in fetch(pairs, sems):
            copy.wait()

    return kernel


def vmem():
    return pl.BlockSpec(memory_space=pltpu.VMEM)


def smem():
    return pl.BlockSpec(memory_space=pltpu.SMEM)


def anywhere():
    return pl.BlockSpec(memory_space=pltpu.MemorySpace.HBM)


def call(kernel, where, args, outs, scratch=(), far_args=(), copies=0, hbm_out=False, aliases=None):
    space = anywhere if hbm_out else vmem
    far_args = [pltpu.with_memory_space_constraint(a, pltpu.MemorySpace.HBM) for a in far_args]
    return pl.pallas_call(
        kernel,
        out_shape=tuple(jax.ShapeDtypeStruct(shape, dtype) for shape, dtype in outs),
        in_specs=[smem()] + [vmem() for _ in args] + [anywhere() for _ in far_args],
        out_specs=tuple(space() for _ in outs),
        scratch_shapes=[pltpu.VMEM(shape, dtype) for shape, dtype in scratch]
        + ([pltpu.SemaphoreType.DMA((copies,))] if copies else []),
        input_output_aliases=aliases or {},
        compiler_params=pltpu.CompilerParams(vmem_limit_bytes=32 << 20),
    )(where, *args, *far_args)


def per_device(history, adjacency, volume_op, face_lift, schmid_map, hardening):
    count = lax.axis_size("zone")
    groups = lax.axis_size("var")
    flat = history.reshape(ROWS, NZ)
    zone = lax.axis_index("zone")
    var = lax.axis_index("var")
    where = jnp.stack([zone * NZ - 192, var >> 1, var & 1, zone & 1]).astype(jnp.int32)
    near = ((ROWS // 2, LANE), F32)
    far = ((ROWS + 8, LANE), F32)
    near_one, near_two, far_one, far_two, local, faces = call(
        pack_kernel,
        where,
        (),
        [near, near, far, far, ((ROWS, NZ), F32), ((NFACE, NZ), jnp.int32)],
        far_args=(flat, adjacency),
        copies=5,
    )

    def swap_pairs(shift):
        pairs = []
        for z in range(count):
            other = ((z + shift) ^ 1) - shift
            for v in range(groups):
                target = other * groups + v if 0 <= other < count else z * groups + (v ^ 1)
                pairs.append((z * groups + v, target))
        return pairs

    one, two = swap_pairs(1), swap_pairs(0)
    axes = ("zone", "var")
    near_one = lax.ppermute(near_one, axes, one)
    near_two = lax.ppermute(near_two, axes, two)
    far_one = lax.ppermute(far_one, axes, one)
    far_two = lax.ppermute(far_two, axes, two)
    buffer = ((2, KDIM, NV * LANE), BF16)
    wide = lambda n: ((ROWS, n * LANE), F32)
    pair = lambda n: ((2 * ROWS, n * LANE), BF16)
    *inner, weights = call(
        inner_kernel,
        where,
        (local, faces),
        [
            wide(5), pair(3), ((7, 256, MATMUL_FACES * LANE), BF16),
            wide(2), pair(2), wide(1), pair(1), ((2 * NP, KDIM), BF16),
        ],
        [buffer, buffer, ((NP, NP), F32), ((NFACE * NP, NP), F32)],
        far_args=(volume_op, face_lift.reshape(NFACE * NP, NP)),
        copies=2,
    )
    onehots = inner[2]
    middle = call(
        middle_kernel,
        where,
        (local, faces, near_one, near_two, *inner, weights),
        [wide(2), pair(2), wide(2), pair(2), wide(3), pair(3)],
        [pair(2), pair(2), wide(4), pair(4), buffer, buffer],
    )
    piece = ((NV, 32, LANE), F32)
    advected = call(
        edge_kernel,
        where,
        (local, faces, far_one, far_two, onehots, weights, *middle),
        [piece] * 8,
        [
            far, far, pair(2), pair(2), pair(2), pair(2), ((4, 256, MATMUL_FACES * LANE), BF16),
            wide(2), wide(5), pair(5), buffer, buffer,
        ],
    )

    def exchange(piece, dx, dc):
        if dx == 0 and dc == 0:
            return piece
        pairs = [(v, ((v // 2 + dx) % 4) * 2 + ((v % 2) ^ dc)) for v in range(8)]
        return lax.ppermute(piece, "var", pairs)

    points = [exchange(piece, dx, dc) for piece, (dx, dc) in zip(advected, SLOTS)]
    mixing, renewing = call(
        table_kernel,
        where,
        (),
        [((192, ROWS), BF16), ((ROWS, 288), BF16)],
        [((12, 48), F32), ((12, 48), F32)],
        far_args=(schmid_map.T, hardening),
        copies=2,
    )
    renewed = call(
        point_kernel,
        where,
        (mixing, renewing, *points),
        [piece] * 8,
        [((ROWS, 512), BF16), ((ROWS, 512), BF16), ((288, 512), BF16)],
    )
    returned = [exchange(piece, (4 - dx) % 4, dc) for piece, (dx, dc) in zip(renewed, SLOTS)]
    out = call(
        merge_kernel(EARLY), where, [returned[i] for i in EARLY], [((NV, NP, NZ), F32)],
        copies=len(EARLY), hbm_out=True,
    )[0]
    return call(
        merge_kernel(LATE), where, [returned[i] for i in LATE], [((NV, NP, NZ), F32)],
        far_args=(out,), copies=len(LATE), hbm_out=True, aliases={1 + len(LATE): 0},
    )[0]


def solution(mesh):
    in_specs = (P("var", None, "zone"), P(None, "zone"), P(), P(), P(), P())
    out_specs = P("var", None, "zone")

    return jax.shard_map(per_device, mesh=mesh, in_specs=in_specs, out_specs=out_specs, check_vma=False)
```

profile of v0, /device:TPU:120, one launch (start us, length us, event | category | flops | bytes accessed | tf_op | source)
XLA Modules:
  0.0 54.0 jit_solution(7962164509873372424)
XLA Ops:
  0.0 0.1 pad_add_fusion.place_ref
  0.1 2.1 %shard_map.65 = (f32[192,128]{1,0:T(8,128)S(1)}, f32[192,128]{1,0:T(8,128)S(1)}, f32[392,128]{1,0:T(8,128)S(1)}, f32[392,128]{1,0:T(8,128)S(1)}, f32[384,512]{1,0:T(8,128)S(1)}, /*index=5*/s32[6,512]{1,0:T(8,128)S(1)}) custom-call(s32[4]{0:T(128)S(1)} %pad_add_fusion.place_ref, f32[384,512]{1,0:T(8,128)} %bitcast.7, s32[6,512]{1,0:T(8,128)} %adjacency_hbm.1), custom_call_target="tpu_custom_call" | custom-call | tf_op jit(solution)/shard_map/pallas_call | solution.py:401
  2.2 2.9 %collective-permute-start = (f32[392,128]{1,0:T(8,128)S(1)}, f32[392,128]{1,0:T(8,128)S(1)}, u32[]{:S(2)}, u32[]{:S(2)}) collective-permute-start(f32[392,128]{1,0:T(8,128)S(1)} %get-tuple-element.47), channel_id=1, source_target_pairs={{0,1},{1,0},{2,3},{3,2},{4,5},{5,4},{6,7},{7,6},{8,16},{9,17},{10,... | collective-permute-start | bytes 602120 | tf_op jit(solution)/shard_map/ppermute | solution.py:444
  5.0 3.1 %collective-permute-start.2 = (f32[192,128]{1,0:T(8,128)S(1)}, f32[192,128]{1,0:T(8,128)S(1)}, u32[]{:S(2)}, u32[]{:S(2)}) collective-permute-start(f32[192,128]{1,0:T(8,128)S(1)} %get-tuple-element.51), channel_id=1, source_target_pairs={{0,1},{1,0},{2,3},{3,2},{4,5},{5,4},{6,7},{7,6},{8,16},{9,17},{10,... | collective-permute-start | bytes 294920 | tf_op jit(solution)/shard_map/ppermute | solution.py:442
  8.2 0.0 collective-permute-start.3
  8.2 4.0 %shard_map.66 = (f32[384,640]{1,0:T(8,128)S(1)}, bf16[768,384]{1,0:T(8,128)(2,1)S(1)}, bf16[7,256,512]{2,1,0:T(8,128)(2,1)S(1)}, f32[384,256]{1,0:T(8,128)S(1)},...) custom-call(s32[4]{0:T(128)S(1)} %pad_add_fusion.place_ref, ...), custom_call_target="tpu_custom_call" | custom-call | tf_op jit(solution)/shard_map/pallas_call | solution.py:401
  12.2 2.2 %collective-permute-done.2.near_one = f32[192,128]{1,0:T(8,128)S(1)} collective-permute-done((f32[192,128]{1,0:T(8,128)S(1)}, f32[192,128]{1,0:T(8,128)S(1)}, u32[]{:S(2)}, u32[]{:S(2)}) %collective-permute-start.2) | collective-permute-done | bytes 98336 | tf_op jit(solution)/shard_map/ppermute | solution.py:442
  14.4 3.0 %shard_map.67 = (f32[384,256]{1,0:T(8,128)S(1)}, bf16[768,256]{1,0:T(8,128)(2,1)S(1)}, f32[384,256]{1,0:T(8,128)S(1)}, bf16[768,256]{1,0:T(8,128)(2,1)S(1)}, f32...) custom-call(s32[4]{0:T(128)S(1)} %pad_add_fusion.place_ref, f32[384,512]{1,0:T(8,128)S(1)} %get-tuple-element.45.history, ...), custom_call_target="tpu_custom_call" | custom-call | tf_op jit(solution)/shard_map/pallas_call | solution.py:401
  17.5 5.4 %shard_map.68 = (f32[6,32,128]{2,1,0:T(8,128)S(1)}, f32[6,32,128]{2,1,0:T(8,128)S(1)}, f32[6,32,128]{2,1,0:T(8,128)S(1)}, f32[6,32,128]{2,1,0:T(8,128)S(1)}, f32...) custom-call(s32[4]{0:T(128)S(1)} %pad_add_fusion.place_ref, ...), custom_call_target="tpu_custom_call" | custom-call | tf_op jit(solution)/shard_map/pallas_call | solution.py:401
  22.9 0.1 collective-permute-start.10
  23.0 3.3 %collective-permute-start.4 = (f32[6,32,128]{2,1,0:T(8,128)S(1)}, f32[6,32,128]{2,1,0:T(8,128)S(1)}, u32[]{:S(2)}, u32[]{:S(2)}) collective-permute-start(f32[6,32,128]{2,1,0:T(8,128)S(1)} %get-tuple-element.66), channel_id=1, source_target_pairs={{0,4},{1,5},{2,6},{3,7},{4,0},{5,1},{6,2},{7,3},{8,12},{9,13},{10,... | collective-permute-start | bytes 294920 | tf_op jit(solution)/shard_map/ppermute | solution.py:485
  26.3 0.1 collective-permute-start.5
  26.3 1.5 %collective-permute-start.6 = (f32[6,32,128]{2,1,0:T(8,128)S(1)}, f32[6,32,128]{2,1,0:T(8,128)S(1)}, u32[]{:S(2)}, u32[]{:S(2)}) collective-permute-start(f32[6,32,128]{2,1,0:T(8,128)S(1)} %get-tuple-element.68), channel_id=1, source_target_pairs={{0,2},{1,3},{2,4},{3,5},{4,6},{5,7},{6,0},{7,1},{8,10},{9,11},{10,... | collective-permute-start | bytes 294920 | tf_op jit(solution)/shard_map/ppermute | solution.py:485
  27.8 1.7 %collective-permute-start.7 = (f32[6,32,128]{2,1,0:T(8,128)S(1)}, f32[6,32,128]{2,1,0:T(8,128)S(1)}, u32[]{:S(2)}, u32[]{:S(2)}) collective-permute-start(f32[6,32,128]{2,1,0:T(8,128)S(1)} %get-tuple-element.69), channel_id=1, source_target_pairs={{0,6},{1,7},{2,0},{3,1},{4,2},{5,3},{6,4},{7,5},{8,14},{9,15},{10,... | collective-permute-start | bytes 294920 | tf_op jit(solution)/shard_map/ppermute | solution.py:485
  29.6 0.1 collective-permute-done.4.rest_1_
  29.7 2.9 %collective-permute-start.9 = (f32[6,32,128]{2,1,0:T(8,128)S(1)}, f32[6,32,128]{2,1,0:T(8,128)S(1)}, u32[]{:S(2)}, u32[]{:S(2)}) collective-permute-start(f32[6,32,128]{2,1,0:T(8,128)S(1)} %get-tuple-element.71), channel_id=1, source_target_pairs={{0,7},{1,6},{2,1},{3,0},{4,3},{5,2},{6,5},{7,4},{8,15},{9,14},{10,... | collective-permute-start | bytes 294920 | tf_op jit(solution)/shard_map/ppermute | solution.py:485
  32.5 2.0 %shard_map.64 = (bf16[192,384]{1,0:T(8,128)(2,1)S(1)}, bf16[384,288]{1,0:T(8,128)(2,1)S(1)}) custom-call(s32[4]{0:T(128)S(1)} %pad_add_fusion.place_ref, f32[12,48]{1,0:T(8,128)} %bitcast.9, f32[12,48]{1,0:T(8,128)} %hardening_hbm.1), custom_call_target="tpu_custom_call" | custom-call | tf_op jit(solution)/shard_map/pallas_call | solution.py:401
  34.5 0.6 %collective-permute-done.6.rest_3_ = f32[6,32,128]{2,1,0:T(8,128)S(1)} collective-permute-done((f32[6,32,128]{2,1,0:T(8,128)S(1)}, f32[6,32,128]{2,1,0:T(8,128)S(1)}, u32[]{:S(2)}, u32[]{:S(2)}) %collective-permute-start.6) | collective-permute-done | bytes 98336 | tf_op jit(solution)/shard_map/ppermute | solution.py:485
  35.1 1.8 %collective-permute-done.8.rest_5_ = f32[6,32,128]{2,1,0:T(8,128)S(1)} collective-permute-done((f32[6,32,128]{2,1,0:T(8,128)S(1)}, f32[6,32,128]{2,1,0:T(8,128)S(1)}, u32[]{:S(2)}, u32[]{:S(2)}) %collective-permute-start.8) | collective-permute-done | bytes 98336 | tf_op jit(solution)/shard_map/ppermute | solution.py:485
  36.9 1.4 %shard_map.69 = (f32[6,32,128]{2,1,0:T(8,128)S(1)}, f32[6,32,128]{2,1,0:T(8,128)S(1)}, f32[6,32,128]{2,1,0:T(8,128)S(1)}, f32[6,32,128]{2,1,0:T(8,128)S(1)}, f32...) custom-call(s32[4]{0:T(128)S(1)} %pad_add_fusion.place_ref, ...), custom_call_target="tpu_custom_call" | custom-call | tf_op jit(solution)/shard_map/pallas_call | solution.py:401
  38.2 2.2 %collective-permute-start.15 = (f32[6,32,128]{2,1,0:T(8,128)S(1)}, f32[6,32,128]{2,1,0:T(8,128)S(1)}, u32[]{:S(2)}, u32[]{:S(2)}) collective-permute-start(f32[6,32,128]{2,1,0:T(8,128)S(1)} %get-tuple-element.78), channel_id=1, source_target_pairs={{0,4},{1,5},{2,6},{3,7},{4,0},{5,1},{6,2},{7,3},{8,12},{9,13},{10,... | collective-permute-start | bytes 294920 | tf_op jit(solution)/shard_map/ppermute | solution.py:485
  40.4 0.8 %collective-permute-start.16 = (f32[6,32,128]{2,1,0:T(8,128)S(1)}, f32[6,32,128]{2,1,0:T(8,128)S(1)}, u32[]{:S(2)}, u32[]{:S(2)}) collective-permute-start(f32[6,32,128]{2,1,0:T(8,128)S(1)} %get-tuple-element.79), channel_id=1, source_target_pairs={{0,5},{1,4},{2,7},{3,6},{4,1},{5,0},{6,3},{7,2},{8,13},{9,12},{10,... | collective-permute-start | bytes 294920 | tf_op jit(solution)/shard_map/ppermute | solution.py:485
  41.3 0.7 %collective-permute-start.17 = (f32[6,32,128]{2,1,0:T(8,128)S(1)}, f32[6,32,128]{2,1,0:T(8,128)S(1)}, u32[]{:S(2)}, u32[]{:S(2)}) collective-permute-start(f32[6,32,128]{2,1,0:T(8,128)S(1)} %get-tuple-element.80), channel_id=1, source_target_pairs={{0,1},{1,0},{2,3},{3,2},{4,5},{5,4},{6,7},{7,6},{8,9},{9,8},{10,11... | collective-permute-start | bytes 294920 | tf_op jit(solution)/shard_map/ppermute | solution.py:485
  42.0 2.3 %collective-permute-start.11 = (f32[6,32,128]{2,1,0:T(8,128)S(1)}, f32[6,32,128]{2,1,0:T(8,128)S(1)}, u32[]{:S(2)}, u32[]{:S(2)}) collective-permute-start(f32[6,32,128]{2,1,0:T(8,128)S(1)} %get-tuple-element.73), channel_id=1, source_target_pairs={{0,6},{1,7},{2,0},{3,1},{4,2},{5,3},{6,4},{7,5},{8,14},{9,15},{10,... | collective-permute-start | bytes 294920 | tf_op jit(solution)/shard_map/ppermute | solution.py:485
  44.2 0.4 collective-permute-done.15.rest_1_
  44.6 1.9 %collective-permute-start.13 = (f32[6,32,128]{2,1,0:T(8,128)S(1)}, f32[6,32,128]{2,1,0:T(8,128)S(1)}, u32[]{:S(2)}, u32[]{:S(2)}) collective-permute-start(f32[6,32,128]{2,1,0:T(8,128)S(1)} %get-tuple-element.75), channel_id=1, source_target_pairs={{0,7},{1,6},{2,1},{3,0},{4,3},{5,2},{6,5},{7,4},{8,15},{9,14},{10,... | collective-permute-start | bytes 294920 | tf_op jit(solution)/shard_map/ppermute | solution.py:485
  46.5 0.5 collective-permute-done.16.rest_2_
  47.0 0.8 %collective-permute-start.14 = (f32[6,32,128]{2,1,0:T(8,128)S(1)}, f32[6,32,128]{2,1,0:T(8,128)S(1)}, u32[]{:S(2)}, u32[]{:S(2)}) collective-permute-start(f32[6,32,128]{2,1,0:T(8,128)S(1)} %get-tuple-element.76), channel_id=1, source_target_pairs={{0,3},{1,2},{2,5},{3,4},{4,7},{5,6},{6,1},{7,0},{8,11},{9,10},{10,... | collective-permute-start | bytes 294920 | tf_op jit(solution)/shard_map/ppermute | solution.py:485
  47.8 1.3 %shard_map.70.rest_4_ = f32[6,64,512]{2,1,0:T(8,128)} custom-call(s32[4]{0:T(128)S(1)} %pad_add_fusion.place_ref, f32[6,32,128]{2,1,0:T(8,128)S(1)} %get-tuple-element.77.rest_0_, f32[6,32,128]{2,1,0:T(8,128)S(1)} %collective-permute-done.15.rest_1_, f32[6,32,128]{2,1,0:T(8,128)S(1)} %collective-permute-done.16.rest_2_, ...), custom_call_target="tpu_custom_call" | custom-call | tf_op jit(solution)/shard_map/pallas_call | solution.py:401
  49.1 0.9 %collective-permute-done.12.rest_1_ = f32[6,32,128]{2,1,0:T(8,128)S(1)} collective-permute-done((f32[6,32,128]{2,1,0:T(8,128)S(1)}, f32[6,32,128]{2,1,0:T(8,128)S(1)}, u32[]{:S(2)}, u32[]{:S(2)}) %collective-permute-start.12) | collective-permute-done | bytes 98336 | tf_op jit(solution)/shard_map/ppermute | solution.py:485
  50.0 2.4 %collective-permute-done.14.rest_3_ = f32[6,32,128]{2,1,0:T(8,128)S(1)} collective-permute-done((f32[6,32,128]{2,1,0:T(8,128)S(1)}, f32[6,32,128]{2,1,0:T(8,128)S(1)}, u32[]{:S(2)}, u32[]{:S(2)}) %collective-permute-start.14) | collective-permute-done | bytes 98336 | tf_op jit(solution)/shard_map/ppermute | solution.py:485
  52.5 1.3 %shard_map.71 = f32[6,64,512]{2,1,0:T(8,128)} custom-call(s32[4]{0:T(128)S(1)} %pad_add_fusion.place_ref, f32[6,32,128]{2,1,0:T(8,128)S(1)} %collective-permute-done.11.rest_0_, f32[6,32,128]{2,1,0:T(8,128)S(1)} %collective-permute-done.12.rest_1_, f32[6,32,128]{2,1,0:T(8,128)S(1)} %collective-permute-done.13.rest_2_, ...), custom_call_target="tpu_custom_call", output_to_operand_aliasing={{}: (5, {})} | custom-call | tf_op jit(solution)/shard_map/pallas_call | solution.py:401
  (13 shorter events, 0.0 us)
Async XLA Ops:
  2.2 15.3 %collective-permute-start = (f32[392,128]{1,0:T(8,128)S(1)}, f32[392,128]{1,0:T(8,128)S(1)}, u32[]{:S(2)}, u32[]{:S(2)}) collective-permute-start(f32[392,128]{1,0:T(8,128)S(1)} %get-tuple-element.47), channel_id=1, source_target_pairs={{0,1},{1,0},{2,3},{3,2},{4,5},{5,4},{6,7},{7,6},{8,16},{9,17},{10,... | collective-permute-start | bytes 602120 | tf_op jit(solution)/shard_map/ppermute | solution.py:444
  5.0 12.4 %collective-permute-start.1 = (f32[392,128]{1,0:T(8,128)S(1)}, f32[392,128]{1,0:T(8,128)S(1)}, u32[]{:S(2)}, u32[]{:S(2)}) collective-permute-start(f32[392,128]{1,0:T(8,128)S(1)} %get-tuple-element.48), channel_id=1, source_target_pairs={{0,8},{1,9},{2,10},{3,11},{4,12},{5,13},{6,14},{7,15},{8,0},{9,1},... | collective-permute-start | bytes 602120 | tf_op jit(solution)/shard_map/ppermute | solution.py:445
  5.0 9.4 %collective-permute-start.2 = (f32[192,128]{1,0:T(8,128)S(1)}, f32[192,128]{1,0:T(8,128)S(1)}, u32[]{:S(2)}, u32[]{:S(2)}) collective-permute-start(f32[192,128]{1,0:T(8,128)S(1)} %get-tuple-element.51), channel_id=1, source_target_pairs={{0,1},{1,0},{2,3},{3,2},{4,5},{5,4},{6,7},{7,6},{8,16},{9,17},{10,... | collective-permute-start | bytes 294920 | tf_op jit(solution)/shard_map/ppermute | solution.py:442
  8.2 6.2 %collective-permute-start.3 = (f32[192,128]{1,0:T(8,128)S(1)}, f32[192,128]{1,0:T(8,128)S(1)}, u32[]{:S(2)}, u32[]{:S(2)}) collective-permute-start(f32[192,128]{1,0:T(8,128)S(1)} %get-tuple-element.52), channel_id=1, source_target_pairs={{0,8},{1,9},{2,10},{3,11},{4,12},{5,13},{6,14},{7,15},{8,0},{9,1},... | collective-permute-start | bytes 294920 | tf_op jit(solution)/shard_map/ppermute | solution.py:443
  22.9 6.7 %collective-permute-start.10 = (f32[6,32,128]{2,1,0:T(8,128)S(1)}, f32[6,32,128]{2,1,0:T(8,128)S(1)}, u32[]{:S(2)}, u32[]{:S(2)}) collective-permute-start(f32[6,32,128]{2,1,0:T(8,128)S(1)} %get-tuple-element.72), channel_id=1, source_target_pairs={{0,1},{1,0},{2,3},{3,2},{4,5},{5,4},{6,7},{7,6},{8,9},{9,8},{10,11... | collective-permute-start | bytes 294920 | tf_op jit(solution)/shard_map/ppermute | solution.py:485
  23.0 6.7 %collective-permute-start.4 = (f32[6,32,128]{2,1,0:T(8,128)S(1)}, f32[6,32,128]{2,1,0:T(8,128)S(1)}, u32[]{:S(2)}, u32[]{:S(2)}) collective-permute-start(f32[6,32,128]{2,1,0:T(8,128)S(1)} %get-tuple-element.66), channel_id=1, source_target_pairs={{0,4},{1,5},{2,6},{3,7},{4,0},{5,1},{6,2},{7,3},{8,12},{9,13},{10,... | collective-permute-start | bytes 294920 | tf_op jit(solution)/shard_map/ppermute | solution.py:485
  26.3 8.2 %collective-permute-start.5 = (f32[6,32,128]{2,1,0:T(8,128)S(1)}, f32[6,32,128]{2,1,0:T(8,128)S(1)}, u32[]{:S(2)}, u32[]{:S(2)}) collective-permute-start(f32[6,32,128]{2,1,0:T(8,128)S(1)} %get-tuple-element.67), channel_id=1, source_target_pairs={{0,5},{1,4},{2,7},{3,6},{4,1},{5,0},{6,3},{7,2},{8,13},{9,12},{10,... | collective-permute-start | bytes 294920 | tf_op jit(solution)/shard_map/ppermute | solution.py:485
  26.3 8.7 %collective-permute-start.6 = (f32[6,32,128]{2,1,0:T(8,128)S(1)}, f32[6,32,128]{2,1,0:T(8,128)S(1)}, u32[]{:S(2)}, u32[]{:S(2)}) collective-permute-start(f32[6,32,128]{2,1,0:T(8,128)S(1)} %get-tuple-element.68), channel_id=1, source_target_pairs={{0,2},{1,3},{2,4},{3,5},{4,6},{5,7},{6,0},{7,1},{8,10},{9,11},{10,... | collective-permute-start | bytes 294920 | tf_op jit(solution)/shard_map/ppermute | solution.py:485
  27.8 7.2 %collective-permute-start.7 = (f32[6,32,128]{2,1,0:T(8,128)S(1)}, f32[6,32,128]{2,1,0:T(8,128)S(1)}, u32[]{:S(2)}, u32[]{:S(2)}) collective-permute-start(f32[6,32,128]{2,1,0:T(8,128)S(1)} %get-tuple-element.69), channel_id=1, source_target_pairs={{0,6},{1,7},{2,0},{3,1},{4,2},{5,3},{6,4},{7,5},{8,14},{9,15},{10,... | collective-permute-start | bytes 294920 | tf_op jit(solution)/shard_map/ppermute | solution.py:485
  29.6 7.3 %collective-permute-start.8 = (f32[6,32,128]{2,1,0:T(8,128)S(1)}, f32[6,32,128]{2,1,0:T(8,128)S(1)}, u32[]{:S(2)}, u32[]{:S(2)}) collective-permute-start(f32[6,32,128]{2,1,0:T(8,128)S(1)} %get-tuple-element.70), channel_id=1, source_target_pairs={{0,3},{1,2},{2,5},{3,4},{4,7},{5,6},{6,1},{7,0},{8,11},{9,10},{10,... | collective-permute-start | bytes 294920 | tf_op jit(solution)/shard_map/ppermute | solution.py:485
  29.7 7.2 %collective-permute-start.9 = (f32[6,32,128]{2,1,0:T(8,128)S(1)}, f32[6,32,128]{2,1,0:T(8,128)S(1)}, u32[]{:S(2)}, u32[]{:S(2)}) collective-permute-start(f32[6,32,128]{2,1,0:T(8,128)S(1)} %get-tuple-element.71), channel_id=1, source_target_pairs={{0,7},{1,6},{2,1},{3,0},{4,3},{5,2},{6,5},{7,4},{8,15},{9,14},{10,... | collective-permute-start | bytes 294920 | tf_op jit(solution)/shard_map/ppermute | solution.py:485
  38.2 6.4 %collective-permute-start.15 = (f32[6,32,128]{2,1,0:T(8,128)S(1)}, f32[6,32,128]{2,1,0:T(8,128)S(1)}, u32[]{:S(2)}, u32[]{:S(2)}) collective-permute-start(f32[6,32,128]{2,1,0:T(8,128)S(1)} %get-tuple-element.78), channel_id=1, source_target_pairs={{0,4},{1,5},{2,6},{3,7},{4,0},{5,1},{6,2},{7,3},{8,12},{9,13},{10,... | collective-permute-start | bytes 294920 | tf_op jit(solution)/shard_map/ppermute | solution.py:485
  40.4 6.6 %collective-permute-start.16 = (f32[6,32,128]{2,1,0:T(8,128)S(1)}, f32[6,32,128]{2,1,0:T(8,128)S(1)}, u32[]{:S(2)}, u32[]{:S(2)}) collective-permute-start(f32[6,32,128]{2,1,0:T(8,128)S(1)} %get-tuple-element.79), channel_id=1, source_target_pairs={{0,5},{1,4},{2,7},{3,6},{4,1},{5,0},{6,3},{7,2},{8,13},{9,12},{10,... | collective-permute-start | bytes 294920 | tf_op jit(solution)/shard_map/ppermute | solution.py:485
  41.3 6.5 %collective-permute-start.17 = (f32[6,32,128]{2,1,0:T(8,128)S(1)}, f32[6,32,128]{2,1,0:T(8,128)S(1)}, u32[]{:S(2)}, u32[]{:S(2)}) collective-permute-start(f32[6,32,128]{2,1,0:T(8,128)S(1)} %get-tuple-element.80), channel_id=1, source_target_pairs={{0,1},{1,0},{2,3},{3,2},{4,5},{5,4},{6,7},{7,6},{8,9},{9,8},{10,11... | collective-permute-start | bytes 294920 | tf_op jit(solution)/shard_map/ppermute | solution.py:485
  42.0 7.2 %collective-permute-start.11 = (f32[6,32,128]{2,1,0:T(8,128)S(1)}, f32[6,32,128]{2,1,0:T(8,128)S(1)}, u32[]{:S(2)}, u32[]{:S(2)}) collective-permute-start(f32[6,32,128]{2,1,0:T(8,128)S(1)} %get-tuple-element.73), channel_id=1, source_target_pairs={{0,6},{1,7},{2,0},{3,1},{4,2},{5,3},{6,4},{7,5},{8,14},{9,15},{10,... | collective-permute-start | bytes 294920 | tf_op jit(solution)/shard_map/ppermute | solution.py:485
  44.2 5.8 %collective-permute-start.12 = (f32[6,32,128]{2,1,0:T(8,128)S(1)}, f32[6,32,128]{2,1,0:T(8,128)S(1)}, u32[]{:S(2)}, u32[]{:S(2)}) collective-permute-start(f32[6,32,128]{2,1,0:T(8,128)S(1)} %get-tuple-element.74), channel_id=1, source_target_pairs={{0,2},{1,3},{2,4},{3,5},{4,6},{5,7},{6,0},{7,1},{8,10},{9,11},{10,... | collective-permute-start | bytes 294920 | tf_op jit(solution)/shard_map/ppermute | solution.py:485
  44.6 5.4 %collective-permute-start.13 = (f32[6,32,128]{2,1,0:T(8,128)S(1)}, f32[6,32,128]{2,1,0:T(8,128)S(1)}, u32[]{:S(2)}, u32[]{:S(2)}) collective-permute-start(f32[6,32,128]{2,1,0:T(8,128)S(1)} %get-tuple-element.75), channel_id=1, source_target_pairs={{0,7},{1,6},{2,1},{3,0},{4,3},{5,2},{6,5},{7,4},{8,15},{9,14},{10,... | collective-permute-start | bytes 294920 | tf_op jit(solution)/shard_map/ppermute | solution.py:485
  47.0 5.5 %collective-permute-start.14 = (f32[6,32,128]{2,1,0:T(8,128)S(1)}, f32[6,32,128]{2,1,0:T(8,128)S(1)}, u32[]{:S(2)}, u32[]{:S(2)}) collective-permute-start(f32[6,32,128]{2,1,0:T(8,128)S(1)} %get-tuple-element.76), channel_id=1, source_target_pairs={{0,3},{1,2},{2,5},{3,4},{4,7},{5,6},{6,1},{7,0},{8,11},{9,10},{10,... | collective-permute-start | bytes 294920 | tf_op jit(solution)/shard_map/ppermute | solution.py:485
where the time goes:
time: 54.9 us; the launch traced here: 54 us
  starting transfers between devices  24.2 us (44%)
  Pallas kernels  20.5 us (37%)
  waiting for transfers between devices  8.96 us (16%)
    pallas_call x8, Pallas kernels, call(): pl.pallas_call(kernel, out_shape=tuple((jax.ShapeDtypeStruct(shape, dtype...  20.5 us
    ppermute x14, starting transfers between devices, exchange(): return lax.ppermute(piece, 'var', pairs)  18.2 us
    ppermute x14, waiting for transfers between devices, exchange(): return lax.ppermute(piece, 'var', pairs)  6.76 us
    ppermute x1, starting transfers between devices, per_device(): near_one = lax.ppermute(near_one, axes, one)  3.15 us
    ppermute x1, starting transfers between devices, per_device(): far_one = lax.ppermute(far_one, axes, one)  2.87 us
    ppermute x1, waiting for transfers between devices, per_device(): near_one = lax.ppermute(near_one, axes, one)  2.19 us
  transfers between devices with their start and end apart: 18, of which 8 were waited for; matrix products, arithmetic and copies ran while one was open for 0% of the time, Pallas kernels for 19%

commit v1 on v0

--- a/solution.py
+++ b/solution.py
@@ -58,36 +58,35 @@
 
 
 def pack_kernel(
-    place_ref, history_hbm, adjacency_hbm, near_one, near_two, far_one, far_two, history, adjacency, sems
+    place_ref, history_hbm, adjacency_hbm, volume_hbm, face_hbm,
+    near_one, near_two, far_one, far_two, history, adjacency, volume_op, face_lift, sems,
 ):
     half = ROWS // 2
     first = first_half(half)
-    odd = place_ref[3] == 1
     copies = fetch(
-        [(history_hbm.at[:, cols(c)], history.at[:, cols(c)]) for c in (0, 3, 1, 2)] + [(adjacency_hbm, adjacency)],
+        [(history_hbm.at[:, cols(c)], history.at[:, cols(c)]) for c in (0, 3, 1, 2)]
+        + [(adjacency_hbm, adjacency), (volume_hbm, volume_op), (face_hbm, face_lift)],
         sems,
     )
-
-    def put(one, two, rows, forward, backward):
-        one[rows, :] = jnp.where(odd, forward, backward)
-        two[rows, :] = jnp.where(odd, backward, forward)
-
-    copies[0].wait()
-    copies[1].wait()
-    forward = jnp.where(first, swap(history[0:half, cols(3)]), history[half:, cols(3)])
-    backward = jnp.where(first, history[0:half, cols(0)], swap(history[half:, cols(0)]))
-    put(near_one, near_two, slice(0, half), forward, backward)
-    copies[2].wait()
-    copies[3].wait()
-    forward = straddle(history[:, cols(2)], history[:, cols(3)])
-    backward = straddle(history[:, cols(0)], history[:, cols(1)])
-    put(far_one, far_two, slice(0, ROWS), forward, backward)
-    copies[4].wait()
-    for target in (far_one, far_two):
-        target[ROWS:, :] = jnp.zeros((8, LANE), F32)
-    put(
-        far_one, far_two, slice(ROWS, ROWS + NFACE), adjacency[:, cols(3)].astype(F32), adjacency[:, cols(0)].astype(F32)
-    )
+    for copy in copies:
+        copy.wait()
+
+    def put(near_up, near_down, far_up, far_down):
+        near_up[...] = jnp.where(first, swap(history[0:half, cols(3)]), history[half:, cols(3)])
+        near_down[...] = jnp.where(first, history[0:half, cols(0)], swap(history[half:, cols(0)]))
+        far_up[0:ROWS, :] = straddle(history[:, cols(2)], history[:, cols(3)])
+        far_down[0:ROWS, :] = straddle(history[:, cols(0)], history[:, cols(1)])
+        for target, c in ((far_up, 3), (far_down, 0)):
+            target[ROWS:, :] = jnp.zeros((8, LANE), F32)
+            target[ROWS : ROWS + NFACE, :] = adjacency[:, cols(c)].astype(F32)
+
+    @pl.when(place_ref[3] == 1)
+    def _():
+        put(near_one, near_two, far_one, far_two)
+
+    @pl.when(place_ref[3] == 0)
+    def _():
+        put(near_two, near_one, far_two, far_one)
 
 
 def place(adjacency, start):
@@ -145,11 +144,10 @@
 
 
 def inner_kernel(
-    place_ref, history, adjacency, volume_hbm, face_hbm,
+    place_ref, history, adjacency, volume_op, face_lift,
     u0, parts, onehots, t1, parts2, t2, parts3, weights,
-    gat_a, gat_b, volume_op, face_lift, sems,
+    gat_a, gat_b,
 ):
-    copies = fetch([(volume_hbm, volume_op), (face_hbm, face_lift)], sems)
     origin = place_ref[0]
     zero = jnp.zeros((ROWS, LANE), F32)
     blocks = [history[:, cols(b)] for b in range(4)]
@@ -163,8 +161,6 @@
     near = [mix(adjacency[:, cols(b)], adjacency[:, cols(b + 1)]) for b in range(3)]
     for b in range(3):
         write_onehots(onehots, 4 + b, place(near[b], origin + (128 * b + 192)))
-    for copy in copies:
-        copy.wait()
     for lanes, matrix in ((slice(0, 384), face_lift[...].T), (slice(384, 448), volume_op[...].T)):
         high, low = split(matrix)
         weights[0:NP, lanes] = high
@@ -387,45 +383,50 @@
     return pl.BlockSpec(memory_space=pltpu.VMEM)
 
 
-def smem():
-    return pl.BlockSpec(memory_space=pltpu.SMEM)
-
-
 def anywhere():
     return pl.BlockSpec(memory_space=pltpu.MemorySpace.HBM)
 
 
-def call(kernel, where, args, outs, scratch=(), far_args=(), copies=0, hbm_out=False, aliases=None):
+def position():
+    zone = lax.axis_index("zone")
+    var = lax.axis_index("var")
+    return zone * NZ - 192, var >> 1, var & 1, zone & 1
+
+
+def call(kernel, args, outs, scratch=(), far_args=(), copies=0, hbm_out=False, aliases=None):
     space = anywhere if hbm_out else vmem
     far_args = [pltpu.with_memory_space_constraint(a, pltpu.MemorySpace.HBM) for a in far_args]
+
+
+    def placed(*refs):
+        kernel(position(), *refs)
+
     return pl.pallas_call(
-        kernel,
+        placed,
         out_shape=tuple(jax.ShapeDtypeStruct(shape, dtype) for shape, dtype in outs),
-        in_specs=[smem()] + [vmem() for _ in args] + [anywhere() for _ in far_args],
+        in_specs=[vmem() for _ in args] + [anywhere() for _ in far_args],
         out_specs=tuple(space() for _ in outs),
         scratch_shapes=[pltpu.VMEM(shape, dtype) for shape, dtype in scratch]
         + ([pltpu.SemaphoreType.DMA((copies,))] if copies else []),
         input_output_aliases=aliases or {},
         compiler_params=pltpu.CompilerParams(vmem_limit_bytes=32 << 20),
-    )(where, *args, *far_args)
+    )(*args, *far_args)
 
 
 def per_device(history, adjacency, volume_op, face_lift, schmid_map, hardening):
     count = lax.axis_size("zone")
     groups = lax.axis_size("var")
     flat = history.reshape(ROWS, NZ)
-    zone = lax.axis_index("zone")
-    var = lax.axis_index("var")
-    where = jnp.stack([zone * NZ - 192, var >> 1, var & 1, zone & 1]).astype(jnp.int32)
     near = ((ROWS // 2, LANE), F32)
     far = ((ROWS + 8, LANE), F32)
-    near_one, near_two, far_one, far_two, local, faces = call(
+    near_one, near_two, far_one, far_two, local, faces, volume, lifts = call(
         pack_kernel,
-        where,
         (),
-        [near, near, far, far, ((ROWS, NZ), F32), ((NFACE, NZ), jnp.int32)],
-        far_args=(flat, adjacency),
-        copies=5,
+        [
+            near, near, far, far, ((ROWS, NZ), F32), ((NFACE, NZ), jnp.int32), ((NP, NP), F32), ((NFACE * NP, NP), F32),
+        ],
+        far_args=(flat, adjacency, volume_op, face_lift.reshape(NFACE * NP, NP)),
+        copies=7,
     )
 
     def swap_pairs(shift):
@@ -448,20 +449,16 @@
     pair = lambda n: ((2 * ROWS, n * LANE), BF16)
     *inner, weights = call(
         inner_kernel,
-        where,
-        (local, faces),
+        (local, faces, volume, lifts),
         [
             wide(5), pair(3), ((7, 256, MATMUL_FACES * LANE), BF16),
             wide(2), pair(2), wide(1), pair(1), ((2 * NP, KDIM), BF16),
         ],
-        [buffer, buffer, ((NP, NP), F32), ((NFACE * NP, NP), F32)],
-        far_args=(volume_op, face_lift.reshape(NFACE * NP, NP)),
-        copies=2,
+        [buffer, buffer],
     )
     onehots = inner[2]
     middle = call(
         middle_kernel,
-        where,
         (local, faces, near_one, near_two, *inner, weights),
         [wide(2), pair(2), wide(2), pair(2), wide(3), pair(3)],
         [pair(2), pair(2), wide(4), pair(4), buffer, buffer],
@@ -469,7 +466,6 @@
     piece = ((NV, 32, LANE), F32)
     advected = call(
         edge_kernel,
-        where,
         (local, faces, far_one, far_two, onehots, weights, *middle),
         [piece] * 8,
         [
@@ -487,7 +483,6 @@
     points = [exchange(piece, dx, dc) for piece, (dx, dc) in zip(advected, SLOTS)]
     mixing, renewing = call(
         table_kernel,
-        where,
         (),
         [((192, ROWS), BF16), ((ROWS, 288), BF16)],
         [((12, 48), F32), ((12, 48), F32)],
@@ -496,19 +491,18 @@
     )
     renewed = call(
         point_kernel,
-        where,
         (mixing, renewing, *points),
         [piece] * 8,
         [((ROWS, 512), BF16), ((ROWS, 512), BF16), ((288, 512), BF16)],
     )
     returned = [exchange(piece, (4 - dx) % 4, dc) for piece, (dx, dc) in zip(renewed, SLOTS)]
     out = call(
-        merge_kernel(EARLY), where, [returned[i] for i in EARLY], [((NV, NP, NZ), F32)],
+        merge_kernel(EARLY), [returned[i] for i in EARLY], [((NV, NP, NZ), F32)],
         copies=len(EARLY), hbm_out=True,
     )[0]
     return call(
-        merge_kernel(LATE), where, [returned[i] for i in LATE], [((NV, NP, NZ), F32)],
-        far_args=(out,), copies=len(LATE), hbm_out=True, aliases={1 + len(LATE): 0},
+        merge_kernel(LATE), [returned[i] for i in LATE], [((NV, NP, NZ), F32)],
+        far_args=(out,), copies=len(LATE), hbm_out=True, aliases={len(LATE): 0},
     )[0]
 
 

time: 54.9 us -> 52.2 us (0.951)
  Pallas kernels: 20.5 us -> 15.1 us
  waiting for transfers between devices: 8.96 us -> 11.9 us
    pallas_call x8, Pallas kernels: 20.5 us -> 15.1 us  [call(): pl.pallas_call(placed, out_shape=tuple((jax.ShapeDtypeStruct(shape, dtype...]
    ppermute x1, waiting for transfers between devices: 2.19 us -> 3.81 us  [per_device(): near_one = lax.ppermute(near_one, axes, one)]
    ppermute x14, waiting for transfers between devices: 6.76 us -> 8.04 us  [exchange(): return lax.ppermute(piece, 'var', pairs)]
  transfers between devices with their start and end apart: 18 -> 18, of which waited for: 8 -> 9; matrix products, arithmetic and copies ran while one was open for 0% -> 0% of each run, Pallas kernels for 19% -> 14%
where the time goes in v1:
time: 52.2 us; the launch traced here: 51.3 us
  starting transfers between devices  24.1 us (46%)
  Pallas kernels  15.1 us (29%)
  waiting for transfers between devices  11.9 us (23%)
    ppermute x14, starting transfers between devices, exchange(): return lax.ppermute(piece, 'var', pairs)  18.1 us
    pallas_call x8, Pallas kernels, call(): pl.pallas_call(placed, out_shape=tuple((jax.ShapeDtypeStruct(shape, dtype...  15.1 us
    ppermute x14, waiting for transfers between devices, exchange(): return lax.ppermute(piece, 'var', pairs)  8.04 us
    ppermute x1, waiting for transfers between devices, per_device(): near_one = lax.ppermute(near_one, axes, one)  3.81 us
    ppermute x1, starting transfers between devices, per_device(): near_one = lax.ppermute(near_one, axes, one)  3.15 us
    ppermute x1, starting transfers between devices, per_device(): far_one = lax.ppermute(far_one, axes, one)  2.87 us
  transfers between devices with their start and end apart: 18, of which 9 were waited for; matrix products, arithmetic and copies ran while one was open for 0% of the time, Pallas kernels for 14%

profile of v1, /device:TPU:120, one launch (start us, length us, event | category | flops | bytes accessed | tf_op | source)
XLA Modules:
  0.0 51.3 jit_solution(18036153993236674541)
XLA Ops:
  0.0 1.7 %shard_map.65 = (f32[192,128]{1,0:T(8,128)S(1)}, f32[192,128]{1,0:T(8,128)S(1)}, f32[392,128]{1,0:T(8,128)S(1)}, f32[392,128]{1,0:T(8,128)S(1)}, f32[384,512]{1,...) custom-call(f32[384,512]{1,0:T(8,128)} %bitcast.3, s32[6,512]{1,0:T(8,128)} %refs_1_.3, ...), custom_call_target="tpu_custom_call" | custom-call | tf_op jit(solution)/shard_map/pallas_call | solution.py:404
  1.7 2.9 %collective-permute-start = (f32[392,128]{1,0:T(8,128)S(1)}, f32[392,128]{1,0:T(8,128)S(1)}, u32[]{:S(2)}, u32[]{:S(2)}) collective-permute-start(f32[392,128]{1,0:T(8,128)S(1)} %get-tuple-element.49), channel_id=1, source_target_pairs={{0,1},{1,0},{2,3},{3,2},{4,5},{5,4},{6,7},{7,6},{8,16},{9,17},{10,... | collective-permute-start | bytes 602120 | tf_op jit(solution)/shard_map/ppermute | solution.py:445
  4.6 3.1 %collective-permute-start.2 = (f32[192,128]{1,0:T(8,128)S(1)}, f32[192,128]{1,0:T(8,128)S(1)}, u32[]{:S(2)}, u32[]{:S(2)}) collective-permute-start(f32[192,128]{1,0:T(8,128)S(1)} %get-tuple-element.55), channel_id=1, source_target_pairs={{0,1},{1,0},{2,3},{3,2},{4,5},{5,4},{6,7},{7,6},{8,16},{9,17},{10,... | collective-permute-start | bytes 294920 | tf_op jit(solution)/shard_map/ppermute | solution.py:443
  7.7 2.4 %shard_map.66 = (f32[384,640]{1,0:T(8,128)S(1)}, bf16[768,384]{1,0:T(8,128)(2,1)S(1)}, bf16[7,256,512]{2,1,0:T(8,128)(2,1)S(1)}, f32[384,256]{1,0:T(8,128)S(1)},...) custom-call(f32[384,512]{1,0:T(8,128)S(1)} %get-tuple-element.47.ref, ...), custom_call_target="tpu_custom_call" | custom-call | tf_op jit(solution)/shard_map/pallas_call | solution.py:404
  10.1 3.8 %collective-permute-done.2.refs_2_ = f32[192,128]{1,0:T(8,128)S(1)} collective-permute-done((f32[192,128]{1,0:T(8,128)S(1)}, f32[192,128]{1,0:T(8,128)S(1)}, u32[]{:S(2)}, u32[]{:S(2)}) %collective-permute-start.2) | collective-permute-done | bytes 98336 | tf_op jit(solution)/shard_map/ppermute | solution.py:443
  14.0 2.4 %shard_map.67 = (f32[384,256]{1,0:T(8,128)S(1)}, bf16[768,256]{1,0:T(8,128)(2,1)S(1)}, f32[384,256]{1,0:T(8,128)S(1)}, bf16[768,256]{1,0:T(8,128)(2,1)S(1)}, f32...) custom-call(f32[384,512]{1,0:T(8,128)S(1)} %get-tuple-element.47.refs_0_, s32[6,512]{1,0:T(8,128)S(1)} %get-tuple-element.48.refs_1_, ...), custom_call_target="tpu_custom_call" | custom-call | tf_op jit(solution)/shard_map/pallas_call | solution.py:404
  16.4 0.0 collective-permute-done.refs_2_
  16.4 4.8 %shard_map.68 = (f32[6,32,128]{2,1,0:T(8,128)S(1)}, f32[6,32,128]{2,1,0:T(8,128)S(1)}, f32[6,32,128]{2,1,0:T(8,128)S(1)}, f32[6,32,128]{2,1,0:T(8,128)S(1)}, f32...) custom-call(f32[384,512]{1,0:T(8,128)S(1)} %get-tuple-element.47.refs, ...), custom_call_target="tpu_custom_call" | custom-call | tf_op jit(solution)/shard_map/pallas_call | solution.py:404
  21.2 0.1 collective-permute-start.10
  21.3 3.3 %collective-permute-start.4 = (f32[6,32,128]{2,1,0:T(8,128)S(1)}, f32[6,32,128]{2,1,0:T(8,128)S(1)}, u32[]{:S(2)}, u32[]{:S(2)}) collective-permute-start(f32[6,32,128]{2,1,0:T(8,128)S(1)} %get-tuple-element.70), channel_id=1, source_target_pairs={{0,4},{1,5},{2,6},{3,7},{4,0},{5,1},{6,2},{7,3},{8,12},{9,13},{10,... | collective-permute-start | bytes 294920 | tf_op jit(solution)/shard_map/ppermute | solution.py:481
  24.6 0.0 collective-permute-start.5
  24.7 1.5 %collective-permute-start.6 = (f32[6,32,128]{2,1,0:T(8,128)S(1)}, f32[6,32,128]{2,1,0:T(8,128)S(1)}, u32[]{:S(2)}, u32[]{:S(2)}) collective-permute-start(f32[6,32,128]{2,1,0:T(8,128)S(1)} %get-tuple-element.72), channel_id=1, source_target_pairs={{0,2},{1,3},{2,4},{3,5},{4,6},{5,7},{6,0},{7,1},{8,10},{9,11},{10,... | collective-permute-start | bytes 294920 | tf_op jit(solution)/shard_map/ppermute | solution.py:481
  26.2 1.7 %collective-permute-start.7 = (f32[6,32,128]{2,1,0:T(8,128)S(1)}, f32[6,32,128]{2,1,0:T(8,128)S(1)}, u32[]{:S(2)}, u32[]{:S(2)}) collective-permute-start(f32[6,32,128]{2,1,0:T(8,128)S(1)} %get-tuple-element.73), channel_id=1, source_target_pairs={{0,6},{1,7},{2,0},{3,1},{4,2},{5,3},{6,4},{7,5},{8,14},{9,15},{10,... | collective-permute-start | bytes 294920 | tf_op jit(solution)/shard_map/ppermute | solution.py:481
  27.9 0.1 collective-permute-done.4.refs_3_
  28.0 2.9 %collective-permute-start.9 = (f32[6,32,128]{2,1,0:T(8,128)S(1)}, f32[6,32,128]{2,1,0:T(8,128)S(1)}, u32[]{:S(2)}, u32[]{:S(2)}) collective-permute-start(f32[6,32,128]{2,1,0:T(8,128)S(1)} %get-tuple-element.75), channel_id=1, source_target_pairs={{0,7},{1,6},{2,1},{3,0},{4,3},{5,2},{6,5},{7,4},{8,15},{9,14},{10,... | collective-permute-start | bytes 294920 | tf_op jit(solution)/shard_map/ppermute | solution.py:481
  30.9 1.4 %shard_map.64 = (bf16[192,384]{1,0:T(8,128)(2,1)S(1)}, bf16[384,288]{1,0:T(8,128)(2,1)S(1)}) custom-call(f32[12,48]{1,0:T(8,128)} %bitcast.5, f32[12,48]{1,0:T(8,128)} %refs_1_.2), custom_call_target="tpu_custom_call" | custom-call | tf_op jit(solution)/shard_map/pallas_call | solution.py:404
  32.3 1.1 %collective-permute-done.6.refs_5_ = f32[6,32,128]{2,1,0:T(8,128)S(1)} collective-permute-done((f32[6,32,128]{2,1,0:T(8,128)S(1)}, f32[6,32,128]{2,1,0:T(8,128)S(1)}, u32[]{:S(2)}, u32[]{:S(2)}) %collective-permute-start.6) | collective-permute-done | bytes 98336 | tf_op jit(solution)/shard_map/ppermute | solution.py:481
  33.4 1.7 %collective-permute-done.8.refs_7_ = f32[6,32,128]{2,1,0:T(8,128)S(1)} collective-permute-done((f32[6,32,128]{2,1,0:T(8,128)S(1)}, f32[6,32,128]{2,1,0:T(8,128)S(1)}, u32[]{:S(2)}, u32[]{:S(2)}) %collective-permute-start.8) | collective-permute-done | bytes 98336 | tf_op jit(solution)/shard_map/ppermute | solution.py:481
  35.2 0.8 %shard_map.69 = (f32[6,32,128]{2,1,0:T(8,128)S(1)}, f32[6,32,128]{2,1,0:T(8,128)S(1)}, f32[6,32,128]{2,1,0:T(8,128)S(1)}, f32[6,32,128]{2,1,0:T(8,128)S(1)}, f32...) custom-call(bf16[192,384]{1,0:T(8,128)(2,1)S(1)} %get-tuple-element.4, ...), custom_call_target="tpu_custom_call" | custom-call | tf_op jit(solution)/shard_map/pallas_call | solution.py:404
  36.0 2.2 %collective-permute-start.15 = (f32[6,32,128]{2,1,0:T(8,128)S(1)}, f32[6,32,128]{2,1,0:T(8,128)S(1)}, u32[]{:S(2)}, u32[]{:S(2)}) collective-permute-start(f32[6,32,128]{2,1,0:T(8,128)S(1)} %get-tuple-element.82), channel_id=1, source_target_pairs={{0,4},{1,5},{2,6},{3,7},{4,0},{5,1},{6,2},{7,3},{8,12},{9,13},{10,... | collective-permute-start | bytes 294920 | tf_op jit(solution)/shard_map/ppermute | solution.py:481
  38.2 0.8 %collective-permute-start.16 = (f32[6,32,128]{2,1,0:T(8,128)S(1)}, f32[6,32,128]{2,1,0:T(8,128)S(1)}, u32[]{:S(2)}, u32[]{:S(2)}) collective-permute-start(f32[6,32,128]{2,1,0:T(8,128)S(1)} %get-tuple-element.83), channel_id=1, source_target_pairs={{0,5},{1,4},{2,7},{3,6},{4,1},{5,0},{6,3},{7,2},{8,13},{9,12},{10,... | collective-permute-start | bytes 294920 | tf_op jit(solution)/shard_map/ppermute | solution.py:481
  39.0 0.7 %collective-permute-start.17 = (f32[6,32,128]{2,1,0:T(8,128)S(1)}, f32[6,32,128]{2,1,0:T(8,128)S(1)}, u32[]{:S(2)}, u32[]{:S(2)}) collective-permute-start(f32[6,32,128]{2,1,0:T(8,128)S(1)} %get-tuple-element.84), channel_id=1, source_target_pairs={{0,1},{1,0},{2,3},{3,2},{4,5},{5,4},{6,7},{7,6},{8,9},{9,8},{10,11... | collective-permute-start | bytes 294920 | tf_op jit(solution)/shard_map/ppermute | solution.py:481
  39.7 2.2 %collective-permute-start.11 = (f32[6,32,128]{2,1,0:T(8,128)S(1)}, f32[6,32,128]{2,1,0:T(8,128)S(1)}, u32[]{:S(2)}, u32[]{:S(2)}) collective-permute-start(f32[6,32,128]{2,1,0:T(8,128)S(1)} %get-tuple-element.77), channel_id=1, source_target_pairs={{0,6},{1,7},{2,0},{3,1},{4,2},{5,3},{6,4},{7,5},{8,14},{9,15},{10,... | collective-permute-start | bytes 294920 | tf_op jit(solution)/shard_map/ppermute | solution.py:481
  41.9 0.4 collective-permute-done.15.refs_1_
  42.4 1.9 %collective-permute-start.13 = (f32[6,32,128]{2,1,0:T(8,128)S(1)}, f32[6,32,128]{2,1,0:T(8,128)S(1)}, u32[]{:S(2)}, u32[]{:S(2)}) collective-permute-start(f32[6,32,128]{2,1,0:T(8,128)S(1)} %get-tuple-element.79), channel_id=1, source_target_pairs={{0,7},{1,6},{2,1},{3,0},{4,3},{5,2},{6,5},{7,4},{8,15},{9,14},{10,... | collective-permute-start | bytes 294920 | tf_op jit(solution)/shard_map/ppermute | solution.py:481
  44.2 0.6 %collective-permute-done.16.refs_2_ = f32[6,32,128]{2,1,0:T(8,128)S(1)} collective-permute-done((f32[6,32,128]{2,1,0:T(8,128)S(1)}, f32[6,32,128]{2,1,0:T(8,128)S(1)}, u32[]{:S(2)}, u32[]{:S(2)}) %collective-permute-start.16) | collective-permute-done | bytes 98336 | tf_op jit(solution)/shard_map/ppermute | solution.py:481
  44.8 0.7 %collective-permute-start.14 = (f32[6,32,128]{2,1,0:T(8,128)S(1)}, f32[6,32,128]{2,1,0:T(8,128)S(1)}, u32[]{:S(2)}, u32[]{:S(2)}) collective-permute-start(f32[6,32,128]{2,1,0:T(8,128)S(1)} %get-tuple-element.80), channel_id=1, source_target_pairs={{0,3},{1,2},{2,5},{3,4},{4,7},{5,6},{6,1},{7,0},{8,11},{9,10},{10,... | collective-permute-start | bytes 294920 | tf_op jit(solution)/shard_map/ppermute | solution.py:481
  45.5 0.8 %shard_map.70.refs_4_ = f32[6,64,512]{2,1,0:T(8,128)} custom-call(f32[6,32,128]{2,1,0:T(8,128)S(1)} %get-tuple-element.81.refs_0_, f32[6,32,128]{2,1,0:T(8,128)S(1)} %collective-permute-done.15.refs_1_, f32[6,32,128]{2,1,0:T(8,128)S(1)} %collective-permute-done.16.refs_2_, f32[6,32,128]{2,1,0:T(8,128)S(1)} %collective-permute-done.17.refs_3_), custom_call_target="tpu_custom_call" | custom-call | tf_op jit(solution)/shard_map/pallas_call | solution.py:404
  46.3 0.5 collective-permute-done.11.refs_0_
  46.8 1.0 %collective-permute-done.12.refs_1_ = f32[6,32,128]{2,1,0:T(8,128)S(1)} collective-permute-done((f32[6,32,128]{2,1,0:T(8,128)S(1)}, f32[6,32,128]{2,1,0:T(8,128)S(1)}, u32[]{:S(2)}, u32[]{:S(2)}) %collective-permute-start.12) | collective-permute-done | bytes 98336 | tf_op jit(solution)/shard_map/ppermute | solution.py:481
  47.8 2.6 %collective-permute-done.14.refs_3_ = f32[6,32,128]{2,1,0:T(8,128)S(1)} collective-permute-done((f32[6,32,128]{2,1,0:T(8,128)S(1)}, f32[6,32,128]{2,1,0:T(8,128)S(1)}, u32[]{:S(2)}, u32[]{:S(2)}) %collective-permute-start.14) | collective-permute-done | bytes 98336 | tf_op jit(solution)/shard_map/ppermute | solution.py:481
  50.4 0.8 %shard_map.71 = f32[6,64,512]{2,1,0:T(8,128)} custom-call(f32[6,32,128]{2,1,0:T(8,128)S(1)} %collective-permute-done.11.refs_0_, f32[6,32,128]{2,1,0:T(8,128)S(1)} %collective-permute-done.12.refs_1_, f32[6,32,128]{2,1,0:T(8,128)S(1)} %collective-permute-done.13.refs_2_, ...), custom_call_target="tpu_custom_call", output_to_operand_aliasing={{}: (4, {})} | custom-call | tf_op jit(solution)/shard_map/pallas_call | solution.py:404
  (12 shorter events, 0.0 us)
Async XLA Ops:
  1.7 14.7 %collective-permute-start = (f32[392,128]{1,0:T(8,128)S(1)}, f32[392,128]{1,0:T(8,128)S(1)}, u32[]{:S(2)}, u32[]{:S(2)}) collective-permute-start(f32[392,128]{1,0:T(8,128)S(1)} %get-tuple-element.49), channel_id=1, source_target_pairs={{0,1},{1,0},{2,3},{3,2},{4,5},{5,4},{6,7},{7,6},{8,16},{9,17},{10,... | collective-permute-start | bytes 602120 | tf_op jit(solution)/shard_map/ppermute | solution.py:445
  4.6 11.8 %collective-permute-start.1 = (f32[392,128]{1,0:T(8,128)S(1)}, f32[392,128]{1,0:T(8,128)S(1)}, u32[]{:S(2)}, u32[]{:S(2)}) collective-permute-start(f32[392,128]{1,0:T(8,128)S(1)} %get-tuple-element.50), channel_id=1, source_target_pairs={{0,8},{1,9},{2,10},{3,11},{4,12},{5,13},{6,14},{7,15},{8,0},{9,1},... | collective-permute-start | bytes 602120 | tf_op jit(solution)/shard_map/ppermute | solution.py:446
  4.6 9.4 %collective-permute-start.2 = (f32[192,128]{1,0:T(8,128)S(1)}, f32[192,128]{1,0:T(8,128)S(1)}, u32[]{:S(2)}, u32[]{:S(2)}) collective-permute-start(f32[192,128]{1,0:T(8,128)S(1)} %get-tuple-element.55), channel_id=1, source_target_pairs={{0,1},{1,0},{2,3},{3,2},{4,5},{5,4},{6,7},{7,6},{8,16},{9,17},{10,... | collective-permute-start | bytes 294920 | tf_op jit(solution)/shard_map/ppermute | solution.py:443
  7.7 6.2 %collective-permute-start.3 = (f32[192,128]{1,0:T(8,128)S(1)}, f32[192,128]{1,0:T(8,128)S(1)}, u32[]{:S(2)}, u32[]{:S(2)}) collective-permute-start(f32[192,128]{1,0:T(8,128)S(1)} %get-tuple-element.56), channel_id=1, source_target_pairs={{0,8},{1,9},{2,10},{3,11},{4,12},{5,13},{6,14},{7,15},{8,0},{9,1},... | collective-permute-start | bytes 294920 | tf_op jit(solution)/shard_map/ppermute | solution.py:444
  21.2 6.7 %collective-permute-start.10 = (f32[6,32,128]{2,1,0:T(8,128)S(1)}, f32[6,32,128]{2,1,0:T(8,128)S(1)}, u32[]{:S(2)}, u32[]{:S(2)}) collective-permute-start(f32[6,32,128]{2,1,0:T(8,128)S(1)} %get-tuple-element.76), channel_id=1, source_target_pairs={{0,1},{1,0},{2,3},{3,2},{4,5},{5,4},{6,7},{7,6},{8,9},{9,8},{10,11... | collective-permute-start | bytes 294920 | tf_op jit(solution)/shard_map/ppermute | solution.py:481
  21.3 6.7 %collective-permute-start.4 = (f32[6,32,128]{2,1,0:T(8,128)S(1)}, f32[6,32,128]{2,1,0:T(8,128)S(1)}, u32[]{:S(2)}, u32[]{:S(2)}) collective-permute-start(f32[6,32,128]{2,1,0:T(8,128)S(1)} %get-tuple-element.70), channel_id=1, source_target_pairs={{0,4},{1,5},{2,6},{3,7},{4,0},{5,1},{6,2},{7,3},{8,12},{9,13},{10,... | collective-permute-start | bytes 294920 | tf_op jit(solution)/shard_map/ppermute | solution.py:481
  24.6 7.7 %collective-permute-start.5 = (f32[6,32,128]{2,1,0:T(8,128)S(1)}, f32[6,32,128]{2,1,0:T(8,128)S(1)}, u32[]{:S(2)}, u32[]{:S(2)}) collective-permute-start(f32[6,32,128]{2,1,0:T(8,128)S(1)} %get-tuple-element.71), channel_id=1, source_target_pairs={{0,5},{1,4},{2,7},{3,6},{4,1},{5,0},{6,3},{7,2},{8,13},{9,12},{10,... | collective-permute-start | bytes 294920 | tf_op jit(solution)/shard_map/ppermute | solution.py:481
  24.7 8.8 %collective-permute-start.6 = (f32[6,32,128]{2,1,0:T(8,128)S(1)}, f32[6,32,128]{2,1,0:T(8,128)S(1)}, u32[]{:S(2)}, u32[]{:S(2)}) collective-permute-start(f32[6,32,128]{2,1,0:T(8,128)S(1)} %get-tuple-element.72), channel_id=1, source_target_pairs={{0,2},{1,3},{2,4},{3,5},{4,6},{5,7},{6,0},{7,1},{8,10},{9,11},{10,... | collective-permute-start | bytes 294920 | tf_op jit(solution)/shard_map/ppermute | solution.py:481
  26.2 7.2 %collective-permute-start.7 = (f32[6,32,128]{2,1,0:T(8,128)S(1)}, f32[6,32,128]{2,1,0:T(8,128)S(1)}, u32[]{:S(2)}, u32[]{:S(2)}) collective-permute-start(f32[6,32,128]{2,1,0:T(8,128)S(1)} %get-tuple-element.73), channel_id=1, source_target_pairs={{0,6},{1,7},{2,0},{3,1},{4,2},{5,3},{6,4},{7,5},{8,14},{9,15},{10,... | collective-permute-start | bytes 294920 | tf_op jit(solution)/shard_map/ppermute | solution.py:481
  27.9 7.3 %collective-permute-start.8 = (f32[6,32,128]{2,1,0:T(8,128)S(1)}, f32[6,32,128]{2,1,0:T(8,128)S(1)}, u32[]{:S(2)}, u32[]{:S(2)}) collective-permute-start(f32[6,32,128]{2,1,0:T(8,128)S(1)} %get-tuple-element.74), channel_id=1, source_target_pairs={{0,3},{1,2},{2,5},{3,4},{4,7},{5,6},{6,1},{7,0},{8,11},{9,10},{10,... | collective-permute-start | bytes 294920 | tf_op jit(solution)/shard_map/ppermute | solution.py:481
  28.0 7.2 %collective-permute-start.9 = (f32[6,32,128]{2,1,0:T(8,128)S(1)}, f32[6,32,128]{2,1,0:T(8,128)S(1)}, u32[]{:S(2)}, u32[]{:S(2)}) collective-permute-start(f32[6,32,128]{2,1,0:T(8,128)S(1)} %get-tuple-element.75), channel_id=1, source_target_pairs={{0,7},{1,6},{2,1},{3,0},{4,3},{5,2},{6,5},{7,4},{8,15},{9,14},{10,... | collective-permute-start | bytes 294920 | tf_op jit(solution)/shard_map/ppermute | solution.py:481
  36.0 6.4 %collective-permute-start.15 = (f32[6,32,128]{2,1,0:T(8,128)S(1)}, f32[6,32,128]{2,1,0:T(8,128)S(1)}, u32[]{:S(2)}, u32[]{:S(2)}) collective-permute-start(f32[6,32,128]{2,1,0:T(8,128)S(1)} %get-tuple-element.82), channel_id=1, source_target_pairs={{0,4},{1,5},{2,6},{3,7},{4,0},{5,1},{6,2},{7,3},{8,12},{9,13},{10,... | collective-permute-start | bytes 294920 | tf_op jit(solution)/shard_map/ppermute | solution.py:481
  38.2 6.6 %collective-permute-start.16 = (f32[6,32,128]{2,1,0:T(8,128)S(1)}, f32[6,32,128]{2,1,0:T(8,128)S(1)}, u32[]{:S(2)}, u32[]{:S(2)}) collective-permute-start(f32[6,32,128]{2,1,0:T(8,128)S(1)} %get-tuple-element.83), channel_id=1, source_target_pairs={{0,5},{1,4},{2,7},{3,6},{4,1},{5,0},{6,3},{7,2},{8,13},{9,12},{10,... | collective-permute-start | bytes 294920 | tf_op jit(solution)/shard_map/ppermute | solution.py:481
  39.0 6.5 %collective-permute-start.17 = (f32[6,32,128]{2,1,0:T(8,128)S(1)}, f32[6,32,128]{2,1,0:T(8,128)S(1)}, u32[]{:S(2)}, u32[]{:S(2)}) collective-permute-start(f32[6,32,128]{2,1,0:T(8,128)S(1)} %get-tuple-element.84), channel_id=1, source_target_pairs={{0,1},{1,0},{2,3},{3,2},{4,5},{5,4},{6,7},{7,6},{8,9},{9,8},{10,11... | collective-permute-start | bytes 294920 | tf_op jit(solution)/shard_map/ppermute | solution.py:481
  39.7 7.1 %collective-permute-start.11 = (f32[6,32,128]{2,1,0:T(8,128)S(1)}, f32[6,32,128]{2,1,0:T(8,128)S(1)}, u32[]{:S(2)}, u32[]{:S(2)}) collective-permute-start(f32[6,32,128]{2,1,0:T(8,128)S(1)} %get-tuple-element.77), channel_id=1, source_target_pairs={{0,6},{1,7},{2,0},{3,1},{4,2},{5,3},{6,4},{7,5},{8,14},{9,15},{10,... | collective-permute-start | bytes 294920 | tf_op jit(solution)/shard_map/ppermute | solution.py:481
  41.9 5.8 %collective-permute-start.12 = (f32[6,32,128]{2,1,0:T(8,128)S(1)}, f32[6,32,128]{2,1,0:T(8,128)S(1)}, u32[]{:S(2)}, u32[]{:S(2)}) collective-permute-start(f32[6,32,128]{2,1,0:T(8,128)S(1)} %get-tuple-element.78), channel_id=1, source_target_pairs={{0,2},{1,3},{2,4},{3,5},{4,6},{5,7},{6,0},{7,1},{8,10},{9,11},{10,... | collective-permute-start | bytes 294920 | tf_op jit(solution)/shard_map/ppermute | solution.py:481
  42.4 5.4 %collective-permute-start.13 = (f32[6,32,128]{2,1,0:T(8,128)S(1)}, f32[6,32,128]{2,1,0:T(8,128)S(1)}, u32[]{:S(2)}, u32[]{:S(2)}) collective-permute-start(f32[6,32,128]{2,1,0:T(8,128)S(1)} %get-tuple-element.79), channel_id=1, source_target_pairs={{0,7},{1,6},{2,1},{3,0},{4,3},{5,2},{6,5},{7,4},{8,15},{9,14},{10,... | collective-permute-start | bytes 294920 | tf_op jit(solution)/shard_map/ppermute | solution.py:481
  44.8 5.6 %collective-permute-start.14 = (f32[6,32,128]{2,1,0:T(8,128)S(1)}, f32[6,32,128]{2,1,0:T(8,128)S(1)}, u32[]{:S(2)}, u32[]{:S(2)}) collective-permute-start(f32[6,32,128]{2,1,0:T(8,128)S(1)} %get-tuple-element.80), channel_id=1, source_target_pairs={{0,3},{1,2},{2,5},{3,4},{4,7},{5,6},{6,1},{7,0},{8,11},{9,10},{10,... | collective-permute-start | bytes 294920 | tf_op jit(solution)/shard_map/ppermute | solution.py:481

commit v2 on v1

--- a/solution.py
+++ b/solution.py
@@ -226,12 +226,10 @@
     place_ref, history, adjacency, far_one, far_two, onehots, weights, ends, end_parts, rim, rim_parts, t2m, parts3m,
     *rest,
 ):
-    outs = rest[:8]
-    low, high, left, right, left2, right2, edge, tips, t2, parts3, gat_a, gat_b = rest[8:]
+    outs = rest[:2]
+    t2, parts3, low, high, left, right, left2, right2, edge, tips, gat_a, gat_b = rest[2:]
     origin = place_ref[0]
-    x = place_ref[1]
     odd = place_ref[3] == 1
-    upper = place_ref[2] == 1
     low[...] = jnp.where(odd, far_two[...], far_one[...])
     high[...] = jnp.where(odd, far_one[...], far_two[...])
     low_adj = low[ROWS:, :].astype(jnp.int32)[0:NFACE]
@@ -266,19 +264,28 @@
     close, beyond = rim[:, cols(1)], tips[:, cols(1)]
     values = apply_block(close, beyond, right2, 0, edge, 3, rels[3], straddle(close, beyond), gat_b, weights)
     finish(values, ends[:, cols(1)], 0.5, t2, parts3, cols(4))
-    for dx, gathered in ((2, gat_a), (1, gat_b), (3, gat_a), (0, gat_b)):
-        b = (x + dx) & 3
-        col = pl.multiple_of(b * LANE, LANE)
-        rel = place(adjacency[:, pl.ds(col, LANE)], origin + 128 + col)
-        close, beyond = t2[:, pl.ds(col, LANE)], t2[:, pl.ds(col + LANE, LANE)]
-        values = apply_block(
-            close, beyond, parts3, col, onehots, b, rel, straddle(close, beyond), gathered, weights
-        )
-        for v in range(NV):
-            result = history[v * NP : (v + 1) * NP, pl.ds(col, LANE)] + values[v]
-            below, above = result[0:32], result[32:64]
-            outs[SLOTS.index((dx, 0))][v] = jnp.where(upper, above, below)
-            outs[SLOTS.index((dx, 1))][v] = jnp.where(upper, below, above)
+    last_block(place_ref, 2, history, adjacency, weights, onehots, t2, parts3, gat_a, outs)
+
+
+def last_block(place_ref, dx, history, adjacency, weights, onehots, t2, parts3, gathered, outs):
+    b = (place_ref[1] + dx) & 3
+    upper = place_ref[2] == 1
+    col = pl.multiple_of(b * LANE, LANE)
+    rel = place(adjacency[:, pl.ds(col, LANE)], place_ref[0] + 128 + col)
+    close, beyond = t2[:, pl.ds(col, LANE)], t2[:, pl.ds(col + LANE, LANE)]
+    values = apply_block(close, beyond, parts3, col, onehots, b, rel, straddle(close, beyond), gathered, weights)
+    for v in range(NV):
+        result = history[v * NP : (v + 1) * NP, pl.ds(col, LANE)] + values[v]
+        below, above = result[0:32], result[32:64]
+        outs[0][v] = jnp.where(upper, above, below)
+        outs[1][v] = jnp.where(upper, below, above)
+
+
+def last_kernel(dx):
+    def kernel(place_ref, history, adjacency, weights, onehots, t2, parts3, kept, crossed, gathered):
+        last_block(place_ref, dx, history, adjacency, weights, onehots, t2, parts3, gathered, (kept, crossed))
+
+    return kernel
 
 
 def source_of(x, core, slot):
@@ -464,15 +471,21 @@
         [pair(2), pair(2), wide(4), pair(4), buffer, buffer],
     )
     piece = ((NV, 32, LANE), F32)
-    advected = call(
+    *ahead, t2, parts3 = call(
         edge_kernel,
         (local, faces, far_one, far_two, onehots, weights, *middle),
-        [piece] * 8,
+        [piece, piece, wide(5), pair(5)],
         [
             far, far, pair(2), pair(2), pair(2), pair(2), ((4, 256, MATMUL_FACES * LANE), BF16),
-            wide(2), wide(5), pair(5), buffer, buffer,
+            wide(2), buffer, buffer,
         ],
     )
+    ready = {(2, 0): ahead[0], (2, 1): ahead[1]}
+    for dx in (1, 3, 0):
+        ready[dx, 0], ready[dx, 1] = call(
+            last_kernel(dx), (local, faces, weights, onehots, t2, parts3), [piece, piece], [buffer]
+        )
+    advected = [ready[slot] for slot in SLOTS]
 
     def exchange(piece, dx, dc):
         if dx == 0 and dc == 0:

time: 52.2 us -> 54.3 us (1.040)
  the two profiles are of different devices: /device:TPU:120 before, /device:TPU:121 now
where the time goes in v2:
time: 54.3 us; the launch traced here: 54.2 us
  starting transfers between devices  21.1 us (39%)
  waiting for transfers between devices  17.1 us (31%)
  Pallas kernels  15.6 us (29%)
    ppermute x14, starting transfers between devices, exchange(): return lax.ppermute(piece, 'var', pairs)  16 us
    pallas_call x11, Pallas kernels, call(): pl.pallas_call(placed, out_shape=tuple((jax.ShapeDtypeStruct(shape, dtype...  15.6 us
    ppermute x14, waiting for transfers between devices, exchange(): return lax.ppermute(piece, 'var', pairs)  13.3 us
    ppermute x1, waiting for transfers between devices, per_device(): near_one = lax.ppermute(near_one, axes, one)  3.8 us
    ppermute x1, starting transfers between devices, per_device(): far_one = lax.ppermute(far_one, axes, one)  2.59 us
    ppermute x1, starting transfers between devices, per_device(): near_one = lax.ppermute(near_one, axes, one)  2.59 us
  transfers between devices with their start and end apart: 18, of which 6 were waited for; matrix products, arithmetic and copies ran while one was open for 0% of the time, Pallas kernels for 16%

profile of v2, /device:TPU:121, one launch (start us, length us, event | category | flops | bytes accessed | tf_op | source)
XLA Modules:
  0.0 54.2 jit_solution(1328966381467713741)
XLA Ops:
  0.0 1.7 %shard_map.65 = (f32[192,128]{1,0:T(8,128)S(1)}, f32[192,128]{1,0:T(8,128)S(1)}, f32[392,128]{1,0:T(8,128)S(1)}, f32[392,128]{1,0:T(8,128)S(1)}, f32[384,512]{1,...) custom-call(f32[384,512]{1,0:T(8,128)} %bitcast.3, s32[6,512]{1,0:T(8,128)} %refs_1_.3, ...), custom_call_target="tpu_custom_call" | custom-call | tf_op jit(solution)/shard_map/pallas_call | solution.py:411
  1.7 2.6 %collective-permute-start = (f32[392,128]{1,0:T(8,128)S(1)}, f32[392,128]{1,0:T(8,128)S(1)}, u32[]{:S(2)}, u32[]{:S(2)}) collective-permute-start(f32[392,128]{1,0:T(8,128)S(1)} %get-tuple-element.55), channel_id=1, source_target_pairs={{0,1},{1,0},{2,3},{3,2},{4,5},{5,4},{6,7},{7,6},{8,16},{9,17},{10,... | collective-permute-start | bytes 602120 | tf_op jit(solution)/shard_map/ppermute | solution.py:452
  4.3 0.0 collective-permute-start.1
  4.3 2.6 %collective-permute-start.2 = (f32[192,128]{1,0:T(8,128)S(1)}, f32[192,128]{1,0:T(8,128)S(1)}, u32[]{:S(2)}, u32[]{:S(2)}) collective-permute-start(f32[192,128]{1,0:T(8,128)S(1)} %get-tuple-element.57), channel_id=1, source_target_pairs={{0,1},{1,0},{2,3},{3,2},{4,5},{5,4},{6,7},{7,6},{8,16},{9,17},{10,... | collective-permute-start | bytes 294920 | tf_op jit(solution)/shard_map/ppermute | solution.py:450
  6.9 0.0 collective-permute-start.3
  6.9 2.4 %shard_map.66 = (f32[384,640]{1,0:T(8,128)S(1)}, bf16[768,384]{1,0:T(8,128)(2,1)S(1)}, bf16[7,256,512]{2,1,0:T(8,128)(2,1)S(1)}, f32[384,256]{1,0:T(8,128)S(1)},...) custom-call(f32[384,512]{1,0:T(8,128)S(1)} %get-tuple-element.49.ref, ...), custom_call_target="tpu_custom_call" | custom-call | tf_op jit(solution)/shard_map/pallas_call | solution.py:411
  9.3 3.8 %collective-permute-done.2.refs_2_ = f32[192,128]{1,0:T(8,128)S(1)} collective-permute-done((f32[192,128]{1,0:T(8,128)S(1)}, f32[192,128]{1,0:T(8,128)S(1)}, u32[]{:S(2)}, u32[]{:S(2)}) %collective-permute-start.2) | collective-permute-done | bytes 98336 | tf_op jit(solution)/shard_map/ppermute | solution.py:450
  13.1 2.4 %shard_map.67 = (f32[384,256]{1,0:T(8,128)S(1)}, bf16[768,256]{1,0:T(8,128)(2,1)S(1)}, f32[384,256]{1,0:T(8,128)S(1)}, bf16[768,256]{1,0:T(8,128)(2,1)S(1)}, f32...) custom-call(f32[384,512]{1,0:T(8,128)S(1)} %get-tuple-element.49.refs_0_, s32[6,512]{1,0:T(8,128)S(1)} %get-tuple-element.50.refs_1_, ...), custom_call_target="tpu_custom_call" | custom-call | tf_op jit(solution)/shard_map/pallas_call | solution.py:411
  15.6 3.2 %shard_map.68 = (f32[6,32,128]{2,1,0:T(8,128)S(1)}, f32[6,32,128]{2,1,0:T(8,128)S(1)}, f32[384,640]{1,0:T(8,128)S(1)}, bf16[768,640]{1,0:T(8,128)(2,1)S(1)}) custom-call(f32[384,512]{1,0:T(8,128)S(1)} %get-tuple-element.49.refs_0_, s32[6,512]{1,0:T(8,128)S(1)} %get-tuple-element.50.refs_1_, f32[392,128]{1,0:T(8,128)S(1)} %collective-permute-done.refs_2_, ...), custom_call_target="tpu_custom_call" | custom-call | tf_op jit(solution)/shard_map/pallas_call | solution.py:411
  18.8 0.7 %shard_map.71 = (f32[6,32,128]{2,1,0:T(8,128)S(1)}, f32[6,32,128]{2,1,0:T(8,128)S(1)}) custom-call(f32[384,512]{1,0:T(8,128)S(1)} %get-tuple-element.49.refs_0_, s32[6,512]{1,0:T(8,128)S(1)} %get-tuple-element.50.refs_1_, bf16[128,448]{1,0:T(8,128)(2,1)S(1)} %get-tuple-element.53.refs_11_.refs_5_.refs_2_, ...), custom_call_target="tpu_custom_call" | custom-call | tf_op jit(solution)/shard_map/pallas_call | solution.py:411
  19.5 2.6 %collective-permute-start.7 = (f32[6,32,128]{2,1,0:T(8,128)S(1)}, f32[6,32,128]{2,1,0:T(8,128)S(1)}, u32[]{:S(2)}, u32[]{:S(2)}) collective-permute-start(f32[6,32,128]{2,1,0:T(8,128)S(1)} %get-tuple-element.77), channel_id=1, source_target_pairs={{0,6},{1,7},{2,0},{3,1},{4,2},{5,3},{6,4},{7,5},{8,14},{9,15},{10,... | collective-permute-start | bytes 294920 | tf_op jit(solution)/shard_map/ppermute | solution.py:494
  22.1 2.2 %collective-permute-start.9 = (f32[6,32,128]{2,1,0:T(8,128)S(1)}, f32[6,32,128]{2,1,0:T(8,128)S(1)}, u32[]{:S(2)}, u32[]{:S(2)}) collective-permute-start(f32[6,32,128]{2,1,0:T(8,128)S(1)} %get-tuple-element.79), channel_id=1, source_target_pairs={{0,7},{1,6},{2,1},{3,0},{4,3},{5,2},{6,5},{7,4},{8,15},{9,14},{10,... | collective-permute-start | bytes 294920 | tf_op jit(solution)/shard_map/ppermute | solution.py:494
  24.3 0.7 %shard_map.70 = (f32[6,32,128]{2,1,0:T(8,128)S(1)}, f32[6,32,128]{2,1,0:T(8,128)S(1)}) custom-call(f32[384,512]{1,0:T(8,128)S(1)} %get-tuple-element.49.refs_0_, s32[6,512]{1,0:T(8,128)S(1)} %get-tuple-element.50.refs_1_, bf16[128,448]{1,0:T(8,128)(2,1)S(1)} %get-tuple-element.53.refs_11_.refs_5_.refs_2_, ...), custom_call_target="tpu_custom_call" | custom-call | tf_op jit(solution)/shard_map/pallas_call | solution.py:411
  25.0 0.7 %shard_map.69 = (f32[6,32,128]{2,1,0:T(8,128)S(1)}, f32[6,32,128]{2,1,0:T(8,128)S(1)}) custom-call(f32[384,512]{1,0:T(8,128)S(1)} %get-tuple-element.49.refs_0_, s32[6,512]{1,0:T(8,128)S(1)} %get-tuple-element.50.refs_1_, bf16[128,448]{1,0:T(8,128)(2,1)S(1)} %get-tuple-element.53.refs_11_.refs_5_.refs_2_, ...), custom_call_target="tpu_custom_call" | custom-call | tf_op jit(solution)/shard_map/pallas_call | solution.py:411
  25.7 1.0 %collective-permute-start.6 = (f32[6,32,128]{2,1,0:T(8,128)S(1)}, f32[6,32,128]{2,1,0:T(8,128)S(1)}, u32[]{:S(2)}, u32[]{:S(2)}) collective-permute-start(f32[6,32,128]{2,1,0:T(8,128)S(1)} %get-tuple-element.76), channel_id=1, source_target_pairs={{0,2},{1,3},{2,4},{3,5},{4,6},{5,7},{6,0},{7,1},{8,10},{9,11},{10,... | collective-permute-start | bytes 294920 | tf_op jit(solution)/shard_map/ppermute | solution.py:494
  26.7 0.5 collective-permute-start.10
  27.2 2.9 %collective-permute-start.4 = (f32[6,32,128]{2,1,0:T(8,128)S(1)}, f32[6,32,128]{2,1,0:T(8,128)S(1)}, u32[]{:S(2)}, u32[]{:S(2)}) collective-permute-start(f32[6,32,128]{2,1,0:T(8,128)S(1)} %get-tuple-element.74), channel_id=1, source_target_pairs={{0,4},{1,5},{2,6},{3,7},{4,0},{5,1},{6,2},{7,3},{8,12},{9,13},{10,... | collective-permute-start | bytes 294920 | tf_op jit(solution)/shard_map/ppermute | solution.py:494
  30.1 0.3 collective-permute-start.5
  30.4 1.4 %shard_map.64 = (bf16[192,384]{1,0:T(8,128)(2,1)S(1)}, bf16[384,288]{1,0:T(8,128)(2,1)S(1)}) custom-call(f32[12,48]{1,0:T(8,128)} %bitcast.5, f32[12,48]{1,0:T(8,128)} %refs_1_.2), custom_call_target="tpu_custom_call" | custom-call | tf_op jit(solution)/shard_map/pallas_call | solution.py:411
  31.8 0.0 collective-permute-done.6.refs_5_
  31.8 6.3 %collective-permute-done.8.refs_7_ = f32[6,32,128]{2,1,0:T(8,128)S(1)} collective-permute-done((f32[6,32,128]{2,1,0:T(8,128)S(1)}, f32[6,32,128]{2,1,0:T(8,128)S(1)}, u32[]{:S(2)}, u32[]{:S(2)}) %collective-permute-start.8) | collective-permute-done | bytes 98336 | tf_op jit(solution)/shard_map/ppermute | solution.py:494
  38.1 0.8 %shard_map.72 = (f32[6,32,128]{2,1,0:T(8,128)S(1)}, f32[6,32,128]{2,1,0:T(8,128)S(1)}, f32[6,32,128]{2,1,0:T(8,128)S(1)}, f32[6,32,128]{2,1,0:T(8,128)S(1)}, f32...) custom-call(bf16[192,384]{1,0:T(8,128)(2,1)S(1)} %get-tuple-element.4, ...), custom_call_target="tpu_custom_call" | custom-call | tf_op jit(solution)/shard_map/pallas_call | solution.py:411
  38.9 0.2 collective-permute-start.15
  39.1 3.5 %collective-permute-start.16 = (f32[6,32,128]{2,1,0:T(8,128)S(1)}, f32[6,32,128]{2,1,0:T(8,128)S(1)}, u32[]{:S(2)}, u32[]{:S(2)}) collective-permute-start(f32[6,32,128]{2,1,0:T(8,128)S(1)} %get-tuple-element.87), channel_id=1, source_target_pairs={{0,5},{1,4},{2,7},{3,6},{4,1},{5,0},{6,3},{7,2},{8,13},{9,12},{10,... | collective-permute-start | bytes 294920 | tf_op jit(solution)/shard_map/ppermute | solution.py:494
  42.6 1.5 %collective-permute-start.12 = (f32[6,32,128]{2,1,0:T(8,128)S(1)}, f32[6,32,128]{2,1,0:T(8,128)S(1)}, u32[]{:S(2)}, u32[]{:S(2)}) collective-permute-start(f32[6,32,128]{2,1,0:T(8,128)S(1)} %get-tuple-element.82), channel_id=1, source_target_pairs={{0,2},{1,3},{2,4},{3,5},{4,6},{5,7},{6,0},{7,1},{8,10},{9,11},{10,... | collective-permute-start | bytes 294920 | tf_op jit(solution)/shard_map/ppermute | solution.py:494
  44.0 0.5 collective-permute-done.15.refs_1_
  44.5 1.4 %collective-permute-start.13 = (f32[6,32,128]{2,1,0:T(8,128)S(1)}, f32[6,32,128]{2,1,0:T(8,128)S(1)}, u32[]{:S(2)}, u32[]{:S(2)}) collective-permute-start(f32[6,32,128]{2,1,0:T(8,128)S(1)} %get-tuple-element.83), channel_id=1, source_target_pairs={{0,7},{1,6},{2,1},{3,0},{4,3},{5,2},{6,5},{7,4},{8,15},{9,14},{10,... | collective-permute-start | bytes 294920 | tf_op jit(solution)/shard_map/ppermute | solution.py:494
  45.9 2.1 %collective-permute-done.16.refs_2_ = f32[6,32,128]{2,1,0:T(8,128)S(1)} collective-permute-done((f32[6,32,128]{2,1,0:T(8,128)S(1)}, f32[6,32,128]{2,1,0:T(8,128)S(1)}, u32[]{:S(2)}, u32[]{:S(2)}) %collective-permute-start.16) | collective-permute-done | bytes 98336 | tf_op jit(solution)/shard_map/ppermute | solution.py:494
  48.0 0.8 %shard_map.73.refs_4_ = f32[6,64,512]{2,1,0:T(8,128)} custom-call(f32[6,32,128]{2,1,0:T(8,128)S(1)} %get-tuple-element.85.refs_0_, f32[6,32,128]{2,1,0:T(8,128)S(1)} %collective-permute-done.15.refs_1_, f32[6,32,128]{2,1,0:T(8,128)S(1)} %collective-permute-done.16.refs_2_, f32[6,32,128]{2,1,0:T(8,128)S(1)} %collective-permute-done.17.refs_3_), custom_call_target="tpu_custom_call" | custom-call | tf_op jit(solution)/shard_map/pallas_call | solution.py:411
  48.8 0.3 collective-permute-done.12.refs_1_
  49.1 4.1 %collective-permute-done.14.refs_3_ = f32[6,32,128]{2,1,0:T(8,128)S(1)} collective-permute-done((f32[6,32,128]{2,1,0:T(8,128)S(1)}, f32[6,32,128]{2,1,0:T(8,128)S(1)}, u32[]{:S(2)}, u32[]{:S(2)}) %collective-permute-start.14) | collective-permute-done | bytes 98336 | tf_op jit(solution)/shard_map/ppermute | solution.py:494
  53.3 0.8 %shard_map.74 = f32[6,64,512]{2,1,0:T(8,128)} custom-call(f32[6,32,128]{2,1,0:T(8,128)S(1)} %collective-permute-done.11.refs_0_, f32[6,32,128]{2,1,0:T(8,128)S(1)} %collective-permute-done.12.refs_1_, f32[6,32,128]{2,1,0:T(8,128)S(1)} %collective-permute-done.13.refs_2_, ...), custom_call_target="tpu_custom_call", output_to_operand_aliasing={{}: (4, {})} | custom-call | tf_op jit(solution)/shard_map/pallas_call | solution.py:411
  (15 shorter events, 0.0 us)
Async XLA Ops:
  1.7 13.8 %collective-permute-start = (f32[392,128]{1,0:T(8,128)S(1)}, f32[392,128]{1,0:T(8,128)S(1)}, u32[]{:S(2)}, u32[]{:S(2)}) collective-permute-start(f32[392,128]{1,0:T(8,128)S(1)} %get-tuple-element.55), channel_id=1, source_target_pairs={{0,1},{1,0},{2,3},{3,2},{4,5},{5,4},{6,7},{7,6},{8,16},{9,17},{10,... | collective-permute-start | bytes 602120 | tf_op jit(solution)/shard_map/ppermute | solution.py:452
  4.3 11.3 %collective-permute-start.1 = (f32[392,128]{1,0:T(8,128)S(1)}, f32[392,128]{1,0:T(8,128)S(1)}, u32[]{:S(2)}, u32[]{:S(2)}) collective-permute-start(f32[392,128]{1,0:T(8,128)S(1)} %get-tuple-element.56), channel_id=1, source_target_pairs={{0,8},{1,9},{2,10},{3,11},{4,12},{5,13},{6,14},{7,15},{8,0},{9,1},... | collective-permute-start | bytes 602120 | tf_op jit(solution)/shard_map/ppermute | solution.py:453
  4.3 8.8 %collective-permute-start.2 = (f32[192,128]{1,0:T(8,128)S(1)}, f32[192,128]{1,0:T(8,128)S(1)}, u32[]{:S(2)}, u32[]{:S(2)}) collective-permute-start(f32[192,128]{1,0:T(8,128)S(1)} %get-tuple-element.57), channel_id=1, source_target_pairs={{0,1},{1,0},{2,3},{3,2},{4,5},{5,4},{6,7},{7,6},{8,16},{9,17},{10,... | collective-permute-start | bytes 294920 | tf_op jit(solution)/shard_map/ppermute | solution.py:450
  6.9 6.2 %collective-permute-start.3 = (f32[192,128]{1,0:T(8,128)S(1)}, f32[192,128]{1,0:T(8,128)S(1)}, u32[]{:S(2)}, u32[]{:S(2)}) collective-permute-start(f32[192,128]{1,0:T(8,128)S(1)} %get-tuple-element.58), channel_id=1, source_target_pairs={{0,8},{1,9},{2,10},{3,11},{4,12},{5,13},{6,14},{7,15},{8,0},{9,1},... | collective-permute-start | bytes 294920 | tf_op jit(solution)/shard_map/ppermute | solution.py:451
  19.5 7.7 %collective-permute-start.7 = (f32[6,32,128]{2,1,0:T(8,128)S(1)}, f32[6,32,128]{2,1,0:T(8,128)S(1)}, u32[]{:S(2)}, u32[]{:S(2)}) collective-permute-start(f32[6,32,128]{2,1,0:T(8,128)S(1)} %get-tuple-element.77), channel_id=1, source_target_pairs={{0,6},{1,7},{2,0},{3,1},{4,2},{5,3},{6,4},{7,5},{8,14},{9,15},{10,... | collective-permute-start | bytes 294920 | tf_op jit(solution)/shard_map/ppermute | solution.py:494
  22.1 8.0 %collective-permute-start.9 = (f32[6,32,128]{2,1,0:T(8,128)S(1)}, f32[6,32,128]{2,1,0:T(8,128)S(1)}, u32[]{:S(2)}, u32[]{:S(2)}) collective-permute-start(f32[6,32,128]{2,1,0:T(8,128)S(1)} %get-tuple-element.79), channel_id=1, source_target_pairs={{0,7},{1,6},{2,1},{3,0},{4,3},{5,2},{6,5},{7,4},{8,15},{9,14},{10,... | collective-permute-start | bytes 294920 | tf_op jit(solution)/shard_map/ppermute | solution.py:494
  25.7 6.1 %collective-permute-start.6 = (f32[6,32,128]{2,1,0:T(8,128)S(1)}, f32[6,32,128]{2,1,0:T(8,128)S(1)}, u32[]{:S(2)}, u32[]{:S(2)}) collective-permute-start(f32[6,32,128]{2,1,0:T(8,128)S(1)} %get-tuple-element.76), channel_id=1, source_target_pairs={{0,2},{1,3},{2,4},{3,5},{4,6},{5,7},{6,0},{7,1},{8,10},{9,11},{10,... | collective-permute-start | bytes 294920 | tf_op jit(solution)/shard_map/ppermute | solution.py:494
  26.7 11.4 %collective-permute-start.8 = (f32[6,32,128]{2,1,0:T(8,128)S(1)}, f32[6,32,128]{2,1,0:T(8,128)S(1)}, u32[]{:S(2)}, u32[]{:S(2)}) collective-permute-start(f32[6,32,128]{2,1,0:T(8,128)S(1)} %get-tuple-element.78), channel_id=1, source_target_pairs={{0,3},{1,2},{2,5},{3,4},{4,7},{5,6},{6,1},{7,0},{8,11},{9,10},{10,... | collective-permute-start | bytes 294920 | tf_op jit(solution)/shard_map/ppermute | solution.py:494
  26.7 11.4 %collective-permute-start.10 = (f32[6,32,128]{2,1,0:T(8,128)S(1)}, f32[6,32,128]{2,1,0:T(8,128)S(1)}, u32[]{:S(2)}, u32[]{:S(2)}) collective-permute-start(f32[6,32,128]{2,1,0:T(8,128)S(1)} %get-tuple-element.80), channel_id=1, source_target_pairs={{0,1},{1,0},{2,3},{3,2},{4,5},{5,4},{6,7},{7,6},{8,9},{9,8},{10,11... | collective-permute-start | bytes 294920 | tf_op jit(solution)/shard_map/ppermute | solution.py:494
  27.2 10.9 %collective-permute-start.4 = (f32[6,32,128]{2,1,0:T(8,128)S(1)}, f32[6,32,128]{2,1,0:T(8,128)S(1)}, u32[]{:S(2)}, u32[]{:S(2)}) collective-permute-start(f32[6,32,128]{2,1,0:T(8,128)S(1)} %get-tuple-element.74), channel_id=1, source_target_pairs={{0,4},{1,5},{2,6},{3,7},{4,0},{5,1},{6,2},{7,3},{8,12},{9,13},{10,... | collective-permute-start | bytes 294920 | tf_op jit(solution)/shard_map/ppermute | solution.py:494
  30.1 8.1 %collective-permute-start.5 = (f32[6,32,128]{2,1,0:T(8,128)S(1)}, f32[6,32,128]{2,1,0:T(8,128)S(1)}, u32[]{:S(2)}, u32[]{:S(2)}) collective-permute-start(f32[6,32,128]{2,1,0:T(8,128)S(1)} %get-tuple-element.75), channel_id=1, source_target_pairs={{0,5},{1,4},{2,7},{3,6},{4,1},{5,0},{6,3},{7,2},{8,13},{9,12},{10,... | collective-permute-start | bytes 294920 | tf_op jit(solution)/shard_map/ppermute | solution.py:494
  38.9 5.5 %collective-permute-start.15 = (f32[6,32,128]{2,1,0:T(8,128)S(1)}, f32[6,32,128]{2,1,0:T(8,128)S(1)}, u32[]{:S(2)}, u32[]{:S(2)}) collective-permute-start(f32[6,32,128]{2,1,0:T(8,128)S(1)} %get-tuple-element.86), channel_id=1, source_target_pairs={{0,4},{1,5},{2,6},{3,7},{4,0},{5,1},{6,2},{7,3},{8,12},{9,13},{10,... | collective-permute-start | bytes 294920 | tf_op jit(solution)/shard_map/ppermute | solution.py:494
  39.1 8.9 %collective-permute-start.16 = (f32[6,32,128]{2,1,0:T(8,128)S(1)}, f32[6,32,128]{2,1,0:T(8,128)S(1)}, u32[]{:S(2)}, u32[]{:S(2)}) collective-permute-start(f32[6,32,128]{2,1,0:T(8,128)S(1)} %get-tuple-element.87), channel_id=1, source_target_pairs={{0,5},{1,4},{2,7},{3,6},{4,1},{5,0},{6,3},{7,2},{8,13},{9,12},{10,... | collective-permute-start | bytes 294920 | tf_op jit(solution)/shard_map/ppermute | solution.py:494
  42.6 5.5 %collective-permute-start.17 = (f32[6,32,128]{2,1,0:T(8,128)S(1)}, f32[6,32,128]{2,1,0:T(8,128)S(1)}, u32[]{:S(2)}, u32[]{:S(2)}) collective-permute-start(f32[6,32,128]{2,1,0:T(8,128)S(1)} %get-tuple-element.88), channel_id=1, source_target_pairs={{0,1},{1,0},{2,3},{3,2},{4,5},{5,4},{6,7},{7,6},{8,9},{9,8},{10,11... | collective-permute-start | bytes 294920 | tf_op jit(solution)/shard_map/ppermute | solution.py:494
  42.6 6.2 %collective-permute-start.11 = (f32[6,32,128]{2,1,0:T(8,128)S(1)}, f32[6,32,128]{2,1,0:T(8,128)S(1)}, u32[]{:S(2)}, u32[]{:S(2)}) collective-permute-start(f32[6,32,128]{2,1,0:T(8,128)S(1)} %get-tuple-element.81), channel_id=1, source_target_pairs={{0,6},{1,7},{2,0},{3,1},{4,2},{5,3},{6,4},{7,5},{8,14},{9,15},{10,... | collective-permute-start | bytes 294920 | tf_op jit(solution)/shard_map/ppermute | solution.py:494
  42.6 6.6 %collective-permute-start.12 = (f32[6,32,128]{2,1,0:T(8,128)S(1)}, f32[6,32,128]{2,1,0:T(8,128)S(1)}, u32[]{:S(2)}, u32[]{:S(2)}) collective-permute-start(f32[6,32,128]{2,1,0:T(8,128)S(1)} %get-tuple-element.82), channel_id=1, source_target_pairs={{0,2},{1,3},{2,4},{3,5},{4,6},{5,7},{6,0},{7,1},{8,10},{9,11},{10,... | collective-permute-start | bytes 294920 | tf_op jit(solution)/shard_map/ppermute | solution.py:494
  44.5 4.6 %collective-permute-start.13 = (f32[6,32,128]{2,1,0:T(8,128)S(1)}, f32[6,32,128]{2,1,0:T(8,128)S(1)}, u32[]{:S(2)}, u32[]{:S(2)}) collective-permute-start(f32[6,32,128]{2,1,0:T(8,128)S(1)} %get-tuple-element.83), channel_id=1, source_target_pairs={{0,7},{1,6},{2,1},{3,0},{4,3},{5,2},{6,5},{7,4},{8,15},{9,14},{10,... | collective-permute-start | bytes 294920 | tf_op jit(solution)/shard_map/ppermute | solution.py:494
  48.0 5.3 %collective-permute-start.14 = (f32[6,32,128]{2,1,0:T(8,128)S(1)}, f32[6,32,128]{2,1,0:T(8,128)S(1)}, u32[]{:S(2)}, u32[]{:S(2)}) collective-permute-start(f32[6,32,128]{2,1,0:T(8,128)S(1)} %get-tuple-element.84), channel_id=1, source_target_pairs={{0,3},{1,2},{2,5},{3,4},{4,7},{5,6},{6,1},{7,0},{8,11},{9,10},{10,... | collective-permute-start | bytes 294920 | tf_op jit(solution)/shard_map/ppermute | solution.py:494

commit v3 on v2

--- a/solution.py
+++ b/solution.py
@@ -64,7 +64,7 @@
     half = ROWS // 2
     first = first_half(half)
     copies = fetch(
-        [(history_hbm.at[:, cols(c)], history.at[:, cols(c)]) for c in (0, 3, 1, 2)]
+        [(history_hbm.at[r : r + 96, :], history.at[r : r + 96, :]) for r in range(0, ROWS, 96)]
         + [(adjacency_hbm, adjacency), (volume_hbm, volume_op), (face_hbm, face_lift)],
         sems,
     )
@@ -281,9 +281,14 @@
         outs[1][v] = jnp.where(upper, below, above)
 
 
-def last_kernel(dx):
-    def kernel(place_ref, history, adjacency, weights, onehots, t2, parts3, kept, crossed, gathered):
-        last_block(place_ref, dx, history, adjacency, weights, onehots, t2, parts3, gathered, (kept, crossed))
+def last_kernel(steps):
+    def kernel(place_ref, history, adjacency, weights, onehots, t2, parts3, *rest):
+        outs = rest[: 2 * len(steps)]
+        buffers = rest[2 * len(steps) :]
+        for i, dx in enumerate(steps):
+            last_block(
+                place_ref, dx, history, adjacency, weights, onehots, t2, parts3, buffers[i], outs[2 * i : 2 * i + 2]
+            )
 
     return kernel
 
@@ -481,10 +486,15 @@
         ],
     )
     ready = {(2, 0): ahead[0], (2, 1): ahead[1]}
-    for dx in (1, 3, 0):
-        ready[dx, 0], ready[dx, 1] = call(
-            last_kernel(dx), (local, faces, weights, onehots, t2, parts3), [piece, piece], [buffer]
+    for steps in ((1, 3), (0,)):
+        pieces = call(
+            last_kernel(steps),
+            (local, faces, weights, onehots, t2, parts3),
+            [piece, piece] * len(steps),
+            [buffer] * len(steps),
         )
+        for i, dx in enumerate(steps):
+            ready[dx, 0], ready[dx, 1] = pieces[2 * i : 2 * i + 2]
     advected = [ready[slot] for slot in SLOTS]
 
     def exchange(piece, dx, dc):

time: 54.3 us -> 52.6 us (0.969)
  the two profiles are of different devices: /device:TPU:121 before, /device:TPU:129 now
where the time goes in v3:
time: 52.6 us; the launch traced here: 52.5 us
  starting transfers between devices  22.6 us (43%)
  Pallas kernels  15.3 us (29%)
  waiting for transfers between devices  14.2 us (27%)
    ppermute x14, starting transfers between devices, exchange(): return lax.ppermute(piece, 'var', pairs)  17.7 us
    pallas_call x10, Pallas kernels, call(): pl.pallas_call(placed, out_shape=tuple((jax.ShapeDtypeStruct(shape, dtype...  15.3 us
    ppermute x14, waiting for transfers between devices, exchange(): return lax.ppermute(piece, 'var', pairs)  10.1 us
    ppermute x1, waiting for transfers between devices, per_device(): near_one = lax.ppermute(near_one, axes, one)  4.11 us
    ppermute x1, starting transfers between devices, per_device(): far_one = lax.ppermute(far_one, axes, one)  2.37 us
    ppermute x1, starting transfers between devices, per_device(): near_one = lax.ppermute(near_one, axes, one)  2.2 us
  transfers between devices with their start and end apart: 18, of which 7 were waited for; matrix products, arithmetic and copies ran while one was open for 0% of the time, Pallas kernels for 15%

profile of v3, /device:TPU:129, one launch (start us, length us, event | category | flops | bytes accessed | tf_op | source)
XLA Modules:
  0.0 52.5 jit_solution(17971468683804563406)
XLA Ops:
  0.0 1.7 %shard_map.65 = (f32[192,128]{1,0:T(8,128)S(1)}, f32[192,128]{1,0:T(8,128)S(1)}, f32[392,128]{1,0:T(8,128)S(1)}, f32[392,128]{1,0:T(8,128)S(1)}, f32[384,512]{1,...) custom-call(f32[384,512]{1,0:T(8,128)} %bitcast.3, s32[6,512]{1,0:T(8,128)} %refs_1_.3, ...), custom_call_target="tpu_custom_call" | custom-call | tf_op jit(solution)/shard_map/pallas_call | solution.py:416
  1.7 2.4 %collective-permute-start = (f32[392,128]{1,0:T(8,128)S(1)}, f32[392,128]{1,0:T(8,128)S(1)}, u32[]{:S(2)}, u32[]{:S(2)}) collective-permute-start(f32[392,128]{1,0:T(8,128)S(1)} %get-tuple-element.55), channel_id=1, source_target_pairs={{0,1},{1,0},{2,3},{3,2},{4,5},{5,4},{6,7},{7,6},{8,16},{9,17},{10,... | collective-permute-start | bytes 602120 | tf_op jit(solution)/shard_map/ppermute | solution.py:457
  4.1 0.3 collective-permute-start.1
  4.4 2.2 %collective-permute-start.2 = (f32[192,128]{1,0:T(8,128)S(1)}, f32[192,128]{1,0:T(8,128)S(1)}, u32[]{:S(2)}, u32[]{:S(2)}) collective-permute-start(f32[192,128]{1,0:T(8,128)S(1)} %get-tuple-element.57), channel_id=1, source_target_pairs={{0,1},{1,0},{2,3},{3,2},{4,5},{5,4},{6,7},{7,6},{8,16},{9,17},{10,... | collective-permute-start | bytes 294920 | tf_op jit(solution)/shard_map/ppermute | solution.py:455
  6.6 2.4 %shard_map.66 = (f32[384,640]{1,0:T(8,128)S(1)}, bf16[768,384]{1,0:T(8,128)(2,1)S(1)}, bf16[7,256,512]{2,1,0:T(8,128)(2,1)S(1)}, f32[384,256]{1,0:T(8,128)S(1)},...) custom-call(f32[384,512]{1,0:T(8,128)S(1)} %get-tuple-element.49.ref, ...), custom_call_target="tpu_custom_call" | custom-call | tf_op jit(solution)/shard_map/pallas_call | solution.py:416
  9.0 4.1 %collective-permute-done.2.refs_2_ = f32[192,128]{1,0:T(8,128)S(1)} collective-permute-done((f32[192,128]{1,0:T(8,128)S(1)}, f32[192,128]{1,0:T(8,128)S(1)}, u32[]{:S(2)}, u32[]{:S(2)}) %collective-permute-start.2) | collective-permute-done | bytes 98336 | tf_op jit(solution)/shard_map/ppermute | solution.py:455
  13.1 2.4 %shard_map.67 = (f32[384,256]{1,0:T(8,128)S(1)}, bf16[768,256]{1,0:T(8,128)(2,1)S(1)}, f32[384,256]{1,0:T(8,128)S(1)}, bf16[768,256]{1,0:T(8,128)(2,1)S(1)}, f32...) custom-call(f32[384,512]{1,0:T(8,128)S(1)} %get-tuple-element.49.refs_0_, s32[6,512]{1,0:T(8,128)S(1)} %get-tuple-element.50.refs_1_, ...), custom_call_target="tpu_custom_call" | custom-call | tf_op jit(solution)/shard_map/pallas_call | solution.py:416
  15.5 3.2 %shard_map.68 = (f32[6,32,128]{2,1,0:T(8,128)S(1)}, f32[6,32,128]{2,1,0:T(8,128)S(1)}, f32[384,640]{1,0:T(8,128)S(1)}, bf16[768,640]{1,0:T(8,128)(2,1)S(1)}) custom-call(f32[384,512]{1,0:T(8,128)S(1)} %get-tuple-element.49.refs_0_, s32[6,512]{1,0:T(8,128)S(1)} %get-tuple-element.50.refs_1_, f32[392,128]{1,0:T(8,128)S(1)} %collective-permute-done.refs_2_, ...), custom_call_target="tpu_custom_call" | custom-call | tf_op jit(solution)/shard_map/pallas_call | solution.py:416
  18.7 1.2 %shard_map.70 = (f32[6,32,128]{2,1,0:T(8,128)S(1)}, f32[6,32,128]{2,1,0:T(8,128)S(1)}, f32[6,32,128]{2,1,0:T(8,128)S(1)}, f32[6,32,128]{2,1,0:T(8,128)S(1)}) custom-call(f32[384,512]{1,0:T(8,128)S(1)} %get-tuple-element.49.refs_0_, s32[6,512]{1,0:T(8,128)S(1)} %get-tuple-element.50.refs_1_, bf16[128,448]{1,0:T(8,128)(2,1)S(1)} %get-tuple-element.53.refs_11_.refs_5_.refs_2_, ...), custom_call_target="tpu_custom_call" | custom-call | tf_op jit(solution)/shard_map/pallas_call | solution.py:416
  19.9 1.3 %collective-permute-start.6 = (f32[6,32,128]{2,1,0:T(8,128)S(1)}, f32[6,32,128]{2,1,0:T(8,128)S(1)}, u32[]{:S(2)}, u32[]{:S(2)}) collective-permute-start(f32[6,32,128]{2,1,0:T(8,128)S(1)} %get-tuple-element.76), channel_id=1, source_target_pairs={{0,2},{1,3},{2,4},{3,5},{4,6},{5,7},{6,0},{7,1},{8,10},{9,11},{10,... | collective-permute-start | bytes 294920 | tf_op jit(solution)/shard_map/ppermute | solution.py:504
  21.2 1.5 %collective-permute-start.7 = (f32[6,32,128]{2,1,0:T(8,128)S(1)}, f32[6,32,128]{2,1,0:T(8,128)S(1)}, u32[]{:S(2)}, u32[]{:S(2)}) collective-permute-start(f32[6,32,128]{2,1,0:T(8,128)S(1)} %get-tuple-element.77), channel_id=1, source_target_pairs={{0,6},{1,7},{2,0},{3,1},{4,2},{5,3},{6,4},{7,5},{8,14},{9,15},{10,... | collective-permute-start | bytes 294920 | tf_op jit(solution)/shard_map/ppermute | solution.py:504
  22.8 0.7 %shard_map.69 = (f32[6,32,128]{2,1,0:T(8,128)S(1)}, f32[6,32,128]{2,1,0:T(8,128)S(1)}) custom-call(f32[384,512]{1,0:T(8,128)S(1)} %get-tuple-element.49.refs_0_, s32[6,512]{1,0:T(8,128)S(1)} %get-tuple-element.50.refs_1_, bf16[128,448]{1,0:T(8,128)(2,1)S(1)} %get-tuple-element.53.refs_11_.refs_5_.refs_2_, ...), custom_call_target="tpu_custom_call" | custom-call | tf_op jit(solution)/shard_map/pallas_call | solution.py:416
  23.5 2.0 %collective-permute-start.8 = (f32[6,32,128]{2,1,0:T(8,128)S(1)}, f32[6,32,128]{2,1,0:T(8,128)S(1)}, u32[]{:S(2)}, u32[]{:S(2)}) collective-permute-start(f32[6,32,128]{2,1,0:T(8,128)S(1)} %get-tuple-element.78), channel_id=1, source_target_pairs={{0,3},{1,2},{2,5},{3,4},{4,7},{5,6},{6,1},{7,0},{8,11},{9,10},{10,... | collective-permute-start | bytes 294920 | tf_op jit(solution)/shard_map/ppermute | solution.py:504
  25.5 1.3 %collective-permute-start.9 = (f32[6,32,128]{2,1,0:T(8,128)S(1)}, f32[6,32,128]{2,1,0:T(8,128)S(1)}, u32[]{:S(2)}, u32[]{:S(2)}) collective-permute-start(f32[6,32,128]{2,1,0:T(8,128)S(1)} %get-tuple-element.79), channel_id=1, source_target_pairs={{0,7},{1,6},{2,1},{3,0},{4,3},{5,2},{6,5},{7,4},{8,15},{9,14},{10,... | collective-permute-start | bytes 294920 | tf_op jit(solution)/shard_map/ppermute | solution.py:504
  26.8 1.7 %collective-permute-start.10 = (f32[6,32,128]{2,1,0:T(8,128)S(1)}, f32[6,32,128]{2,1,0:T(8,128)S(1)}, u32[]{:S(2)}, u32[]{:S(2)}) collective-permute-start(f32[6,32,128]{2,1,0:T(8,128)S(1)} %get-tuple-element.80), channel_id=1, source_target_pairs={{0,1},{1,0},{2,3},{3,2},{4,5},{5,4},{6,7},{7,6},{8,9},{9,8},{10,11... | collective-permute-start | bytes 294920 | tf_op jit(solution)/shard_map/ppermute | solution.py:504
  28.5 0.3 collective-permute-start.4
  28.8 2.8 %collective-permute-start.5 = (f32[6,32,128]{2,1,0:T(8,128)S(1)}, f32[6,32,128]{2,1,0:T(8,128)S(1)}, u32[]{:S(2)}, u32[]{:S(2)}) collective-permute-start(f32[6,32,128]{2,1,0:T(8,128)S(1)} %get-tuple-element.75), channel_id=1, source_target_pairs={{0,5},{1,4},{2,7},{3,6},{4,1},{5,0},{6,3},{7,2},{8,13},{9,12},{10,... | collective-permute-start | bytes 294920 | tf_op jit(solution)/shard_map/ppermute | solution.py:504
  31.7 1.4 %shard_map.64 = (bf16[192,384]{1,0:T(8,128)(2,1)S(1)}, bf16[384,288]{1,0:T(8,128)(2,1)S(1)}) custom-call(f32[12,48]{1,0:T(8,128)} %bitcast.5, f32[12,48]{1,0:T(8,128)} %refs_1_.2), custom_call_target="tpu_custom_call" | custom-call | tf_op jit(solution)/shard_map/pallas_call | solution.py:416
  33.1 1.3 %collective-permute-done.4.refs_3_ = f32[6,32,128]{2,1,0:T(8,128)S(1)} collective-permute-done((f32[6,32,128]{2,1,0:T(8,128)S(1)}, f32[6,32,128]{2,1,0:T(8,128)S(1)}, u32[]{:S(2)}, u32[]{:S(2)}) %collective-permute-start.4) | collective-permute-done | bytes 98336 | tf_op jit(solution)/shard_map/ppermute | solution.py:504
  34.4 2.3 %collective-permute-done.5.refs_4_ = f32[6,32,128]{2,1,0:T(8,128)S(1)} collective-permute-done((f32[6,32,128]{2,1,0:T(8,128)S(1)}, f32[6,32,128]{2,1,0:T(8,128)S(1)}, u32[]{:S(2)}, u32[]{:S(2)}) %collective-permute-start.5) | collective-permute-done | bytes 98336 | tf_op jit(solution)/shard_map/ppermute | solution.py:504
  36.7 0.8 %shard_map.71 = (f32[6,32,128]{2,1,0:T(8,128)S(1)}, f32[6,32,128]{2,1,0:T(8,128)S(1)}, f32[6,32,128]{2,1,0:T(8,128)S(1)}, f32[6,32,128]{2,1,0:T(8,128)S(1)}, f32...) custom-call(bf16[192,384]{1,0:T(8,128)(2,1)S(1)} %get-tuple-element.4, ...), custom_call_target="tpu_custom_call" | custom-call | tf_op jit(solution)/shard_map/pallas_call | solution.py:416
  37.4 1.1 %collective-permute-start.15 = (f32[6,32,128]{2,1,0:T(8,128)S(1)}, f32[6,32,128]{2,1,0:T(8,128)S(1)}, u32[]{:S(2)}, u32[]{:S(2)}) collective-permute-start(f32[6,32,128]{2,1,0:T(8,128)S(1)} %get-tuple-element.86), channel_id=1, source_target_pairs={{0,4},{1,5},{2,6},{3,7},{4,0},{5,1},{6,2},{7,3},{8,12},{9,13},{10,... | collective-permute-start | bytes 294920 | tf_op jit(solution)/shard_map/ppermute | solution.py:504
  38.6 2.3 %collective-permute-start.16 = (f32[6,32,128]{2,1,0:T(8,128)S(1)}, f32[6,32,128]{2,1,0:T(8,128)S(1)}, u32[]{:S(2)}, u32[]{:S(2)}) collective-permute-start(f32[6,32,128]{2,1,0:T(8,128)S(1)} %get-tuple-element.87), channel_id=1, source_target_pairs={{0,5},{1,4},{2,7},{3,6},{4,1},{5,0},{6,3},{7,2},{8,13},{9,12},{10,... | collective-permute-start | bytes 294920 | tf_op jit(solution)/shard_map/ppermute | solution.py:504
  40.9 1.0 %collective-permute-start.11 = (f32[6,32,128]{2,1,0:T(8,128)S(1)}, f32[6,32,128]{2,1,0:T(8,128)S(1)}, u32[]{:S(2)}, u32[]{:S(2)}) collective-permute-start(f32[6,32,128]{2,1,0:T(8,128)S(1)} %get-tuple-element.81), channel_id=1, source_target_pairs={{0,6},{1,7},{2,0},{3,1},{4,2},{5,3},{6,4},{7,5},{8,14},{9,15},{10,... | collective-permute-start | bytes 294920 | tf_op jit(solution)/shard_map/ppermute | solution.py:504
  41.9 0.5 collective-permute-start.12
  42.4 0.8 %collective-permute-done.15.refs_1_ = f32[6,32,128]{2,1,0:T(8,128)S(1)} collective-permute-done((f32[6,32,128]{2,1,0:T(8,128)S(1)}, f32[6,32,128]{2,1,0:T(8,128)S(1)}, u32[]{:S(2)}, u32[]{:S(2)}) %collective-permute-start.15) | collective-permute-done | bytes 98336 | tf_op jit(solution)/shard_map/ppermute | solution.py:504
  43.2 1.8 %collective-permute-start.13 = (f32[6,32,128]{2,1,0:T(8,128)S(1)}, f32[6,32,128]{2,1,0:T(8,128)S(1)}, u32[]{:S(2)}, u32[]{:S(2)}) collective-permute-start(f32[6,32,128]{2,1,0:T(8,128)S(1)} %get-tuple-element.83), channel_id=1, source_target_pairs={{0,7},{1,6},{2,1},{3,0},{4,3},{5,2},{6,5},{7,4},{8,15},{9,14},{10,... | collective-permute-start | bytes 294920 | tf_op jit(solution)/shard_map/ppermute | solution.py:504
  45.0 1.3 %collective-permute-done.16.refs_2_ = f32[6,32,128]{2,1,0:T(8,128)S(1)} collective-permute-done((f32[6,32,128]{2,1,0:T(8,128)S(1)}, f32[6,32,128]{2,1,0:T(8,128)S(1)}, u32[]{:S(2)}, u32[]{:S(2)}) %collective-permute-start.16) | collective-permute-done | bytes 98336 | tf_op jit(solution)/shard_map/ppermute | solution.py:504
  46.3 0.8 %shard_map.72.refs_4_ = f32[6,64,512]{2,1,0:T(8,128)} custom-call(f32[6,32,128]{2,1,0:T(8,128)S(1)} %get-tuple-element.85.refs_0_, f32[6,32,128]{2,1,0:T(8,128)S(1)} %collective-permute-done.15.refs_1_, f32[6,32,128]{2,1,0:T(8,128)S(1)} %collective-permute-done.16.refs_2_, f32[6,32,128]{2,1,0:T(8,128)S(1)} %collective-permute-done.17.refs_3_), custom_call_target="tpu_custom_call" | custom-call | tf_op jit(solution)/shard_map/pallas_call | solution.py:416
  47.1 0.8 %collective-permute-done.12.refs_1_ = f32[6,32,128]{2,1,0:T(8,128)S(1)} collective-permute-done((f32[6,32,128]{2,1,0:T(8,128)S(1)}, f32[6,32,128]{2,1,0:T(8,128)S(1)}, u32[]{:S(2)}, u32[]{:S(2)}) %collective-permute-start.12) | collective-permute-done | bytes 98336 | tf_op jit(solution)/shard_map/ppermute | solution.py:504
  47.9 3.6 %collective-permute-done.14.refs_3_ = f32[6,32,128]{2,1,0:T(8,128)S(1)} collective-permute-done((f32[6,32,128]{2,1,0:T(8,128)S(1)}, f32[6,32,128]{2,1,0:T(8,128)S(1)}, u32[]{:S(2)}, u32[]{:S(2)}) %collective-permute-start.14) | collective-permute-done | bytes 98336 | tf_op jit(solution)/shard_map/ppermute | solution.py:504
  51.5 0.8 %shard_map.73 = f32[6,64,512]{2,1,0:T(8,128)} custom-call(f32[6,32,128]{2,1,0:T(8,128)S(1)} %collective-permute-done.11.refs_0_, f32[6,32,128]{2,1,0:T(8,128)S(1)} %collective-permute-done.12.refs_1_, f32[6,32,128]{2,1,0:T(8,128)S(1)} %collective-permute-done.13.refs_2_, ...), custom_call_target="tpu_custom_call", output_to_operand_aliasing={{}: (4, {})} | custom-call | tf_op jit(solution)/shard_map/pallas_call | solution.py:416
  (14 shorter events, 0.0 us)
Async XLA Ops:
  1.7 13.8 %collective-permute-start = (f32[392,128]{1,0:T(8,128)S(1)}, f32[392,128]{1,0:T(8,128)S(1)}, u32[]{:S(2)}, u32[]{:S(2)}) collective-permute-start(f32[392,128]{1,0:T(8,128)S(1)} %get-tuple-element.55), channel_id=1, source_target_pairs={{0,1},{1,0},{2,3},{3,2},{4,5},{5,4},{6,7},{7,6},{8,16},{9,17},{10,... | collective-permute-start | bytes 602120 | tf_op jit(solution)/shard_map/ppermute | solution.py:457
  4.1 11.5 %collective-permute-start.1 = (f32[392,128]{1,0:T(8,128)S(1)}, f32[392,128]{1,0:T(8,128)S(1)}, u32[]{:S(2)}, u32[]{:S(2)}) collective-permute-start(f32[392,128]{1,0:T(8,128)S(1)} %get-tuple-element.56), channel_id=1, source_target_pairs={{0,8},{1,9},{2,10},{3,11},{4,12},{5,13},{6,14},{7,15},{8,0},{9,1},... | collective-permute-start | bytes 602120 | tf_op jit(solution)/shard_map/ppermute | solution.py:458
  4.4 8.7 %collective-permute-start.2 = (f32[192,128]{1,0:T(8,128)S(1)}, f32[192,128]{1,0:T(8,128)S(1)}, u32[]{:S(2)}, u32[]{:S(2)}) collective-permute-start(f32[192,128]{1,0:T(8,128)S(1)} %get-tuple-element.57), channel_id=1, source_target_pairs={{0,1},{1,0},{2,3},{3,2},{4,5},{5,4},{6,7},{7,6},{8,16},{9,17},{10,... | collective-permute-start | bytes 294920 | tf_op jit(solution)/shard_map/ppermute | solution.py:455
  6.6 6.5 %collective-permute-start.3 = (f32[192,128]{1,0:T(8,128)S(1)}, f32[192,128]{1,0:T(8,128)S(1)}, u32[]{:S(2)}, u32[]{:S(2)}) collective-permute-start(f32[192,128]{1,0:T(8,128)S(1)} %get-tuple-element.58), channel_id=1, source_target_pairs={{0,8},{1,9},{2,10},{3,11},{4,12},{5,13},{6,14},{7,15},{8,0},{9,1},... | collective-permute-start | bytes 294920 | tf_op jit(solution)/shard_map/ppermute | solution.py:456
  19.9 8.6 %collective-permute-start.6 = (f32[6,32,128]{2,1,0:T(8,128)S(1)}, f32[6,32,128]{2,1,0:T(8,128)S(1)}, u32[]{:S(2)}, u32[]{:S(2)}) collective-permute-start(f32[6,32,128]{2,1,0:T(8,128)S(1)} %get-tuple-element.76), channel_id=1, source_target_pairs={{0,2},{1,3},{2,4},{3,5},{4,6},{5,7},{6,0},{7,1},{8,10},{9,11},{10,... | collective-permute-start | bytes 294920 | tf_op jit(solution)/shard_map/ppermute | solution.py:504
  21.2 7.6 %collective-permute-start.7 = (f32[6,32,128]{2,1,0:T(8,128)S(1)}, f32[6,32,128]{2,1,0:T(8,128)S(1)}, u32[]{:S(2)}, u32[]{:S(2)}) collective-permute-start(f32[6,32,128]{2,1,0:T(8,128)S(1)} %get-tuple-element.77), channel_id=1, source_target_pairs={{0,6},{1,7},{2,0},{3,1},{4,2},{5,3},{6,4},{7,5},{8,14},{9,15},{10,... | collective-permute-start | bytes 294920 | tf_op jit(solution)/shard_map/ppermute | solution.py:504
  23.5 9.6 %collective-permute-start.8 = (f32[6,32,128]{2,1,0:T(8,128)S(1)}, f32[6,32,128]{2,1,0:T(8,128)S(1)}, u32[]{:S(2)}, u32[]{:S(2)}) collective-permute-start(f32[6,32,128]{2,1,0:T(8,128)S(1)} %get-tuple-element.78), channel_id=1, source_target_pairs={{0,3},{1,2},{2,5},{3,4},{4,7},{5,6},{6,1},{7,0},{8,11},{9,10},{10,... | collective-permute-start | bytes 294920 | tf_op jit(solution)/shard_map/ppermute | solution.py:504
  25.5 7.7 %collective-permute-start.9 = (f32[6,32,128]{2,1,0:T(8,128)S(1)}, f32[6,32,128]{2,1,0:T(8,128)S(1)}, u32[]{:S(2)}, u32[]{:S(2)}) collective-permute-start(f32[6,32,128]{2,1,0:T(8,128)S(1)} %get-tuple-element.79), channel_id=1, source_target_pairs={{0,7},{1,6},{2,1},{3,0},{4,3},{5,2},{6,5},{7,4},{8,15},{9,14},{10,... | collective-permute-start | bytes 294920 | tf_op jit(solution)/shard_map/ppermute | solution.py:504
  26.8 6.3 %collective-permute-start.10 = (f32[6,32,128]{2,1,0:T(8,128)S(1)}, f32[6,32,128]{2,1,0:T(8,128)S(1)}, u32[]{:S(2)}, u32[]{:S(2)}) collective-permute-start(f32[6,32,128]{2,1,0:T(8,128)S(1)} %get-tuple-element.80), channel_id=1, source_target_pairs={{0,1},{1,0},{2,3},{3,2},{4,5},{5,4},{6,7},{7,6},{8,9},{9,8},{10,11... | collective-permute-start | bytes 294920 | tf_op jit(solution)/shard_map/ppermute | solution.py:504
  28.5 5.9 %collective-permute-start.4 = (f32[6,32,128]{2,1,0:T(8,128)S(1)}, f32[6,32,128]{2,1,0:T(8,128)S(1)}, u32[]{:S(2)}, u32[]{:S(2)}) collective-permute-start(f32[6,32,128]{2,1,0:T(8,128)S(1)} %get-tuple-element.74), channel_id=1, source_target_pairs={{0,4},{1,5},{2,6},{3,7},{4,0},{5,1},{6,2},{7,3},{8,12},{9,13},{10,... | collective-permute-start | bytes 294920 | tf_op jit(solution)/shard_map/ppermute | solution.py:504
  28.8 7.8 %collective-permute-start.5 = (f32[6,32,128]{2,1,0:T(8,128)S(1)}, f32[6,32,128]{2,1,0:T(8,128)S(1)}, u32[]{:S(2)}, u32[]{:S(2)}) collective-permute-start(f32[6,32,128]{2,1,0:T(8,128)S(1)} %get-tuple-element.75), channel_id=1, source_target_pairs={{0,5},{1,4},{2,7},{3,6},{4,1},{5,0},{6,3},{7,2},{8,13},{9,12},{10,... | collective-permute-start | bytes 294920 | tf_op jit(solution)/shard_map/ppermute | solution.py:504
  37.4 5.7 %collective-permute-start.15 = (f32[6,32,128]{2,1,0:T(8,128)S(1)}, f32[6,32,128]{2,1,0:T(8,128)S(1)}, u32[]{:S(2)}, u32[]{:S(2)}) collective-permute-start(f32[6,32,128]{2,1,0:T(8,128)S(1)} %get-tuple-element.86), channel_id=1, source_target_pairs={{0,4},{1,5},{2,6},{3,7},{4,0},{5,1},{6,2},{7,3},{8,12},{9,13},{10,... | collective-permute-start | bytes 294920 | tf_op jit(solution)/shard_map/ppermute | solution.py:504
  38.6 7.7 %collective-permute-start.16 = (f32[6,32,128]{2,1,0:T(8,128)S(1)}, f32[6,32,128]{2,1,0:T(8,128)S(1)}, u32[]{:S(2)}, u32[]{:S(2)}) collective-permute-start(f32[6,32,128]{2,1,0:T(8,128)S(1)} %get-tuple-element.87), channel_id=1, source_target_pairs={{0,5},{1,4},{2,7},{3,6},{4,1},{5,0},{6,3},{7,2},{8,13},{9,12},{10,... | collective-permute-start | bytes 294920 | tf_op jit(solution)/shard_map/ppermute | solution.py:504
  40.9 5.4 %collective-permute-start.17 = (f32[6,32,128]{2,1,0:T(8,128)S(1)}, f32[6,32,128]{2,1,0:T(8,128)S(1)}, u32[]{:S(2)}, u32[]{:S(2)}) collective-permute-start(f32[6,32,128]{2,1,0:T(8,128)S(1)} %get-tuple-element.88), channel_id=1, source_target_pairs={{0,1},{1,0},{2,3},{3,2},{4,5},{5,4},{6,7},{7,6},{8,9},{9,8},{10,11... | collective-permute-start | bytes 294920 | tf_op jit(solution)/shard_map/ppermute | solution.py:504
  40.9 6.2 %collective-permute-start.11 = (f32[6,32,128]{2,1,0:T(8,128)S(1)}, f32[6,32,128]{2,1,0:T(8,128)S(1)}, u32[]{:S(2)}, u32[]{:S(2)}) collective-permute-start(f32[6,32,128]{2,1,0:T(8,128)S(1)} %get-tuple-element.81), channel_id=1, source_target_pairs={{0,6},{1,7},{2,0},{3,1},{4,2},{5,3},{6,4},{7,5},{8,14},{9,15},{10,... | collective-permute-start | bytes 294920 | tf_op jit(solution)/shard_map/ppermute | solution.py:504
  41.9 6.1 %collective-permute-start.12 = (f32[6,32,128]{2,1,0:T(8,128)S(1)}, f32[6,32,128]{2,1,0:T(8,128)S(1)}, u32[]{:S(2)}, u32[]{:S(2)}) collective-permute-start(f32[6,32,128]{2,1,0:T(8,128)S(1)} %get-tuple-element.82), channel_id=1, source_target_pairs={{0,2},{1,3},{2,4},{3,5},{4,6},{5,7},{6,0},{7,1},{8,10},{9,11},{10,... | collective-permute-start | bytes 294920 | tf_op jit(solution)/shard_map/ppermute | solution.py:504
  43.2 4.7 %collective-permute-start.13 = (f32[6,32,128]{2,1,0:T(8,128)S(1)}, f32[6,32,128]{2,1,0:T(8,128)S(1)}, u32[]{:S(2)}, u32[]{:S(2)}) collective-permute-start(f32[6,32,128]{2,1,0:T(8,128)S(1)} %get-tuple-element.83), channel_id=1, source_target_pairs={{0,7},{1,6},{2,1},{3,0},{4,3},{5,2},{6,5},{7,4},{8,15},{9,14},{10,... | collective-permute-start | bytes 294920 | tf_op jit(solution)/shard_map/ppermute | solution.py:504
  46.3 5.3 %collective-permute-start.14 = (f32[6,32,128]{2,1,0:T(8,128)S(1)}, f32[6,32,128]{2,1,0:T(8,128)S(1)}, u32[]{:S(2)}, u32[]{:S(2)}) collective-permute-start(f32[6,32,128]{2,1,0:T(8,128)S(1)} %get-tuple-element.84), channel_id=1, source_target_pairs={{0,3},{1,2},{2,5},{3,4},{4,7},{5,6},{6,1},{7,0},{8,11},{9,10},{10,... | collective-permute-start | bytes 294920 | tf_op jit(solution)/shard_map/ppermute | solution.py:504

commit v4 on v3

--- a/solution.py
+++ b/solution.py
@@ -18,8 +18,8 @@
 MATMUL_FACES = 4
 KDIM = (NFACE + 1) * NP
 SLOTS = [(0, 0), (2, 0), (2, 1), (1, 0), (3, 0), (1, 1), (3, 1), (0, 1)]
-EARLY = (0, 1, 2, 7)
-LATE = (3, 4, 5, 6)
+EARLY = (0, 3, 4)
+LATE = (1, 2, 5, 6, 7)
 
 
 def first_half(rows):
@@ -57,36 +57,47 @@
     return copies
 
 
-def pack_kernel(
-    place_ref, history_hbm, adjacency_hbm, volume_hbm, face_hbm,
-    near_one, near_two, far_one, far_two, history, adjacency, volume_op, face_lift, sems,
-):
+def by_parity(place_ref, put, one, two):
+    @pl.when(place_ref[3] == 1)
+    def _():
+        put(one, two)
+
+    @pl.when(place_ref[3] == 0)
+    def _():
+        put(two, one)
+
+
+def near_kernel(place_ref, history_hbm, adjacency_hbm, near_one, near_two, bottom, top, adjacency, sems):
     half = ROWS // 2
     first = first_half(half)
-    copies = fetch(
-        [(history_hbm.at[r : r + 96, :], history.at[r : r + 96, :]) for r in range(0, ROWS, 96)]
-        + [(adjacency_hbm, adjacency), (volume_hbm, volume_op), (face_hbm, face_lift)],
-        sems,
-    )
-    for copy in copies:
+    pairs = [(history_hbm.at[:, cols(0)], bottom), (history_hbm.at[:, cols(3)], top), (adjacency_hbm, adjacency)]
+    for copy in fetch(pairs, sems):
         copy.wait()
 
-    def put(near_up, near_down, far_up, far_down):
-        near_up[...] = jnp.where(first, swap(history[0:half, cols(3)]), history[half:, cols(3)])
-        near_down[...] = jnp.where(first, history[0:half, cols(0)], swap(history[half:, cols(0)]))
-        far_up[0:ROWS, :] = straddle(history[:, cols(2)], history[:, cols(3)])
-        far_down[0:ROWS, :] = straddle(history[:, cols(0)], history[:, cols(1)])
-        for target, c in ((far_up, 3), (far_down, 0)):
-            target[ROWS:, :] = jnp.zeros((8, LANE), F32)
-            target[ROWS : ROWS + NFACE, :] = adjacency[:, cols(c)].astype(F32)
-
-    @pl.when(place_ref[3] == 1)
-    def _():
-        put(near_one, near_two, far_one, far_two)
-
-    @pl.when(place_ref[3] == 0)
-    def _():
-        put(near_two, near_one, far_two, far_one)
+    def put(up, down):
+        up[0:half, :] = jnp.where(first, swap(top[0:half, :]), top[half:, :])
+        down[0:half, :] = jnp.where(first, bottom[0:half, :], swap(bottom[half:, :]))
+        for target, c in ((up, 3), (down, 0)):
+            target[half:, :] = jnp.zeros((8, LANE), F32)
+            target[half : half + NFACE, :] = adjacency[:, cols(c)].astype(F32)
+
+    by_parity(place_ref, put, near_one, near_two)
+
+
+def far_kernel(
+    place_ref, history_hbm, adjacency_hbm, volume_hbm, face_hbm,
+    far_one, far_two, history, adjacency, volume_op, face_lift, sems,
+):
+    pairs = [(history_hbm.at[r : r + 96, :], history.at[r : r + 96, :]) for r in range(0, ROWS, 96)]
+    pairs += [(adjacency_hbm, adjacency), (volume_hbm, volume_op), (face_hbm, face_lift)]
+    for copy in fetch(pairs, sems):
+        copy.wait()
+
+    def put(up, down):
+        up[...] = straddle(history[:, cols(2)], history[:, cols(3)])
+        down[...] = straddle(history[:, cols(0)], history[:, cols(1)])
+
+    by_parity(place_ref, put, far_one, far_two)
 
 
 def place(adjacency, start):
@@ -179,15 +190,26 @@
 
 def middle_kernel(
     place_ref, history, adjacency, near_one, near_two, u0m, partsm, onehots, t1m, parts2m, t2m, parts3m, weights,
-    ends, end_parts, rim, rim_parts, t2, parts3,
+    ends, end_parts, rim, rim_parts, t2, parts3, edge, edge_rels,
     left, right, t1, parts2, gat_a, gat_b,
 ):
     origin = place_ref[0]
     odd = place_ref[3] == 1
     half = ROWS // 2
     first = first_half(half)
-    low = jnp.where(odd, near_two[...], near_one[...])
-    high = jnp.where(odd, near_one[...], near_two[...])
+    low = jnp.where(odd, near_two[0:half, :], near_one[0:half, :])
+    high = jnp.where(odd, near_one[0:half, :], near_two[0:half, :])
+    low_adj = jnp.where(odd, near_two[half:, :], near_one[half:, :]).astype(jnp.int32)[0:NFACE]
+    high_adj = jnp.where(odd, near_one[half:, :], near_two[half:, :]).astype(jnp.int32)[0:NFACE]
+    rels = [
+        place(low_adj, origin),
+        place(high_adj, origin + 640),
+        place(mix(low_adj, adjacency[:, cols(0)]), origin + 64),
+        place(mix(adjacency[:, cols(3)], high_adj), origin + 576),
+    ]
+    for slot, rel in enumerate(rels):
+        write_onehots(edge, slot, rel)
+        edge_rels[slot, 0:NFACE, :] = rel
     ends[0:half, cols(0)] = jnp.where(first, low, u0m[0:half, cols(0)])
     ends[half:, cols(0)] = jnp.where(first, swap(low), u0m[half:, cols(0)])
     ends[0:half, cols(1)] = jnp.where(first, u0m[0:half, cols(4)], swap(high))
@@ -224,24 +246,14 @@
 
 def edge_kernel(
     place_ref, history, adjacency, far_one, far_two, onehots, weights, ends, end_parts, rim, rim_parts, t2m, parts3m,
-    *rest,
+    edge, edge_rels, *rest,
 ):
     outs = rest[:2]
-    t2, parts3, low, high, left, right, left2, right2, edge, tips, gat_a, gat_b = rest[2:]
-    origin = place_ref[0]
+    t2, parts3, low, high, left, right, left2, right2, tips, gat_a, gat_b = rest[2:]
     odd = place_ref[3] == 1
     low[...] = jnp.where(odd, far_two[...], far_one[...])
     high[...] = jnp.where(odd, far_one[...], far_two[...])
-    low_adj = low[ROWS:, :].astype(jnp.int32)[0:NFACE]
-    high_adj = high[ROWS:, :].astype(jnp.int32)[0:NFACE]
-    rels = [
-        place(low_adj, origin),
-        place(high_adj, origin + 640),
-        place(mix(low_adj, adjacency[:, cols(0)]), origin + 64),
-        place(mix(adjacency[:, cols(3)], high_adj), origin + 576),
-    ]
-    for slot, rel in enumerate(rels):
-        write_onehots(edge, slot, rel)
+    rels = [edge_rels[slot, 0:NFACE, :] for slot in range(4)]
     put_parts(left, cols(0), low[0:ROWS, :])
     left[:, cols(1)] = end_parts[:, cols(0)]
     right[:, cols(0)] = end_parts[:, cols(1)]
@@ -268,7 +280,7 @@
 
 
 def last_block(place_ref, dx, history, adjacency, weights, onehots, t2, parts3, gathered, outs):
-    b = (place_ref[1] + dx) & 3
+    b = place_ref[1] ^ dx
     upper = place_ref[2] == 1
     col = pl.multiple_of(b * LANE, LANE)
     rel = place(adjacency[:, pl.ds(col, LANE)], place_ref[0] + 128 + col)
@@ -295,7 +307,7 @@
 
 def source_of(x, core, slot):
     dx, dc = SLOTS[slot]
-    return ((x - dx) & 3) * 2 + (core ^ dc)
+    return (x ^ dx) * 2 + (core ^ dc)
 
 
 def table_kernel(place_ref, schmid_hbm, hardening_hbm, mixing, renewing, schmid_map, hardening, sems):
@@ -382,7 +394,7 @@
         pairs = []
         for piece, slot in zip(pieces, slots):
             dx, dc = SLOTS[slot]
-            col = pl.multiple_of(((x + dx) & 3) * LANE, LANE)
+            col = pl.multiple_of((x ^ dx) * LANE, LANE)
             row = pl.multiple_of((core ^ dc) * 32, 32)
             pairs.append((piece, out.at[:, pl.ds(row, 32), pl.ds(col, LANE)]))
         for copy in fetch(pairs, sems):
@@ -429,14 +441,15 @@
     count = lax.axis_size("zone")
     groups = lax.axis_size("var")
     flat = history.reshape(ROWS, NZ)
-    near = ((ROWS // 2, LANE), F32)
-    far = ((ROWS + 8, LANE), F32)
-    near_one, near_two, far_one, far_two, local, faces, volume, lifts = call(
-        pack_kernel,
+    near = ((ROWS // 2 + 8, LANE), F32)
+    far = ((ROWS, LANE), F32)
+    near_one, near_two = call(
+        near_kernel, (), [near, near], [far, far, ((NFACE, NZ), jnp.int32)], far_args=(flat, adjacency), copies=3
+    )
+    far_one, far_two, local, faces, volume, lifts = call(
+        far_kernel,
         (),
-        [
-            near, near, far, far, ((ROWS, NZ), F32), ((NFACE, NZ), jnp.int32), ((NP, NP), F32), ((NFACE * NP, NP), F32),
-        ],
+        [far, far, ((ROWS, NZ), F32), ((NFACE, NZ), jnp.int32), ((NP, NP), F32), ((NFACE * NP, NP), F32)],
         far_args=(flat, adjacency, volume_op, face_lift.reshape(NFACE * NP, NP)),
         copies=7,
     )
@@ -472,7 +485,10 @@
     middle = call(
         middle_kernel,
         (local, faces, near_one, near_two, *inner, weights),
-        [wide(2), pair(2), wide(2), pair(2), wide(3), pair(3)],
+        [
+            wide(2), pair(2), wide(2), pair(2), wide(3), pair(3),
+            ((4, 256, MATMUL_FACES * LANE), BF16), ((4, 8, LANE), jnp.int32),
+        ],
         [pair(2), pair(2), wide(4), pair(4), buffer, buffer],
     )
     piece = ((NV, 32, LANE), F32)
@@ -481,8 +497,7 @@
         (local, faces, far_one, far_two, onehots, weights, *middle),
         [piece, piece, wide(5), pair(5)],
         [
-            far, far, pair(2), pair(2), pair(2), pair(2), ((4, 256, MATMUL_FACES * LANE), BF16),
-            wide(2), buffer, buffer,
+            far, far, pair(2), pair(2), pair(2), pair(2), wide(2), buffer, buffer,
         ],
     )
     ready = {(2, 0): ahead[0], (2, 1): ahead[1]}
@@ -500,7 +515,7 @@
     def exchange(piece, dx, dc):
         if dx == 0 and dc == 0:
             return piece
-        pairs = [(v, ((v // 2 + dx) % 4) * 2 + ((v % 2) ^ dc)) for v in range(8)]
+        pairs = [(v, v ^ (2 * dx + dc)) for v in range(groups)]
         return lax.ppermute(piece, "var", pairs)
 
     points = [exchange(piece, dx, dc) for piece, (dx, dc) in zip(advected, SLOTS)]
@@ -518,7 +533,7 @@
         [piece] * 8,
         [((ROWS, 512), BF16), ((ROWS, 512), BF16), ((288, 512), BF16)],
     )
-    returned = [exchange(piece, (4 - dx) % 4, dc) for piece, (dx, dc) in zip(renewed, SLOTS)]
+    returned = [exchange(piece, dx, dc) for piece, (dx, dc) in zip(renewed, SLOTS)]
     out = call(
         merge_kernel(EARLY), [returned[i] for i in EARLY], [((NV, NP, NZ), F32)],
         copies=len(EARLY), hbm_out=True,

time: 52.6 us -> 51.3 us (0.975)
  the two profiles are of different devices: /device:TPU:129 before, /device:TPU:120 now
where the time goes in v4:
time: 51.3 us; the launch traced here: 50.6 us
  starting transfers between devices  21.5 us (42%)
  Pallas kernels  16.9 us (33%)
  waiting for transfers between devices  11.8 us (23%)
    pallas_call x11, Pallas kernels, call(): pl.pallas_call(placed, out_shape=tuple((jax.ShapeDtypeStruct(shape, dtype...  16.9 us
    ppermute x14, starting transfers between devices, exchange(): return lax.ppermute(piece, 'var', pairs)  15.4 us
    ppermute x14, waiting for transfers between devices, exchange(): return lax.ppermute(piece, 'var', pairs)  9.32 us
    ppermute x1, starting transfers between devices, per_device(): near_one = lax.ppermute(near_one, axes, one)  3.24 us
    ppermute x1, starting transfers between devices, per_device(): far_one = lax.ppermute(far_one, axes, one)  2.87 us
    ppermute x1, waiting for transfers between devices, per_device(): near_one = lax.ppermute(near_one, axes, one)  2.5 us
  transfers between devices with their start and end apart: 18, of which 7 were waited for; matrix products, arithmetic and copies ran while one was open for 0% of the time, Pallas kernels for 19%

profile of v4, /device:TPU:120, one launch (start us, length us, event | category | flops | bytes accessed | tf_op | source)
XLA Modules:
  0.0 50.6 jit_solution(11918236426693350206)
XLA Ops:
  0.0 1.6 %shard_map.65 = (f32[384,128]{1,0:T(8,128)S(1)}, f32[384,128]{1,0:T(8,128)S(1)}, f32[384,512]{1,0:T(8,128)S(1)}, s32[6,512]{1,0:T(8,128)S(1)}, f32[64,64]{1,0:T(8,128)S(1)}, /*index=5*/f32[384,64]{1,0:T(8,128)S(1)}) custom-call(f32[384,512]{1,0:T(8,128)} %bitcast.3, s32[6,512]{1,0:T(8,128)} %refs_1_.5, f32[64,64]{1,0:T(8,128)} %refs_2_.1, f32[384,64]{1,0:T(8,128)} %bitcast.5), custom_call_target="tpu_custom_call" | custom-call | tf_op jit(solution)/shard_map/pallas_call | solution.py:428
  1.6 2.9 %collective-permute-start = (f32[384,128]{1,0:T(8,128)S(1)}, f32[384,128]{1,0:T(8,128)S(1)}, u32[]{:S(2)}, u32[]{:S(2)}) collective-permute-start(f32[384,128]{1,0:T(8,128)S(1)} %get-tuple-element.57), channel_id=1, source_target_pairs={{0,1},{1,0},{2,3},{3,2},{4,5},{5,4},{6,7},{7,6},{8,16},{9,17},{10,... | collective-permute-start | bytes 589832 | tf_op jit(solution)/shard_map/ppermute | solution.py:470
  4.5 1.2 %shard_map.67 = (f32[200,128]{1,0:T(8,128)S(1)}, f32[200,128]{1,0:T(8,128)S(1)}) custom-call(f32[384,512]{1,0:T(8,128)} %bitcast.4, s32[6,512]{1,0:T(8,128)} %refs_1_.5), custom_call_target="tpu_custom_call" | custom-call | tf_op jit(solution)/shard_map/pallas_call | solution.py:428
  5.7 3.2 %collective-permute-start.2 = (f32[200,128]{1,0:T(8,128)S(1)}, f32[200,128]{1,0:T(8,128)S(1)}, u32[]{:S(2)}, u32[]{:S(2)}) collective-permute-start(f32[200,128]{1,0:T(8,128)S(1)} %get-tuple-element.59), channel_id=1, source_target_pairs={{0,1},{1,0},{2,3},{3,2},{4,5},{5,4},{6,7},{7,6},{8,16},{9,17},{10,... | collective-permute-start | bytes 307208 | tf_op jit(solution)/shard_map/ppermute | solution.py:468
  8.9 2.4 %shard_map.66 = (f32[384,640]{1,0:T(8,128)S(1)}, bf16[768,384]{1,0:T(8,128)(2,1)S(1)}, bf16[7,256,512]{2,1,0:T(8,128)(2,1)S(1)}, f32[384,256]{1,0:T(8,128)S(1)},...) custom-call(f32[384,512]{1,0:T(8,128)S(1)} %get-tuple-element.51.ref, ...), custom_call_target="tpu_custom_call" | custom-call | tf_op jit(solution)/shard_map/pallas_call | solution.py:428
  11.4 2.5 %collective-permute-done.2.refs_2_ = f32[200,128]{1,0:T(8,128)S(1)} collective-permute-done((f32[200,128]{1,0:T(8,128)S(1)}, f32[200,128]{1,0:T(8,128)S(1)}, u32[]{:S(2)}, u32[]{:S(2)}) %collective-permute-start.2) | collective-permute-done | bytes 102432 | tf_op jit(solution)/shard_map/ppermute | solution.py:468
  13.9 2.9 %shard_map.68 = (f32[384,256]{1,0:T(8,128)S(1)}, bf16[768,256]{1,0:T(8,128)(2,1)S(1)}, f32[384,256]{1,0:T(8,128)S(1)}, bf16[768,256]{1,0:T(8,128)(2,1)S(1)}, f32...) custom-call(f32[384,512]{1,0:T(8,128)S(1)} %get-tuple-element.51.ref, ...), custom_call_target="tpu_custom_call" | custom-call | tf_op jit(solution)/shard_map/pallas_call | solution.py:428
  16.9 3.1 %shard_map.69 = (f32[6,32,128]{2,1,0:T(8,128)S(1)}, f32[6,32,128]{2,1,0:T(8,128)S(1)}, f32[384,640]{1,0:T(8,128)S(1)}, bf16[768,640]{1,0:T(8,128)(2,1)S(1)}) custom-call(f32[384,512]{1,0:T(8,128)S(1)} %get-tuple-element.51.refs_0_, s32[6,512]{1,0:T(8,128)S(1)} %get-tuple-element.52.refs_1_, f32[384,128]{1,0:T(8,128)S(1)} %collective-permute-done.refs_2_, ...), custom_call_target="tpu_custom_call" | custom-call | tf_op jit(solution)/shard_map/pallas_call | solution.py:428
  20.0 1.2 %shard_map.71 = (f32[6,32,128]{2,1,0:T(8,128)S(1)}, f32[6,32,128]{2,1,0:T(8,128)S(1)}, f32[6,32,128]{2,1,0:T(8,128)S(1)}, f32[6,32,128]{2,1,0:T(8,128)S(1)}) custom-call(f32[384,512]{1,0:T(8,128)S(1)} %get-tuple-element.51.refs_0_, s32[6,512]{1,0:T(8,128)S(1)} %get-tuple-element.52.refs_1_, bf16[128,448]{1,0:T(8,128)(2,1)S(1)} %get-tuple-element.55.refs_11_.refs_5_.refs_2_, ...), custom_call_target="tpu_custom_call" | custom-call | tf_op jit(solution)/shard_map/pallas_call | solution.py:428
  21.2 1.6 %collective-permute-start.6 = (f32[6,32,128]{2,1,0:T(8,128)S(1)}, f32[6,32,128]{2,1,0:T(8,128)S(1)}, u32[]{:S(2)}, u32[]{:S(2)}) collective-permute-start(f32[6,32,128]{2,1,0:T(8,128)S(1)} %get-tuple-element.80), channel_id=1, source_target_pairs={{0,2},{1,3},{2,0},{3,1},{4,6},{5,7},{6,4},{7,5},{8,10},{9,11},{10,... | collective-permute-start | bytes 294920 | tf_op jit(solution)/shard_map/ppermute | solution.py:519
  22.8 2.1 %collective-permute-start.7 = (f32[6,32,128]{2,1,0:T(8,128)S(1)}, f32[6,32,128]{2,1,0:T(8,128)S(1)}, u32[]{:S(2)}, u32[]{:S(2)}) collective-permute-start(f32[6,32,128]{2,1,0:T(8,128)S(1)} %get-tuple-element.81), channel_id=1, source_target_pairs={{0,6},{1,7},{2,4},{3,5},{4,2},{5,3},{6,0},{7,1},{8,14},{9,15},{10,... | collective-permute-start | bytes 294920 | tf_op jit(solution)/shard_map/ppermute | solution.py:519
  24.9 0.7 %shard_map.70 = (f32[6,32,128]{2,1,0:T(8,128)S(1)}, f32[6,32,128]{2,1,0:T(8,128)S(1)}) custom-call(f32[384,512]{1,0:T(8,128)S(1)} %get-tuple-element.51.refs_0_, s32[6,512]{1,0:T(8,128)S(1)} %get-tuple-element.52.refs_1_, bf16[128,448]{1,0:T(8,128)(2,1)S(1)} %get-tuple-element.55.refs_11_.refs_5_.refs_2_, ...), custom_call_target="tpu_custom_call" | custom-call | tf_op jit(solution)/shard_map/pallas_call | solution.py:428
  25.7 0.9 %collective-permute-start.9 = (f32[6,32,128]{2,1,0:T(8,128)S(1)}, f32[6,32,128]{2,1,0:T(8,128)S(1)}, u32[]{:S(2)}, u32[]{:S(2)}) collective-permute-start(f32[6,32,128]{2,1,0:T(8,128)S(1)} %get-tuple-element.83), channel_id=1, source_target_pairs={{0,7},{1,6},{2,5},{3,4},{4,3},{5,2},{6,1},{7,0},{8,15},{9,14},{10,... | collective-permute-start | bytes 294920 | tf_op jit(solution)/shard_map/ppermute | solution.py:519
  26.6 0.4 collective-permute-start.10
  27.0 2.4 %collective-permute-start.4 = (f32[6,32,128]{2,1,0:T(8,128)S(1)}, f32[6,32,128]{2,1,0:T(8,128)S(1)}, u32[]{:S(2)}, u32[]{:S(2)}) collective-permute-start(f32[6,32,128]{2,1,0:T(8,128)S(1)} %get-tuple-element.78), channel_id=1, source_target_pairs={{0,4},{1,5},{2,6},{3,7},{4,0},{5,1},{6,2},{7,3},{8,12},{9,13},{10,... | collective-permute-start | bytes 294920 | tf_op jit(solution)/shard_map/ppermute | solution.py:519
  29.5 0.5 collective-permute-start.5
  30.0 1.4 %shard_map.64 = (bf16[192,384]{1,0:T(8,128)(2,1)S(1)}, bf16[384,288]{1,0:T(8,128)(2,1)S(1)}) custom-call(f32[12,48]{1,0:T(8,128)} %bitcast.6, f32[12,48]{1,0:T(8,128)} %refs_1_.3), custom_call_target="tpu_custom_call" | custom-call | tf_op jit(solution)/shard_map/pallas_call | solution.py:428
  31.4 2.0 %collective-permute-done.4.refs_3_ = f32[6,32,128]{2,1,0:T(8,128)S(1)} collective-permute-done((f32[6,32,128]{2,1,0:T(8,128)S(1)}, f32[6,32,128]{2,1,0:T(8,128)S(1)}, u32[]{:S(2)}, u32[]{:S(2)}) %collective-permute-start.4) | collective-permute-done | bytes 98336 | tf_op jit(solution)/shard_map/ppermute | solution.py:519
  33.4 2.3 %collective-permute-done.5.refs_4_ = f32[6,32,128]{2,1,0:T(8,128)S(1)} collective-permute-done((f32[6,32,128]{2,1,0:T(8,128)S(1)}, f32[6,32,128]{2,1,0:T(8,128)S(1)}, u32[]{:S(2)}, u32[]{:S(2)}) %collective-permute-start.5) | collective-permute-done | bytes 98336 | tf_op jit(solution)/shard_map/ppermute | solution.py:519
  35.7 0.8 %shard_map.72 = (f32[6,32,128]{2,1,0:T(8,128)S(1)}, f32[6,32,128]{2,1,0:T(8,128)S(1)}, f32[6,32,128]{2,1,0:T(8,128)S(1)}, f32[6,32,128]{2,1,0:T(8,128)S(1)}, f32...) custom-call(bf16[192,384]{1,0:T(8,128)(2,1)S(1)} %get-tuple-element.4, ...), custom_call_target="tpu_custom_call" | custom-call | tf_op jit(solution)/shard_map/pallas_call | solution.py:428
  36.4 0.9 %collective-permute-start.16 = (f32[6,32,128]{2,1,0:T(8,128)S(1)}, f32[6,32,128]{2,1,0:T(8,128)S(1)}, u32[]{:S(2)}, u32[]{:S(2)}) collective-permute-start(f32[6,32,128]{2,1,0:T(8,128)S(1)} %get-tuple-element.91), channel_id=1, source_target_pairs={{0,2},{1,3},{2,0},{3,1},{4,6},{5,7},{6,4},{7,5},{8,10},{9,11},{10,... | collective-permute-start | bytes 294920 | tf_op jit(solution)/shard_map/ppermute | solution.py:519
  37.3 1.9 %collective-permute-start.17 = (f32[6,32,128]{2,1,0:T(8,128)S(1)}, f32[6,32,128]{2,1,0:T(8,128)S(1)}, u32[]{:S(2)}, u32[]{:S(2)}) collective-permute-start(f32[6,32,128]{2,1,0:T(8,128)S(1)} %get-tuple-element.92), channel_id=1, source_target_pairs={{0,6},{1,7},{2,4},{3,5},{4,2},{5,3},{6,0},{7,1},{8,14},{9,15},{10,... | collective-permute-start | bytes 294920 | tf_op jit(solution)/shard_map/ppermute | solution.py:519
  39.3 1.4 %collective-permute-start.11 = (f32[6,32,128]{2,1,0:T(8,128)S(1)}, f32[6,32,128]{2,1,0:T(8,128)S(1)}, u32[]{:S(2)}, u32[]{:S(2)}) collective-permute-start(f32[6,32,128]{2,1,0:T(8,128)S(1)} %get-tuple-element.85), channel_id=1, source_target_pairs={{0,4},{1,5},{2,6},{3,7},{4,0},{5,1},{6,2},{7,3},{8,12},{9,13},{10,... | collective-permute-start | bytes 294920 | tf_op jit(solution)/shard_map/ppermute | solution.py:519
  40.6 1.2 %collective-permute-start.12 = (f32[6,32,128]{2,1,0:T(8,128)S(1)}, f32[6,32,128]{2,1,0:T(8,128)S(1)}, u32[]{:S(2)}, u32[]{:S(2)}) collective-permute-start(f32[6,32,128]{2,1,0:T(8,128)S(1)} %get-tuple-element.86), channel_id=1, source_target_pairs={{0,5},{1,4},{2,7},{3,6},{4,1},{5,0},{6,3},{7,2},{8,13},{9,12},{10,... | collective-permute-start | bytes 294920 | tf_op jit(solution)/shard_map/ppermute | solution.py:519
  41.8 1.3 %collective-permute-start.13 = (f32[6,32,128]{2,1,0:T(8,128)S(1)}, f32[6,32,128]{2,1,0:T(8,128)S(1)}, u32[]{:S(2)}, u32[]{:S(2)}) collective-permute-start(f32[6,32,128]{2,1,0:T(8,128)S(1)} %get-tuple-element.87), channel_id=1, source_target_pairs={{0,3},{1,2},{2,1},{3,0},{4,7},{5,6},{6,5},{7,4},{8,11},{9,10},{10,... | collective-permute-start | bytes 294920 | tf_op jit(solution)/shard_map/ppermute | solution.py:519
  43.1 0.7 %collective-permute-start.14 = (f32[6,32,128]{2,1,0:T(8,128)S(1)}, f32[6,32,128]{2,1,0:T(8,128)S(1)}, u32[]{:S(2)}, u32[]{:S(2)}) collective-permute-start(f32[6,32,128]{2,1,0:T(8,128)S(1)} %get-tuple-element.88), channel_id=1, source_target_pairs={{0,7},{1,6},{2,5},{3,4},{4,3},{5,2},{6,1},{7,0},{8,15},{9,14},{10,... | collective-permute-start | bytes 294920 | tf_op jit(solution)/shard_map/ppermute | solution.py:519
  43.8 2.3 %collective-permute-done.17.refs_2_ = f32[6,32,128]{2,1,0:T(8,128)S(1)} collective-permute-done((f32[6,32,128]{2,1,0:T(8,128)S(1)}, f32[6,32,128]{2,1,0:T(8,128)S(1)}, u32[]{:S(2)}, u32[]{:S(2)}) %collective-permute-start.17) | collective-permute-done | bytes 98336 | tf_op jit(solution)/shard_map/ppermute | solution.py:519
  46.2 0.7 %shard_map.73.refs_5_ = f32[6,64,512]{2,1,0:T(8,128)} custom-call(f32[6,32,128]{2,1,0:T(8,128)S(1)} %get-tuple-element.90.refs_0_, f32[6,32,128]{2,1,0:T(8,128)S(1)} %collective-permute-done.16.refs_1_, f32[6,32,128]{2,1,0:T(8,128)S(1)} %collective-permute-done.17.refs_2_), custom_call_target="tpu_custom_call" | custom-call | tf_op jit(solution)/shard_map/pallas_call | solution.py:428
  46.9 0.3 collective-permute-done.12.refs_1_
  47.2 1.0 %collective-permute-done.13.refs_2_ = f32[6,32,128]{2,1,0:T(8,128)S(1)} collective-permute-done((f32[6,32,128]{2,1,0:T(8,128)S(1)}, f32[6,32,128]{2,1,0:T(8,128)S(1)}, u32[]{:S(2)}, u32[]{:S(2)}) %collective-permute-start.13) | collective-permute-done | bytes 98336 | tf_op jit(solution)/shard_map/ppermute | solution.py:519
  48.2 1.4 %collective-permute-done.14.refs_3_ = f32[6,32,128]{2,1,0:T(8,128)S(1)} collective-permute-done((f32[6,32,128]{2,1,0:T(8,128)S(1)}, f32[6,32,128]{2,1,0:T(8,128)S(1)}, u32[]{:S(2)}, u32[]{:S(2)}) %collective-permute-start.14) | collective-permute-done | bytes 98336 | tf_op jit(solution)/shard_map/ppermute | solution.py:519
  49.6 0.8 %shard_map.74 = f32[6,64,512]{2,1,0:T(8,128)} custom-call(f32[6,32,128]{2,1,0:T(8,128)S(1)} %collective-permute-done.11.refs_0_, f32[6,32,128]{2,1,0:T(8,128)S(1)} %collective-permute-done.12.refs_1_, f32[6,32,128]{2,1,0:T(8,128)S(1)} %collective-permute-done.13.refs_2_, ...), custom_call_target="tpu_custom_call", output_to_operand_aliasing={{}: (5, {})} | custom-call | tf_op jit(solution)/shard_map/pallas_call | solution.py:428
  (15 shorter events, 0.1 us)
Async XLA Ops:
  1.6 15.2 %collective-permute-start = (f32[384,128]{1,0:T(8,128)S(1)}, f32[384,128]{1,0:T(8,128)S(1)}, u32[]{:S(2)}, u32[]{:S(2)}) collective-permute-start(f32[384,128]{1,0:T(8,128)S(1)} %get-tuple-element.57), channel_id=1, source_target_pairs={{0,1},{1,0},{2,3},{3,2},{4,5},{5,4},{6,7},{7,6},{8,16},{9,17},{10,... | collective-permute-start | bytes 589832 | tf_op jit(solution)/shard_map/ppermute | solution.py:470
  4.5 12.3 %collective-permute-start.1 = (f32[384,128]{1,0:T(8,128)S(1)}, f32[384,128]{1,0:T(8,128)S(1)}, u32[]{:S(2)}, u32[]{:S(2)}) collective-permute-start(f32[384,128]{1,0:T(8,128)S(1)} %get-tuple-element.58), channel_id=1, source_target_pairs={{0,8},{1,9},{2,10},{3,11},{4,12},{5,13},{6,14},{7,15},{8,0},{9,1},... | collective-permute-start | bytes 589832 | tf_op jit(solution)/shard_map/ppermute | solution.py:471
  5.7 8.2 %collective-permute-start.2 = (f32[200,128]{1,0:T(8,128)S(1)}, f32[200,128]{1,0:T(8,128)S(1)}, u32[]{:S(2)}, u32[]{:S(2)}) collective-permute-start(f32[200,128]{1,0:T(8,128)S(1)} %get-tuple-element.59), channel_id=1, source_target_pairs={{0,1},{1,0},{2,3},{3,2},{4,5},{5,4},{6,7},{7,6},{8,16},{9,17},{10,... | collective-permute-start | bytes 307208 | tf_op jit(solution)/shard_map/ppermute | solution.py:468
  8.9 5.0 %collective-permute-start.3 = (f32[200,128]{1,0:T(8,128)S(1)}, f32[200,128]{1,0:T(8,128)S(1)}, u32[]{:S(2)}, u32[]{:S(2)}) collective-permute-start(f32[200,128]{1,0:T(8,128)S(1)} %get-tuple-element.60), channel_id=1, source_target_pairs={{0,8},{1,9},{2,10},{3,11},{4,12},{5,13},{6,14},{7,15},{8,0},{9,1},... | collective-permute-start | bytes 307208 | tf_op jit(solution)/shard_map/ppermute | solution.py:469
  21.2 5.8 %collective-permute-start.6 = (f32[6,32,128]{2,1,0:T(8,128)S(1)}, f32[6,32,128]{2,1,0:T(8,128)S(1)}, u32[]{:S(2)}, u32[]{:S(2)}) collective-permute-start(f32[6,32,128]{2,1,0:T(8,128)S(1)} %get-tuple-element.80), channel_id=1, source_target_pairs={{0,2},{1,3},{2,0},{3,1},{4,6},{5,7},{6,4},{7,5},{8,10},{9,11},{10,... | collective-permute-start | bytes 294920 | tf_op jit(solution)/shard_map/ppermute | solution.py:519
  22.8 6.7 %collective-permute-start.7 = (f32[6,32,128]{2,1,0:T(8,128)S(1)}, f32[6,32,128]{2,1,0:T(8,128)S(1)}, u32[]{:S(2)}, u32[]{:S(2)}) collective-permute-start(f32[6,32,128]{2,1,0:T(8,128)S(1)} %get-tuple-element.81), channel_id=1, source_target_pairs={{0,6},{1,7},{2,4},{3,5},{4,2},{5,3},{6,0},{7,1},{8,14},{9,15},{10,... | collective-permute-start | bytes 294920 | tf_op jit(solution)/shard_map/ppermute | solution.py:519
  25.6 5.8 %collective-permute-start.8 = (f32[6,32,128]{2,1,0:T(8,128)S(1)}, f32[6,32,128]{2,1,0:T(8,128)S(1)}, u32[]{:S(2)}, u32[]{:S(2)}) collective-permute-start(f32[6,32,128]{2,1,0:T(8,128)S(1)} %get-tuple-element.82), channel_id=1, source_target_pairs={{0,3},{1,2},{2,1},{3,0},{4,7},{5,6},{6,5},{7,4},{8,11},{9,10},{10,... | collective-permute-start | bytes 294920 | tf_op jit(solution)/shard_map/ppermute | solution.py:519
  25.7 5.7 %collective-permute-start.9 = (f32[6,32,128]{2,1,0:T(8,128)S(1)}, f32[6,32,128]{2,1,0:T(8,128)S(1)}, u32[]{:S(2)}, u32[]{:S(2)}) collective-permute-start(f32[6,32,128]{2,1,0:T(8,128)S(1)} %get-tuple-element.83), channel_id=1, source_target_pairs={{0,7},{1,6},{2,5},{3,4},{4,3},{5,2},{6,1},{7,0},{8,15},{9,14},{10,... | collective-permute-start | bytes 294920 | tf_op jit(solution)/shard_map/ppermute | solution.py:519
  26.6 4.8 %collective-permute-start.10 = (f32[6,32,128]{2,1,0:T(8,128)S(1)}, f32[6,32,128]{2,1,0:T(8,128)S(1)}, u32[]{:S(2)}, u32[]{:S(2)}) collective-permute-start(f32[6,32,128]{2,1,0:T(8,128)S(1)} %get-tuple-element.84), channel_id=1, source_target_pairs={{0,1},{1,0},{2,3},{3,2},{4,5},{5,4},{6,7},{7,6},{8,9},{9,8},{10,11... | collective-permute-start | bytes 294920 | tf_op jit(solution)/shard_map/ppermute | solution.py:519
  27.0 6.4 %collective-permute-start.4 = (f32[6,32,128]{2,1,0:T(8,128)S(1)}, f32[6,32,128]{2,1,0:T(8,128)S(1)}, u32[]{:S(2)}, u32[]{:S(2)}) collective-permute-start(f32[6,32,128]{2,1,0:T(8,128)S(1)} %get-tuple-element.78), channel_id=1, source_target_pairs={{0,4},{1,5},{2,6},{3,7},{4,0},{5,1},{6,2},{7,3},{8,12},{9,13},{10,... | collective-permute-start | bytes 294920 | tf_op jit(solution)/shard_map/ppermute | solution.py:519
  29.5 6.2 %collective-permute-start.5 = (f32[6,32,128]{2,1,0:T(8,128)S(1)}, f32[6,32,128]{2,1,0:T(8,128)S(1)}, u32[]{:S(2)}, u32[]{:S(2)}) collective-permute-start(f32[6,32,128]{2,1,0:T(8,128)S(1)} %get-tuple-element.79), channel_id=1, source_target_pairs={{0,5},{1,4},{2,7},{3,6},{4,1},{5,0},{6,3},{7,2},{8,13},{9,12},{10,... | collective-permute-start | bytes 294920 | tf_op jit(solution)/shard_map/ppermute | solution.py:519
  36.4 6.7 %collective-permute-start.16 = (f32[6,32,128]{2,1,0:T(8,128)S(1)}, f32[6,32,128]{2,1,0:T(8,128)S(1)}, u32[]{:S(2)}, u32[]{:S(2)}) collective-permute-start(f32[6,32,128]{2,1,0:T(8,128)S(1)} %get-tuple-element.91), channel_id=1, source_target_pairs={{0,2},{1,3},{2,0},{3,1},{4,6},{5,7},{6,4},{7,5},{8,10},{9,11},{10,... | collective-permute-start | bytes 294920 | tf_op jit(solution)/shard_map/ppermute | solution.py:519
  37.3 8.8 %collective-permute-start.17 = (f32[6,32,128]{2,1,0:T(8,128)S(1)}, f32[6,32,128]{2,1,0:T(8,128)S(1)}, u32[]{:S(2)}, u32[]{:S(2)}) collective-permute-start(f32[6,32,128]{2,1,0:T(8,128)S(1)} %get-tuple-element.92), channel_id=1, source_target_pairs={{0,6},{1,7},{2,4},{3,5},{4,2},{5,3},{6,0},{7,1},{8,14},{9,15},{10,... | collective-permute-start | bytes 294920 | tf_op jit(solution)/shard_map/ppermute | solution.py:519
  39.3 7.6 %collective-permute-start.11 = (f32[6,32,128]{2,1,0:T(8,128)S(1)}, f32[6,32,128]{2,1,0:T(8,128)S(1)}, u32[]{:S(2)}, u32[]{:S(2)}) collective-permute-start(f32[6,32,128]{2,1,0:T(8,128)S(1)} %get-tuple-element.85), channel_id=1, source_target_pairs={{0,4},{1,5},{2,6},{3,7},{4,0},{5,1},{6,2},{7,3},{8,12},{9,13},{10,... | collective-permute-start | bytes 294920 | tf_op jit(solution)/shard_map/ppermute | solution.py:519
  40.6 6.6 %collective-permute-start.12 = (f32[6,32,128]{2,1,0:T(8,128)S(1)}, f32[6,32,128]{2,1,0:T(8,128)S(1)}, u32[]{:S(2)}, u32[]{:S(2)}) collective-permute-start(f32[6,32,128]{2,1,0:T(8,128)S(1)} %get-tuple-element.86), channel_id=1, source_target_pairs={{0,5},{1,4},{2,7},{3,6},{4,1},{5,0},{6,3},{7,2},{8,13},{9,12},{10,... | collective-permute-start | bytes 294920 | tf_op jit(solution)/shard_map/ppermute | solution.py:519
  41.8 6.4 %collective-permute-start.13 = (f32[6,32,128]{2,1,0:T(8,128)S(1)}, f32[6,32,128]{2,1,0:T(8,128)S(1)}, u32[]{:S(2)}, u32[]{:S(2)}) collective-permute-start(f32[6,32,128]{2,1,0:T(8,128)S(1)} %get-tuple-element.87), channel_id=1, source_target_pairs={{0,3},{1,2},{2,1},{3,0},{4,7},{5,6},{6,5},{7,4},{8,11},{9,10},{10,... | collective-permute-start | bytes 294920 | tf_op jit(solution)/shard_map/ppermute | solution.py:519
  43.1 6.5 %collective-permute-start.14 = (f32[6,32,128]{2,1,0:T(8,128)S(1)}, f32[6,32,128]{2,1,0:T(8,128)S(1)}, u32[]{:S(2)}, u32[]{:S(2)}) collective-permute-start(f32[6,32,128]{2,1,0:T(8,128)S(1)} %get-tuple-element.88), channel_id=1, source_target_pairs={{0,7},{1,6},{2,5},{3,4},{4,3},{5,2},{6,1},{7,0},{8,15},{9,14},{10,... | collective-permute-start | bytes 294920 | tf_op jit(solution)/shard_map/ppermute | solution.py:519
  46.1 3.5 %collective-permute-start.15 = (f32[6,32,128]{2,1,0:T(8,128)S(1)}, f32[6,32,128]{2,1,0:T(8,128)S(1)}, u32[]{:S(2)}, u32[]{:S(2)}) collective-permute-start(f32[6,32,128]{2,1,0:T(8,128)S(1)} %get-tuple-element.89), channel_id=1, source_target_pairs={{0,1},{1,0},{2,3},{3,2},{4,5},{5,4},{6,7},{7,6},{8,9},{9,8},{10,11... | collective-permute-start | bytes 294920 | tf_op jit(solution)/shard_map/ppermute | solution.py:519

commit v5 on v3

--- a/solution.py
+++ b/solution.py
@@ -18,8 +18,8 @@
 MATMUL_FACES = 4
 KDIM = (NFACE + 1) * NP
 SLOTS = [(0, 0), (2, 0), (2, 1), (1, 0), (3, 0), (1, 1), (3, 1), (0, 1)]
-EARLY = (0, 1, 2, 7)
-LATE = (3, 4, 5, 6)
+EARLY = (0, 3, 4)
+LATE = (1, 2, 5, 6, 7)
 
 
 def first_half(rows):
@@ -268,7 +268,7 @@
 
 
 def last_block(place_ref, dx, history, adjacency, weights, onehots, t2, parts3, gathered, outs):
-    b = (place_ref[1] + dx) & 3
+    b = place_ref[1] ^ dx
     upper = place_ref[2] == 1
     col = pl.multiple_of(b * LANE, LANE)
     rel = place(adjacency[:, pl.ds(col, LANE)], place_ref[0] + 128 + col)
@@ -295,7 +295,7 @@
 
 def source_of(x, core, slot):
     dx, dc = SLOTS[slot]
-    return ((x - dx) & 3) * 2 + (core ^ dc)
+    return (x ^ dx) * 2 + (core ^ dc)
 
 
 def table_kernel(place_ref, schmid_hbm, hardening_hbm, mixing, renewing, schmid_map, hardening, sems):
@@ -382,7 +382,7 @@
         pairs = []
         for piece, slot in zip(pieces, slots):
             dx, dc = SLOTS[slot]
-            col = pl.multiple_of(((x + dx) & 3) * LANE, LANE)
+            col = pl.multiple_of((x ^ dx) * LANE, LANE)
             row = pl.multiple_of((core ^ dc) * 32, 32)
             pairs.append((piece, out.at[:, pl.ds(row, 32), pl.ds(col, LANE)]))
         for copy in fetch(pairs, sems):
@@ -500,7 +500,7 @@
     def exchange(piece, dx, dc):
         if dx == 0 and dc == 0:
             return piece
-        pairs = [(v, ((v // 2 + dx) % 4) * 2 + ((v % 2) ^ dc)) for v in range(8)]
+        pairs = [(v, v ^ (2 * dx + dc)) for v in range(groups)]
         return lax.ppermute(piece, "var", pairs)
 
     points = [exchange(piece, dx, dc) for piece, (dx, dc) in zip(advected, SLOTS)]
@@ -518,7 +518,7 @@
         [piece] * 8,
         [((ROWS, 512), BF16), ((ROWS, 512), BF16), ((288, 512), BF16)],
     )
-    returned = [exchange(piece, (4 - dx) % 4, dc) for piece, (dx, dc) in zip(renewed, SLOTS)]
+    returned = [exchange(piece, dx, dc) for piece, (dx, dc) in zip(renewed, SLOTS)]
     out = call(
         merge_kernel(EARLY), [returned[i] for i in EARLY], [((NV, NP, NZ), F32)],
         copies=len(EARLY), hbm_out=True,

time: 52.6 us -> 50.6 us (0.962)
  the two profiles are of different devices: /device:TPU:129 before, /device:TPU:120 now
where the time goes in v5:
time: 50.6 us; the launch traced here: 50.2 us
  starting transfers between devices  21.4 us (42%)
  Pallas kernels  15.3 us (30%)
  waiting for transfers between devices  13.2 us (26%)
    ppermute x14, starting transfers between devices, exchange(): return lax.ppermute(piece, 'var', pairs)  15.4 us
    pallas_call x10, Pallas kernels, call(): pl.pallas_call(placed, out_shape=tuple((jax.ShapeDtypeStruct(shape, dtype...  15.3 us
    ppermute x14, waiting for transfers between devices, exchange(): return lax.ppermute(piece, 'var', pairs)  9.35 us
    ppermute x1, waiting for transfers between devices, per_device(): near_one = lax.ppermute(near_one, axes, one)  3.82 us
    ppermute x1, starting transfers between devices, per_device(): near_one = lax.ppermute(near_one, axes, one)  3.15 us
    ppermute x1, starting transfers between devices, per_device(): far_one = lax.ppermute(far_one, axes, one)  2.87 us
  transfers between devices with their start and end apart: 18, of which 7 were waited for; matrix products, arithmetic and copies ran while one was open for 0% of the time, Pallas kernels for 15%

profile of v5, /device:TPU:120, one launch (start us, length us, event | category | flops | bytes accessed | tf_op | source)
XLA Modules:
  0.0 50.2 jit_solution(4766170451270264196)
XLA Ops:
  0.0 1.7 %shard_map.65 = (f32[192,128]{1,0:T(8,128)S(1)}, f32[192,128]{1,0:T(8,128)S(1)}, f32[392,128]{1,0:T(8,128)S(1)}, f32[392,128]{1,0:T(8,128)S(1)}, f32[384,512]{1,...) custom-call(f32[384,512]{1,0:T(8,128)} %bitcast.3, s32[6,512]{1,0:T(8,128)} %refs_1_.3, ...), custom_call_target="tpu_custom_call" | custom-call | tf_op jit(solution)/shard_map/pallas_call | solution.py:416
  1.7 2.9 %collective-permute-start = (f32[392,128]{1,0:T(8,128)S(1)}, f32[392,128]{1,0:T(8,128)S(1)}, u32[]{:S(2)}, u32[]{:S(2)}) collective-permute-start(f32[392,128]{1,0:T(8,128)S(1)} %get-tuple-element.55), channel_id=1, source_target_pairs={{0,1},{1,0},{2,3},{3,2},{4,5},{5,4},{6,7},{7,6},{8,16},{9,17},{10,... | collective-permute-start | bytes 602120 | tf_op jit(solution)/shard_map/ppermute | solution.py:457
  4.6 3.1 %collective-permute-start.2 = (f32[192,128]{1,0:T(8,128)S(1)}, f32[192,128]{1,0:T(8,128)S(1)}, u32[]{:S(2)}, u32[]{:S(2)}) collective-permute-start(f32[192,128]{1,0:T(8,128)S(1)} %get-tuple-element.57), channel_id=1, source_target_pairs={{0,1},{1,0},{2,3},{3,2},{4,5},{5,4},{6,7},{7,6},{8,16},{9,17},{10,... | collective-permute-start | bytes 294920 | tf_op jit(solution)/shard_map/ppermute | solution.py:455
  7.7 2.4 %shard_map.66 = (f32[384,640]{1,0:T(8,128)S(1)}, bf16[768,384]{1,0:T(8,128)(2,1)S(1)}, bf16[7,256,512]{2,1,0:T(8,128)(2,1)S(1)}, f32[384,256]{1,0:T(8,128)S(1)},...) custom-call(f32[384,512]{1,0:T(8,128)S(1)} %get-tuple-element.49.ref, ...), custom_call_target="tpu_custom_call" | custom-call | tf_op jit(solution)/shard_map/pallas_call | solution.py:416
  10.1 3.8 %collective-permute-done.2.refs_2_ = f32[192,128]{1,0:T(8,128)S(1)} collective-permute-done((f32[192,128]{1,0:T(8,128)S(1)}, f32[192,128]{1,0:T(8,128)S(1)}, u32[]{:S(2)}, u32[]{:S(2)}) %collective-permute-start.2) | collective-permute-done | bytes 98336 | tf_op jit(solution)/shard_map/ppermute | solution.py:455
  13.9 2.4 %shard_map.67 = (f32[384,256]{1,0:T(8,128)S(1)}, bf16[768,256]{1,0:T(8,128)(2,1)S(1)}, f32[384,256]{1,0:T(8,128)S(1)}, bf16[768,256]{1,0:T(8,128)(2,1)S(1)}, f32...) custom-call(f32[384,512]{1,0:T(8,128)S(1)} %get-tuple-element.49.refs_0_, s32[6,512]{1,0:T(8,128)S(1)} %get-tuple-element.50.refs_1_, ...), custom_call_target="tpu_custom_call" | custom-call | tf_op jit(solution)/shard_map/pallas_call | solution.py:416
  16.4 3.2 %shard_map.68 = (f32[6,32,128]{2,1,0:T(8,128)S(1)}, f32[6,32,128]{2,1,0:T(8,128)S(1)}, f32[384,640]{1,0:T(8,128)S(1)}, bf16[768,640]{1,0:T(8,128)(2,1)S(1)}) custom-call(f32[384,512]{1,0:T(8,128)S(1)} %get-tuple-element.49.refs_0_, s32[6,512]{1,0:T(8,128)S(1)} %get-tuple-element.50.refs_1_, f32[392,128]{1,0:T(8,128)S(1)} %collective-permute-done.refs_2_, ...), custom_call_target="tpu_custom_call" | custom-call | tf_op jit(solution)/shard_map/pallas_call | solution.py:416
  19.6 1.2 %shard_map.70 = (f32[6,32,128]{2,1,0:T(8,128)S(1)}, f32[6,32,128]{2,1,0:T(8,128)S(1)}, f32[6,32,128]{2,1,0:T(8,128)S(1)}, f32[6,32,128]{2,1,0:T(8,128)S(1)}) custom-call(f32[384,512]{1,0:T(8,128)S(1)} %get-tuple-element.49.refs_0_, s32[6,512]{1,0:T(8,128)S(1)} %get-tuple-element.50.refs_1_, bf16[128,448]{1,0:T(8,128)(2,1)S(1)} %get-tuple-element.53.refs_11_.refs_5_.refs_2_, ...), custom_call_target="tpu_custom_call" | custom-call | tf_op jit(solution)/shard_map/pallas_call | solution.py:416
  20.8 1.6 %collective-permute-start.6 = (f32[6,32,128]{2,1,0:T(8,128)S(1)}, f32[6,32,128]{2,1,0:T(8,128)S(1)}, u32[]{:S(2)}, u32[]{:S(2)}) collective-permute-start(f32[6,32,128]{2,1,0:T(8,128)S(1)} %get-tuple-element.76), channel_id=1, source_target_pairs={{0,2},{1,3},{2,0},{3,1},{4,6},{5,7},{6,4},{7,5},{8,10},{9,11},{10,... | collective-permute-start | bytes 294920 | tf_op jit(solution)/shard_map/ppermute | solution.py:504
  22.4 2.1 %collective-permute-start.7 = (f32[6,32,128]{2,1,0:T(8,128)S(1)}, f32[6,32,128]{2,1,0:T(8,128)S(1)}, u32[]{:S(2)}, u32[]{:S(2)}) collective-permute-start(f32[6,32,128]{2,1,0:T(8,128)S(1)} %get-tuple-element.77), channel_id=1, source_target_pairs={{0,6},{1,7},{2,4},{3,5},{4,2},{5,3},{6,0},{7,1},{8,14},{9,15},{10,... | collective-permute-start | bytes 294920 | tf_op jit(solution)/shard_map/ppermute | solution.py:504
  24.5 0.7 %shard_map.69 = (f32[6,32,128]{2,1,0:T(8,128)S(1)}, f32[6,32,128]{2,1,0:T(8,128)S(1)}) custom-call(f32[384,512]{1,0:T(8,128)S(1)} %get-tuple-element.49.refs_0_, s32[6,512]{1,0:T(8,128)S(1)} %get-tuple-element.50.refs_1_, bf16[128,448]{1,0:T(8,128)(2,1)S(1)} %get-tuple-element.53.refs_11_.refs_5_.refs_2_, ...), custom_call_target="tpu_custom_call" | custom-call | tf_op jit(solution)/shard_map/pallas_call | solution.py:416
  25.2 0.1 collective-permute-start.8
  25.3 0.9 %collective-permute-start.9 = (f32[6,32,128]{2,1,0:T(8,128)S(1)}, f32[6,32,128]{2,1,0:T(8,128)S(1)}, u32[]{:S(2)}, u32[]{:S(2)}) collective-permute-start(f32[6,32,128]{2,1,0:T(8,128)S(1)} %get-tuple-element.79), channel_id=1, source_target_pairs={{0,7},{1,6},{2,5},{3,4},{4,3},{5,2},{6,1},{7,0},{8,15},{9,14},{10,... | collective-permute-start | bytes 294920 | tf_op jit(solution)/shard_map/ppermute | solution.py:504
  26.2 0.4 collective-permute-start.10
  26.6 2.5 %collective-permute-start.4 = (f32[6,32,128]{2,1,0:T(8,128)S(1)}, f32[6,32,128]{2,1,0:T(8,128)S(1)}, u32[]{:S(2)}, u32[]{:S(2)}) collective-permute-start(f32[6,32,128]{2,1,0:T(8,128)S(1)} %get-tuple-element.74), channel_id=1, source_target_pairs={{0,4},{1,5},{2,6},{3,7},{4,0},{5,1},{6,2},{7,3},{8,12},{9,13},{10,... | collective-permute-start | bytes 294920 | tf_op jit(solution)/shard_map/ppermute | solution.py:504
  29.1 0.5 collective-permute-start.5
  29.5 1.4 %shard_map.64 = (bf16[192,384]{1,0:T(8,128)(2,1)S(1)}, bf16[384,288]{1,0:T(8,128)(2,1)S(1)}) custom-call(f32[12,48]{1,0:T(8,128)} %bitcast.5, f32[12,48]{1,0:T(8,128)} %refs_1_.2), custom_call_target="tpu_custom_call" | custom-call | tf_op jit(solution)/shard_map/pallas_call | solution.py:416
  31.0 2.0 %collective-permute-done.4.refs_3_ = f32[6,32,128]{2,1,0:T(8,128)S(1)} collective-permute-done((f32[6,32,128]{2,1,0:T(8,128)S(1)}, f32[6,32,128]{2,1,0:T(8,128)S(1)}, u32[]{:S(2)}, u32[]{:S(2)}) %collective-permute-start.4) | collective-permute-done | bytes 98336 | tf_op jit(solution)/shard_map/ppermute | solution.py:504
  33.0 2.3 %collective-permute-done.5.refs_4_ = f32[6,32,128]{2,1,0:T(8,128)S(1)} collective-permute-done((f32[6,32,128]{2,1,0:T(8,128)S(1)}, f32[6,32,128]{2,1,0:T(8,128)S(1)}, u32[]{:S(2)}, u32[]{:S(2)}) %collective-permute-start.5) | collective-permute-done | bytes 98336 | tf_op jit(solution)/shard_map/ppermute | solution.py:504
  35.3 0.8 %shard_map.71 = (f32[6,32,128]{2,1,0:T(8,128)S(1)}, f32[6,32,128]{2,1,0:T(8,128)S(1)}, f32[6,32,128]{2,1,0:T(8,128)S(1)}, f32[6,32,128]{2,1,0:T(8,128)S(1)}, f32...) custom-call(bf16[192,384]{1,0:T(8,128)(2,1)S(1)} %get-tuple-element.4, ...), custom_call_target="tpu_custom_call" | custom-call | tf_op jit(solution)/shard_map/pallas_call | solution.py:416
  36.0 0.9 %collective-permute-start.16 = (f32[6,32,128]{2,1,0:T(8,128)S(1)}, f32[6,32,128]{2,1,0:T(8,128)S(1)}, u32[]{:S(2)}, u32[]{:S(2)}) collective-permute-start(f32[6,32,128]{2,1,0:T(8,128)S(1)} %get-tuple-element.87), channel_id=1, source_target_pairs={{0,2},{1,3},{2,0},{3,1},{4,6},{5,7},{6,4},{7,5},{8,10},{9,11},{10,... | collective-permute-start | bytes 294920 | tf_op jit(solution)/shard_map/ppermute | solution.py:504
  36.9 1.9 %collective-permute-start.17 = (f32[6,32,128]{2,1,0:T(8,128)S(1)}, f32[6,32,128]{2,1,0:T(8,128)S(1)}, u32[]{:S(2)}, u32[]{:S(2)}) collective-permute-start(f32[6,32,128]{2,1,0:T(8,128)S(1)} %get-tuple-element.88), channel_id=1, source_target_pairs={{0,6},{1,7},{2,4},{3,5},{4,2},{5,3},{6,0},{7,1},{8,14},{9,15},{10,... | collective-permute-start | bytes 294920 | tf_op jit(solution)/shard_map/ppermute | solution.py:504
  38.9 1.4 %collective-permute-start.11 = (f32[6,32,128]{2,1,0:T(8,128)S(1)}, f32[6,32,128]{2,1,0:T(8,128)S(1)}, u32[]{:S(2)}, u32[]{:S(2)}) collective-permute-start(f32[6,32,128]{2,1,0:T(8,128)S(1)} %get-tuple-element.81), channel_id=1, source_target_pairs={{0,4},{1,5},{2,6},{3,7},{4,0},{5,1},{6,2},{7,3},{8,12},{9,13},{10,... | collective-permute-start | bytes 294920 | tf_op jit(solution)/shard_map/ppermute | solution.py:504
  40.2 1.2 %collective-permute-start.12 = (f32[6,32,128]{2,1,0:T(8,128)S(1)}, f32[6,32,128]{2,1,0:T(8,128)S(1)}, u32[]{:S(2)}, u32[]{:S(2)}) collective-permute-start(f32[6,32,128]{2,1,0:T(8,128)S(1)} %get-tuple-element.82), channel_id=1, source_target_pairs={{0,5},{1,4},{2,7},{3,6},{4,1},{5,0},{6,3},{7,2},{8,13},{9,12},{10,... | collective-permute-start | bytes 294920 | tf_op jit(solution)/shard_map/ppermute | solution.py:504
  41.4 1.3 %collective-permute-start.13 = (f32[6,32,128]{2,1,0:T(8,128)S(1)}, f32[6,32,128]{2,1,0:T(8,128)S(1)}, u32[]{:S(2)}, u32[]{:S(2)}) collective-permute-start(f32[6,32,128]{2,1,0:T(8,128)S(1)} %get-tuple-element.83), channel_id=1, source_target_pairs={{0,3},{1,2},{2,1},{3,0},{4,7},{5,6},{6,5},{7,4},{8,11},{9,10},{10,... | collective-permute-start | bytes 294920 | tf_op jit(solution)/shard_map/ppermute | solution.py:504
  42.7 0.7 %collective-permute-start.14 = (f32[6,32,128]{2,1,0:T(8,128)S(1)}, f32[6,32,128]{2,1,0:T(8,128)S(1)}, u32[]{:S(2)}, u32[]{:S(2)}) collective-permute-start(f32[6,32,128]{2,1,0:T(8,128)S(1)} %get-tuple-element.84), channel_id=1, source_target_pairs={{0,7},{1,6},{2,5},{3,4},{4,3},{5,2},{6,1},{7,0},{8,15},{9,14},{10,... | collective-permute-start | bytes 294920 | tf_op jit(solution)/shard_map/ppermute | solution.py:504
  43.4 2.3 %collective-permute-done.17.refs_2_ = f32[6,32,128]{2,1,0:T(8,128)S(1)} collective-permute-done((f32[6,32,128]{2,1,0:T(8,128)S(1)}, f32[6,32,128]{2,1,0:T(8,128)S(1)}, u32[]{:S(2)}, u32[]{:S(2)}) %collective-permute-start.17) | collective-permute-done | bytes 98336 | tf_op jit(solution)/shard_map/ppermute | solution.py:504
  45.8 0.7 %shard_map.72.refs_5_ = f32[6,64,512]{2,1,0:T(8,128)} custom-call(f32[6,32,128]{2,1,0:T(8,128)S(1)} %get-tuple-element.86.refs_0_, f32[6,32,128]{2,1,0:T(8,128)S(1)} %collective-permute-done.16.refs_1_, f32[6,32,128]{2,1,0:T(8,128)S(1)} %collective-permute-done.17.refs_2_), custom_call_target="tpu_custom_call" | custom-call | tf_op jit(solution)/shard_map/pallas_call | solution.py:416
  46.5 0.3 collective-permute-done.12.refs_1_
  46.8 1.0 %collective-permute-done.13.refs_2_ = f32[6,32,128]{2,1,0:T(8,128)S(1)} collective-permute-done((f32[6,32,128]{2,1,0:T(8,128)S(1)}, f32[6,32,128]{2,1,0:T(8,128)S(1)}, u32[]{:S(2)}, u32[]{:S(2)}) %collective-permute-start.13) | collective-permute-done | bytes 98336 | tf_op jit(solution)/shard_map/ppermute | solution.py:504
  47.8 1.4 %collective-permute-done.14.refs_3_ = f32[6,32,128]{2,1,0:T(8,128)S(1)} collective-permute-done((f32[6,32,128]{2,1,0:T(8,128)S(1)}, f32[6,32,128]{2,1,0:T(8,128)S(1)}, u32[]{:S(2)}, u32[]{:S(2)}) %collective-permute-start.14) | collective-permute-done | bytes 98336 | tf_op jit(solution)/shard_map/ppermute | solution.py:504
  49.2 0.8 %shard_map.73 = f32[6,64,512]{2,1,0:T(8,128)} custom-call(f32[6,32,128]{2,1,0:T(8,128)S(1)} %collective-permute-done.11.refs_0_, f32[6,32,128]{2,1,0:T(8,128)S(1)} %collective-permute-done.12.refs_1_, f32[6,32,128]{2,1,0:T(8,128)S(1)} %collective-permute-done.13.refs_2_, ...), custom_call_target="tpu_custom_call", output_to_operand_aliasing={{}: (5, {})} | custom-call | tf_op jit(solution)/shard_map/pallas_call | solution.py:416
  (14 shorter events, 0.0 us)
Async XLA Ops:
  1.7 14.7 %collective-permute-start = (f32[392,128]{1,0:T(8,128)S(1)}, f32[392,128]{1,0:T(8,128)S(1)}, u32[]{:S(2)}, u32[]{:S(2)}) collective-permute-start(f32[392,128]{1,0:T(8,128)S(1)} %get-tuple-element.55), channel_id=1, source_target_pairs={{0,1},{1,0},{2,3},{3,2},{4,5},{5,4},{6,7},{7,6},{8,16},{9,17},{10,... | collective-permute-start | bytes 602120 | tf_op jit(solution)/shard_map/ppermute | solution.py:457
  4.6 11.8 %collective-permute-start.1 = (f32[392,128]{1,0:T(8,128)S(1)}, f32[392,128]{1,0:T(8,128)S(1)}, u32[]{:S(2)}, u32[]{:S(2)}) collective-permute-start(f32[392,128]{1,0:T(8,128)S(1)} %get-tuple-element.56), channel_id=1, source_target_pairs={{0,8},{1,9},{2,10},{3,11},{4,12},{5,13},{6,14},{7,15},{8,0},{9,1},... | collective-permute-start | bytes 602120 | tf_op jit(solution)/shard_map/ppermute | solution.py:458
  4.6 9.4 %collective-permute-start.2 = (f32[192,128]{1,0:T(8,128)S(1)}, f32[192,128]{1,0:T(8,128)S(1)}, u32[]{:S(2)}, u32[]{:S(2)}) collective-permute-start(f32[192,128]{1,0:T(8,128)S(1)} %get-tuple-element.57), channel_id=1, source_target_pairs={{0,1},{1,0},{2,3},{3,2},{4,5},{5,4},{6,7},{7,6},{8,16},{9,17},{10,... | collective-permute-start | bytes 294920 | tf_op jit(solution)/shard_map/ppermute | solution.py:455
  7.7 6.2 %collective-permute-start.3 = (f32[192,128]{1,0:T(8,128)S(1)}, f32[192,128]{1,0:T(8,128)S(1)}, u32[]{:S(2)}, u32[]{:S(2)}) collective-permute-start(f32[192,128]{1,0:T(8,128)S(1)} %get-tuple-element.58), channel_id=1, source_target_pairs={{0,8},{1,9},{2,10},{3,11},{4,12},{5,13},{6,14},{7,15},{8,0},{9,1},... | collective-permute-start | bytes 294920 | tf_op jit(solution)/shard_map/ppermute | solution.py:456
  20.8 5.8 %collective-permute-start.6 = (f32[6,32,128]{2,1,0:T(8,128)S(1)}, f32[6,32,128]{2,1,0:T(8,128)S(1)}, u32[]{:S(2)}, u32[]{:S(2)}) collective-permute-start(f32[6,32,128]{2,1,0:T(8,128)S(1)} %get-tuple-element.76), channel_id=1, source_target_pairs={{0,2},{1,3},{2,0},{3,1},{4,6},{5,7},{6,4},{7,5},{8,10},{9,11},{10,... | collective-permute-start | bytes 294920 | tf_op jit(solution)/shard_map/ppermute | solution.py:504
  22.4 6.7 %collective-permute-start.7 = (f32[6,32,128]{2,1,0:T(8,128)S(1)}, f32[6,32,128]{2,1,0:T(8,128)S(1)}, u32[]{:S(2)}, u32[]{:S(2)}) collective-permute-start(f32[6,32,128]{2,1,0:T(8,128)S(1)} %get-tuple-element.77), channel_id=1, source_target_pairs={{0,6},{1,7},{2,4},{3,5},{4,2},{5,3},{6,0},{7,1},{8,14},{9,15},{10,... | collective-permute-start | bytes 294920 | tf_op jit(solution)/shard_map/ppermute | solution.py:504
  25.2 5.8 %collective-permute-start.8 = (f32[6,32,128]{2,1,0:T(8,128)S(1)}, f32[6,32,128]{2,1,0:T(8,128)S(1)}, u32[]{:S(2)}, u32[]{:S(2)}) collective-permute-start(f32[6,32,128]{2,1,0:T(8,128)S(1)} %get-tuple-element.78), channel_id=1, source_target_pairs={{0,3},{1,2},{2,1},{3,0},{4,7},{5,6},{6,5},{7,4},{8,11},{9,10},{10,... | collective-permute-start | bytes 294920 | tf_op jit(solution)/shard_map/ppermute | solution.py:504
  25.3 5.7 %collective-permute-start.9 = (f32[6,32,128]{2,1,0:T(8,128)S(1)}, f32[6,32,128]{2,1,0:T(8,128)S(1)}, u32[]{:S(2)}, u32[]{:S(2)}) collective-permute-start(f32[6,32,128]{2,1,0:T(8,128)S(1)} %get-tuple-element.79), channel_id=1, source_target_pairs={{0,7},{1,6},{2,5},{3,4},{4,3},{5,2},{6,1},{7,0},{8,15},{9,14},{10,... | collective-permute-start | bytes 294920 | tf_op jit(solution)/shard_map/ppermute | solution.py:504
  26.2 4.8 %collective-permute-start.10 = (f32[6,32,128]{2,1,0:T(8,128)S(1)}, f32[6,32,128]{2,1,0:T(8,128)S(1)}, u32[]{:S(2)}, u32[]{:S(2)}) collective-permute-start(f32[6,32,128]{2,1,0:T(8,128)S(1)} %get-tuple-element.80), channel_id=1, source_target_pairs={{0,1},{1,0},{2,3},{3,2},{4,5},{5,4},{6,7},{7,6},{8,9},{9,8},{10,11... | collective-permute-start | bytes 294920 | tf_op jit(solution)/shard_map/ppermute | solution.py:504
  26.6 6.4 %collective-permute-start.4 = (f32[6,32,128]{2,1,0:T(8,128)S(1)}, f32[6,32,128]{2,1,0:T(8,128)S(1)}, u32[]{:S(2)}, u32[]{:S(2)}) collective-permute-start(f32[6,32,128]{2,1,0:T(8,128)S(1)} %get-tuple-element.74), channel_id=1, source_target_pairs={{0,4},{1,5},{2,6},{3,7},{4,0},{5,1},{6,2},{7,3},{8,12},{9,13},{10,... | collective-permute-start | bytes 294920 | tf_op jit(solution)/shard_map/ppermute | solution.py:504
  29.1 6.2 %collective-permute-start.5 = (f32[6,32,128]{2,1,0:T(8,128)S(1)}, f32[6,32,128]{2,1,0:T(8,128)S(1)}, u32[]{:S(2)}, u32[]{:S(2)}) collective-permute-start(f32[6,32,128]{2,1,0:T(8,128)S(1)} %get-tuple-element.75), channel_id=1, source_target_pairs={{0,5},{1,4},{2,7},{3,6},{4,1},{5,0},{6,3},{7,2},{8,13},{9,12},{10,... | collective-permute-start | bytes 294920 | tf_op jit(solution)/shard_map/ppermute | solution.py:504
  36.0 6.7 %collective-permute-start.16 = (f32[6,32,128]{2,1,0:T(8,128)S(1)}, f32[6,32,128]{2,1,0:T(8,128)S(1)}, u32[]{:S(2)}, u32[]{:S(2)}) collective-permute-start(f32[6,32,128]{2,1,0:T(8,128)S(1)} %get-tuple-element.87), channel_id=1, source_target_pairs={{0,2},{1,3},{2,0},{3,1},{4,6},{5,7},{6,4},{7,5},{8,10},{9,11},{10,... | collective-permute-start | bytes 294920 | tf_op jit(solution)/shard_map/ppermute | solution.py:504
  36.9 8.8 %collective-permute-start.17 = (f32[6,32,128]{2,1,0:T(8,128)S(1)}, f32[6,32,128]{2,1,0:T(8,128)S(1)}, u32[]{:S(2)}, u32[]{:S(2)}) collective-permute-start(f32[6,32,128]{2,1,0:T(8,128)S(1)} %get-tuple-element.88), channel_id=1, source_target_pairs={{0,6},{1,7},{2,4},{3,5},{4,2},{5,3},{6,0},{7,1},{8,14},{9,15},{10,... | collective-permute-start | bytes 294920 | tf_op jit(solution)/shard_map/ppermute | solution.py:504
  38.9 7.6 %collective-permute-start.11 = (f32[6,32,128]{2,1,0:T(8,128)S(1)}, f32[6,32,128]{2,1,0:T(8,128)S(1)}, u32[]{:S(2)}, u32[]{:S(2)}) collective-permute-start(f32[6,32,128]{2,1,0:T(8,128)S(1)} %get-tuple-element.81), channel_id=1, source_target_pairs={{0,4},{1,5},{2,6},{3,7},{4,0},{5,1},{6,2},{7,3},{8,12},{9,13},{10,... | collective-permute-start | bytes 294920 | tf_op jit(solution)/shard_map/ppermute | solution.py:504
  40.2 6.6 %collective-permute-start.12 = (f32[6,32,128]{2,1,0:T(8,128)S(1)}, f32[6,32,128]{2,1,0:T(8,128)S(1)}, u32[]{:S(2)}, u32[]{:S(2)}) collective-permute-start(f32[6,32,128]{2,1,0:T(8,128)S(1)} %get-tuple-element.82), channel_id=1, source_target_pairs={{0,5},{1,4},{2,7},{3,6},{4,1},{5,0},{6,3},{7,2},{8,13},{9,12},{10,... | collective-permute-start | bytes 294920 | tf_op jit(solution)/shard_map/ppermute | solution.py:504
  41.4 6.4 %collective-permute-start.13 = (f32[6,32,128]{2,1,0:T(8,128)S(1)}, f32[6,32,128]{2,1,0:T(8,128)S(1)}, u32[]{:S(2)}, u32[]{:S(2)}) collective-permute-start(f32[6,32,128]{2,1,0:T(8,128)S(1)} %get-tuple-element.83), channel_id=1, source_target_pairs={{0,3},{1,2},{2,1},{3,0},{4,7},{5,6},{6,5},{7,4},{8,11},{9,10},{10,... | collective-permute-start | bytes 294920 | tf_op jit(solution)/shard_map/ppermute | solution.py:504
  42.7 6.5 %collective-permute-start.14 = (f32[6,32,128]{2,1,0:T(8,128)S(1)}, f32[6,32,128]{2,1,0:T(8,128)S(1)}, u32[]{:S(2)}, u32[]{:S(2)}) collective-permute-start(f32[6,32,128]{2,1,0:T(8,128)S(1)} %get-tuple-element.84), channel_id=1, source_target_pairs={{0,7},{1,6},{2,5},{3,4},{4,3},{5,2},{6,1},{7,0},{8,15},{9,14},{10,... | collective-permute-start | bytes 294920 | tf_op jit(solution)/shard_map/ppermute | solution.py:504
  45.8 3.5 %collective-permute-start.15 = (f32[6,32,128]{2,1,0:T(8,128)S(1)}, f32[6,32,128]{2,1,0:T(8,128)S(1)}, u32[]{:S(2)}, u32[]{:S(2)}) collective-permute-start(f32[6,32,128]{2,1,0:T(8,128)S(1)} %get-tuple-element.85), channel_id=1, source_target_pairs={{0,1},{1,0},{2,3},{3,2},{4,5},{5,4},{6,7},{7,6},{8,9},{9,8},{10,11... | collective-permute-start | bytes 294920 | tf_op jit(solution)/shard_map/ppermute | solution.py:504
